TPU v7x, 32 devices: a whole 2x2x4 slice. The times are simulated.
32 devices in a mesh: dp: 4 (over z), row: 4 (over x, core), col: 2 (over y).
Axes of the slice: x: 2, y: 2, z: 4, core: 2. Of those that a mesh axis runs over, the one named last changes fastest.
Arguments:
- layer_input: bfloat16 [8, 512, 2048], P('dp', 'row'), may hold values from -12 to 12, as said below
- cotangent: bfloat16 [8, 512, 2048], P('dp', 'row'), may hold values from -6 to 6
- lengths: int32 [8], replicated, may hold values from 128 to 512, as said below
- deal_slot: int32 [8], replicated, may hold values from 0 to 7, as said below
- query_weight: bfloat16 [2048, 2048], P('row', 'col'), may hold values from -0.125 to 0.125
- key_weight: bfloat16 [2048, 2048], P('row', 'col'), may hold values from -0.125 to 0.125
- value_weight: bfloat16 [2048, 2048], P('row', 'col'), may hold values from -0.125 to 0.125
- out_weight: bfloat16 [2048, 2048], P('col', 'row'), may hold values from -0.125 to 0.125
- query_gain: bfloat16 [2048], P('col'), may hold values from 0.5 to 1.5
- key_gain: bfloat16 [2048], P('col'), may hold values from 0.5 to 1.5
- attn_gain: bfloat16 [2048], P('row'), may hold values from 0.5 to 1.5
- gate_weight: bfloat16 [2048, 8192], P('row', 'col'), may hold values from -0.125 to 0.125
- up_weight: bfloat16 [2048, 8192], P('row', 'col'), may hold values from -0.125 to 0.125
- down_weight: bfloat16 [8192, 2048], P('col', 'row'), may hold values from -0.0625 to 0.0625
- mlp_gain: bfloat16 [2048], P('row'), may hold values from 0.5 to 1.5
Outputs:
- output: bfloat16 [8, 512, 2048], P('dp', 'row')
- grad_input: bfloat16 [8, 512, 2048], P('dp', 'row')
- grad_query: float32 [2048, 2048], P('row', 'col')
- grad_key: float32 [2048, 2048], P('row', 'col')
- grad_value: float32 [2048, 2048], P('row', 'col')
- grad_out: float32 [2048, 2048], P('col', 'row')
- grad_query_gain: float32 [2048], P('col')
- grad_key_gain: float32 [2048], P('col')
- grad_attn_gain: float32 [2048], P('row')
- grad_gate: float32 [2048, 8192], P('row', 'col')
- grad_up: float32 [2048, 8192], P('row', 'col')
- grad_down: float32 [8192, 2048], P('col', 'row')
- grad_mlp_gain: float32 [2048], P('row')
- rms_stats: float32 [4, 3], replicated
Inputs may be any that keep to these rules, and one draw needn't show every extreme that they name: `layer_input`: activations; each sequence has its own scale. `lengths`: some sequence has 512 valid tokens and some 512 // 4. A permutation of the 8 slots; sequence i goes to position deal_slot[i] % 2 of group deal_slot[i] // 2; the 2 sequences held by one group, sequences i with i // 2 equal, go to 2 different groups.
All inputs are finite; a program needn't handle non-finite values.
Results may differ from a plain program's by a relative error of at most 0.023.
Values may be sent and summed in bfloat16 or wider, within the bound.
No kernel may reach another device: no remote copies, remote signals or barrier semaphores. Data moves between devices by JAX's collectives and lax.ppermute only.
A program may use at most 512 MiB of HBM per device.

v0:
```python
import jax
import jax.numpy as jnp
from jax import lax
from jax.sharding import PartitionSpec as P

HD = 128


EPSILON = 1e-06
ROPE_THETA = 500000.0
MASK_VALUE = 1e30


def rms_scale(matrix):
    return lax.rsqrt(jnp.mean(matrix * matrix, axis=-1, keepdims=True) + EPSILON)


def rotate_pairs(matrix, cos_table, sin_table):
    half_size = matrix.shape[-1] // 2
    first_half = matrix[..., :half_size]
    second_half = matrix[..., half_size:]
    return jnp.concatenate(
        [
            first_half * cos_table - second_half * sin_table,
            second_half * cos_table + first_half * sin_table,
        ],
        axis=-1,
    )


def rotate_back(matrix, cos_table, sin_table):
    half_size = matrix.shape[-1] // 2
    first_half = matrix[..., :half_size]
    second_half = matrix[..., half_size:]
    return jnp.concatenate(
        [
            first_half * cos_table + second_half * sin_table,
            second_half * cos_table - first_half * sin_table,
        ],
        axis=-1,
    )


def against(left_side, right_side):
    return lax.dot_general(
        left_side, right_side, (((0,), (0,)), ((), ())), preferred_element_type=jnp.float32
    )


def through(left_side, weight):
    return lax.dot_general(
        left_side, weight, (((1,), (1,)), ((), ())), preferred_element_type=jnp.float32
    )


def unchanged(matrix):
    return matrix


def shards(
    layer_input,
    cotangent,
    lengths,
    deal_slot,
    query_weight,
    key_weight,
    value_weight,
    out_weight,
    query_gain,
    key_gain,
    attn_gain,
    gate_weight,
    up_weight,
    down_weight,
    mlp_gain,
):
    groups = lax.axis_size("dp")
    rows_axis = lax.axis_size("row")
    my_group = lax.axis_index("dp")
    my_row = lax.axis_index("row")
    seq_grp, tok_seq, width = layer_input.shape
    seq_count = lengths.shape[0]
    heads_cols = query_weight.shape[1]
    heads_here = heads_cols // HD
    ff_cols = gate_weight.shape[1]
    seq_len = tok_seq * rows_axis
    tok_rows = seq_grp * tok_seq
    peer_ids = jnp.arange(groups, dtype=jnp.int32)
    slot_ids = jnp.arange(seq_count, dtype=jnp.int32)
    sent_to = lax.dynamic_slice_in_dim(deal_slot, my_group * seq_grp, seq_grp) // seq_grp
    send_pick = (peer_ids[:, None] == sent_to[None, :]).astype(jnp.bfloat16)
    out_input = jnp.einsum(
        "pj,jtd->ptd", send_pick, layer_input, preferred_element_type=jnp.float32
    ).astype(jnp.bfloat16)
    out_cot = jnp.einsum(
        "pj,jtd->ptd", send_pick, cotangent, preferred_element_type=jnp.float32
    ).astype(jnp.bfloat16)
    arrive_input, arrive_cot = (
        lax.all_to_all(out_input, "dp", split_axis=0, concat_axis=0, tiled=True),
        lax.all_to_all(out_cot, "dp", split_axis=0, concat_axis=0, tiled=True),
    )
    own_slots = my_group * seq_grp + jnp.arange(seq_grp, dtype=jnp.int32)
    source = jnp.sum(
        jnp.where(deal_slot[None, :] == own_slots[:, None], slot_ids[None, :], 0), axis=1
    )
    take_pick = ((source // seq_grp)[:, None] == peer_ids[None, :]).astype(jnp.bfloat16)
    dealt_input = jnp.einsum(
        "jp,ptd->jtd", take_pick, arrive_input, preferred_element_type=jnp.float32
    ).astype(jnp.bfloat16)
    dealt_cot = jnp.einsum(
        "jp,ptd->jtd", take_pick, arrive_cot, preferred_element_type=jnp.float32
    ).astype(jnp.bfloat16)
    live_len = jnp.sum(jnp.where(slot_ids[None, :] == source[:, None], lengths[None, :], 0), axis=1)
    places = my_row * tok_seq + jnp.arange(tok_seq, dtype=jnp.int32)
    valid_rows = (places[None, :] < live_len[:, None]).astype(jnp.float32).reshape(tok_rows, 1)
    inputs_low = dealt_input.reshape(tok_rows, width) * valid_rows.astype(jnp.bfloat16)
    inputs = inputs_low.astype(jnp.float32)
    grad_rows_in = dealt_cot.reshape(tok_rows, width).astype(jnp.float32) * valid_rows
    (
        full_query,
        full_key,
        full_value,
        full_out,
        full_attn_gain,
        full_gate,
        full_up,
        full_down,
        full_mlp_gain,
    ) = (
        lax.all_gather(query_weight, "row", axis=0, tiled=True),
        lax.all_gather(key_weight, "row", axis=0, tiled=True),
        lax.all_gather(value_weight, "row", axis=0, tiled=True),
        lax.all_gather(out_weight, "row", axis=1, tiled=True),
        lax.all_gather(attn_gain, "row", axis=0, tiled=True),
        lax.all_gather(gate_weight, "row", axis=0, tiled=True),
        lax.all_gather(up_weight, "row", axis=0, tiled=True),
        lax.all_gather(down_weight, "row", axis=1, tiled=True),
        lax.all_gather(mlp_gain, "row", axis=0, tiled=True),
    )
    query_raw = jnp.dot(inputs_low, full_query, preferred_element_type=jnp.float32)
    key_raw = jnp.dot(inputs_low, full_key, preferred_element_type=jnp.float32)
    value_raw = jnp.dot(inputs_low, full_value, preferred_element_type=jnp.float32)
    q_total, k_total = lax.psum(
        (jnp.sum(query_raw * query_raw, axis=1), jnp.sum(key_raw * key_raw, axis=1)), "col"
    )
    q_scale = lax.rsqrt(q_total / width + EPSILON)[:, None]
    k_scale = lax.rsqrt(k_total / width + EPSILON)[:, None]
    q_unit = query_raw * q_scale
    k_unit = key_raw * k_scale
    q_gain_f = query_gain.astype(jnp.float32)
    k_gain_f = key_gain.astype(jnp.float32)
    frequency = ROPE_THETA ** (-(jnp.arange(HD // 2).astype(jnp.float32) * 2.0 / HD))
    angles = places.astype(jnp.float32)[:, None] * frequency[None, :]
    cos_table = jnp.cos(angles)[None, :, None, :]
    sin_table = jnp.sin(angles)[None, :, None, :]
    head_shape = (seq_grp, tok_seq, heads_here, HD)
    q_turned = rotate_pairs((q_unit * q_gain_f).reshape(head_shape), cos_table, sin_table).astype(
        jnp.bfloat16
    )
    k_turned = rotate_pairs((k_unit * k_gain_f).reshape(head_shape), cos_table, sin_table).astype(
        jnp.bfloat16
    )
    value_low = value_raw.astype(jnp.bfloat16)
    keys_all, values_all = (
        lax.all_gather(k_turned.reshape(seq_grp, tok_seq, heads_cols), "row", axis=1, tiled=True),
        lax.all_gather(value_low.reshape(seq_grp, tok_seq, heads_cols), "row", axis=1, tiled=True),
    )
    key_heads = keys_all.reshape(seq_grp, seq_len, heads_here, HD)
    value_heads = values_all.reshape(seq_grp, seq_len, heads_here, HD)
    key_places = jnp.arange(seq_len, dtype=jnp.int32)
    allowed = (key_places[None, None, :] <= places[None, :, None]) & (
        key_places[None, None, :] < live_len[:, None, None]
    )
    score_scale = HD ** (-0.5)

    def scores_of(query_heads):
        raw_scores = (
            jnp.einsum(
                "sqhd,skhd->shqk", query_heads, key_heads, preferred_element_type=jnp.float32
            )
            * score_scale
        )
        return jnp.where(allowed[:, None], raw_scores, -MASK_VALUE)

    scores = scores_of(q_turned)
    row_max = jnp.max(scores, axis=-1, keepdims=True)
    exponent = jnp.exp(scores - row_max)
    row_total = jnp.sum(exponent, axis=-1, keepdims=True)
    prob_attn = exponent / row_total
    log_total = row_max + jnp.log(row_total)
    attn_mix = jnp.einsum(
        "shqk,skhd->sqhd",
        prob_attn.astype(jnp.bfloat16),
        value_heads,
        preferred_element_type=jnp.float32,
    )
    attn_mix = attn_mix.reshape(tok_rows, heads_cols).astype(jnp.bfloat16)
    attn_raw = lax.psum(jnp.dot(attn_mix, full_out, preferred_element_type=jnp.float32), "col")
    a_scale = rms_scale(attn_raw)
    a_unit = attn_raw * a_scale
    attn_gain_f = full_attn_gain.astype(jnp.float32)
    branch_a = a_unit * attn_gain_f
    hidden = inputs + branch_a
    hidden_low = hidden.astype(jnp.bfloat16)
    gate_pre = jnp.dot(hidden_low, full_gate, preferred_element_type=jnp.float32)
    up_pre = jnp.dot(hidden_low, full_up, preferred_element_type=jnp.float32)
    gate_sig = jax.nn.sigmoid(gate_pre)
    gate_act = gate_pre * gate_sig
    inner_low = (gate_act * up_pre).astype(jnp.bfloat16)
    mlp_raw = lax.psum(
        jnp.dot(inner_low, full_down, preferred_element_type=jnp.float32).astype(jnp.bfloat16),
        "col",
    ).astype(jnp.float32)
    m_scale = rms_scale(mlp_raw)
    m_unit = mlp_raw * m_scale
    mlp_gain_f = full_mlp_gain.astype(jnp.float32)
    branch_m = m_unit * mlp_gain_f
    result = (hidden + branch_m) * valid_rows
    local_sums = jnp.stack(
        [
            jnp.sum(result * result),
            jnp.sum(branch_a * branch_a * valid_rows),
            jnp.sum(branch_m * branch_m * valid_rows),
        ]
    )
    grad_mlp_gain_part = jnp.sum(grad_rows_in * m_unit, axis=0)
    d_m_unit = grad_rows_in * mlp_gain_f
    d_mlp = m_scale * (d_m_unit - m_unit * jnp.mean(d_m_unit * m_unit, axis=-1, keepdims=True))
    d_mlp_low = d_mlp.astype(jnp.bfloat16)
    d_inner = through(d_mlp_low, full_down)
    d_gate_low = (d_inner * up_pre * (gate_sig * (1.0 + gate_pre * (1.0 - gate_sig)))).astype(
        jnp.bfloat16
    )
    d_up_low = (d_inner * gate_act).astype(jnp.bfloat16)
    d_hidden = grad_rows_in + lax.psum(
        through(d_gate_low, full_gate) + through(d_up_low, full_up), "col"
    )
    grad_attn_gain_part = jnp.sum(d_hidden * a_unit, axis=0)
    d_a_unit = d_hidden * attn_gain_f
    d_attn_low = (
        a_scale * (d_a_unit - a_unit * jnp.mean(d_a_unit * a_unit, axis=-1, keepdims=True))
    ).astype(jnp.bfloat16)
    d_mix = through(d_attn_low, full_out).astype(jnp.bfloat16).reshape(head_shape)
    prob_again = jnp.exp(scores_of(q_turned) - log_total)
    d_prob = jnp.einsum("sqhd,skhd->shqk", d_mix, value_heads, preferred_element_type=jnp.float32)
    row_delta = jnp.sum(prob_again * d_prob, axis=-1, keepdims=True)
    d_scores = (prob_again * (d_prob - row_delta)).astype(jnp.bfloat16)
    d_q_heads = (
        jnp.einsum("shqk,skhd->sqhd", d_scores, key_heads, preferred_element_type=jnp.float32)
        * score_scale
    )
    d_key_heads = (
        jnp.einsum("shqk,sqhd->skhd", d_scores, q_turned, preferred_element_type=jnp.float32)
        * score_scale
    )
    d_value_heads = jnp.einsum(
        "shqk,sqhd->skhd",
        prob_again.astype(jnp.bfloat16),
        d_mix,
        preferred_element_type=jnp.float32,
    )
    d_key_mine, d_value_mine = (
        lax.psum_scatter(
            d_key_heads.reshape(seq_grp, seq_len, heads_cols).astype(jnp.bfloat16),
            "row",
            scatter_dimension=1,
            tiled=True,
        ).astype(jnp.float32),
        lax.psum_scatter(
            d_value_heads.reshape(seq_grp, seq_len, heads_cols).astype(jnp.bfloat16),
            "row",
            scatter_dimension=1,
            tiled=True,
        ).astype(jnp.float32),
    )
    d_q_normed = rotate_back(d_q_heads, cos_table, sin_table).reshape(tok_rows, heads_cols)
    d_k_normed = rotate_back(d_key_mine.reshape(head_shape), cos_table, sin_table).reshape(
        tok_rows, heads_cols
    )
    grad_q_gain_part = jnp.sum(d_q_normed * q_unit, axis=0)
    grad_k_gain_part = jnp.sum(d_k_normed * k_unit, axis=0)
    d_q_hat = d_q_normed * q_gain_f
    d_k_hat = d_k_normed * k_gain_f
    q_inner, k_inner = lax.psum(
        (jnp.sum(d_q_hat * q_unit, axis=1), jnp.sum(d_k_hat * k_unit, axis=1)), "col"
    )
    d_query = (q_scale * (d_q_hat - q_unit * (q_inner / width)[:, None])).astype(jnp.bfloat16)
    d_key = (k_scale * (d_k_hat - k_unit * (k_inner / width)[:, None])).astype(jnp.bfloat16)
    d_value = d_value_mine.reshape(tok_rows, heads_cols).astype(jnp.bfloat16)
    input_part = (
        through(d_query, full_query) + through(d_key, full_key) + through(d_value, full_value)
    )
    d_inputs = d_hidden + lax.psum(input_part.astype(jnp.bfloat16), "col").astype(jnp.float32)
    grad_in_low = (d_inputs * valid_rows).astype(jnp.bfloat16).reshape(seq_grp, tok_seq, width)
    output_low = result.astype(jnp.bfloat16).reshape(seq_grp, tok_seq, width)
    stat_slots = (peer_ids == my_group).astype(jnp.float32)[:, None] * local_sums[None, :]
    small_vec = jnp.concatenate([grad_q_gain_part, grad_k_gain_part, stat_slots.reshape(-1)])
    gains_two = jnp.stack([grad_attn_gain_part, grad_mlp_gain_part], axis=0)
    row_side = (inputs_low, d_attn_low, hidden_low, d_mlp_low)

    def make_term(per_dev, count_dev, reorder):
        cell_count = per_dev * 126
        tile_block = jnp.pad(small_vec, (0, cell_count - small_vec.shape[0])).reshape(per_dev, 126)
        tiled_block = jnp.tile(tile_block, (count_dev, 1))
        input_side = reorder(row_side[0])
        attn_side = reorder(row_side[1])
        hidden_side = reorder(row_side[2])
        inner_side = reorder(row_side[3])
        small_block = jnp.concatenate([reorder(gains_two).T, tiled_block], axis=1)

        def grad_term(row_start, row_count):
            return jnp.concatenate(
                [
                    against(input_side, d_query),
                    against(input_side, d_key),
                    against(input_side, d_value),
                    against(attn_side, attn_mix),
                    against(hidden_side, d_gate_low),
                    against(hidden_side, d_up_low),
                    against(inner_side, inner_low),
                    small_block,
                ],
                axis=1,
            )

        return grad_term

    per_rows = width // rows_axis
    grad_term = make_term(per_rows, rows_axis, unchanged)
    summed = lax.psum(
        lax.psum_scatter(
            grad_term(jnp.int32(0), per_rows * lax.axis_size("row")).astype(jnp.bfloat16),
            "row",
            scatter_dimension=0,
            tiled=True,
        ),
        "dp",
    ).astype(jnp.float32)
    home_out, home_grad = (
        lax.all_to_all(
            jnp.einsum(
                "jp,jtd->ptd", take_pick, output_low, preferred_element_type=jnp.float32
            ).astype(jnp.bfloat16),
            "dp",
            split_axis=0,
            concat_axis=0,
            tiled=True,
        ),
        lax.all_to_all(
            jnp.einsum(
                "jp,jtd->ptd", take_pick, grad_in_low, preferred_element_type=jnp.float32
            ).astype(jnp.bfloat16),
            "dp",
            split_axis=0,
            concat_axis=0,
            tiled=True,
        ),
    )
    output = jnp.einsum(
        "pj,ptd->jtd", send_pick, home_out, preferred_element_type=jnp.float32
    ).astype(jnp.bfloat16)
    grad_input = jnp.einsum(
        "pj,ptd->jtd", send_pick, home_grad, preferred_element_type=jnp.float32
    ).astype(jnp.bfloat16)
    grad_query = summed[:, :heads_cols]
    grad_key = summed[:, heads_cols : 2 * heads_cols]
    grad_value = summed[:, 2 * heads_cols : 3 * heads_cols]
    grad_out = summed[:, 3 * heads_cols : 4 * heads_cols].T
    base_col = 4 * heads_cols
    grad_gate = summed[:, base_col : base_col + ff_cols]
    grad_up = summed[:, base_col + ff_cols : base_col + 2 * ff_cols]
    grad_down = summed[:, base_col + 2 * ff_cols : base_col + 3 * ff_cols].T
    tail_cols = summed[:, base_col + 3 * ff_cols :]
    grad_attn_gain = tail_cols[:, 0]
    grad_mlp_gain = tail_cols[:, 1]
    vector = tail_cols[:, 2:].reshape(-1)
    grad_query_gain = vector[:heads_cols]
    grad_key_gain = vector[heads_cols : 2 * heads_cols]
    stat_sums = vector[2 * heads_cols : 2 * heads_cols + 3 * groups].reshape(groups, 3)
    member = ((deal_slot // seq_grp)[:, None] == peer_ids[None, :]).astype(jnp.float32)
    counts = jnp.sum(member * lengths.astype(jnp.float32)[:, None], axis=0)
    rms_stats = jnp.sqrt(stat_sums / (counts[:, None] * width))
    return (
        output,
        grad_input,
        grad_query,
        grad_key,
        grad_value,
        grad_out,
        grad_query_gain,
        grad_key_gain,
        grad_attn_gain,
        grad_gate,
        grad_up,
        grad_down,
        grad_mlp_gain,
        rms_stats,
    )


def solution(mesh):
    in_specs = (
        P("dp", "row", None),
        P("dp", "row", None),
        P(),
        P(),
        P("row", "col"),
        P("row", "col"),
        P("row", "col"),
        P("col", "row"),
        P("col"),
        P("col"),
        P("row"),
        P("row", "col"),
        P("row", "col"),
        P("col", "row"),
        P("row"),
    )
    out_specs = (
        P("dp", "row", None),
        P("dp", "row", None),
        P("row", "col"),
        P("row", "col"),
        P("row", "col"),
        P("col", "row"),
        P("col"),
        P("col"),
        P("row"),
        P("row", "col"),
        P("row", "col"),
        P("col", "row"),
        P("row"),
        P(),
    )
    return jax.shard_map(shards, mesh=mesh, in_specs=in_specs, out_specs=out_specs, check_vma=False)
```

profile of v0, /device:TPU:0, one launch (start us, length us, event | category | flops | bytes accessed | tf_op | source)
XLA Modules:
  0.0 2227.7 jit_solution(4983280698162245161)
XLA Ops:
  13.9 6.4 all-to-all-start
  21.1 47.5 %all-to-all-done = bf16[4,128,2048]{2,1,0:T(8,128)(2,1)S(1)} async-done(((bf16[4,128,2048]{2,1,0:T(8,128)(2,1)}), bf16[4,128,2048]{2,1,0:T(8,128)(2,1)S(1)}, u32[]{:S(2)}, u32[]{:S(2)}) %all-to-all-start) | async-done | bytes 2097184 | tf_op jit(solution)/shard_map/all_to_all | solution.py:99
  68.5 4.0 broadcast_multiply_fusion
  74.2 4.6 convolution_convert_fusion.16
  79.1 3.8 all-gather.16.cloned.1.call-done
  82.9 3.5 multiply_reduce_fusion.9
  86.4 32.6 %all-gather.18.cloned.1.call-done = bf16[2048,1024]{1,0:T(8,128)(2,1)} async-done(((bf16[512,1024]{1,0:T(8,128)(2,1)}), bf16[2048,1024]{1,0:T(8,128)(2,1)}) %all-gather.18.cloned.1.call-update) | async-done | bytes 4194320 | tf_op jit(solution)/shard_map/all_gather | solution.py:131
  119.0 3.5 multiply_reduce_fusion.8
  122.5 4.9 all-reduce.3
  132.6 11.0 all-gather.14.cloned.1.call-done
  146.5 22.0 all-gather.20.cloned.1.call-done
  175.1 29.3 %all-gather.22.cloned.1.call-done = bf16[1024,2048]{1,0:T(8,128)(2,1)} async-done(((bf16[1024,512]{1,0:T(8,128)(2,1)}), bf16[1024,2048]{1,0:T(8,128)(2,1)}) %all-gather.22.cloned.1.call-update) | async-done | bytes 4194320 | tf_op jit(solution)/shard_map/all_gather | solution.py:133
  204.4 4.8 fusion.45
  216.3 4.7 all-to-all-start.2
  221.0 5.6 all-gather
  226.6 45.7 %all-reduce.10.cloned.1.call-done = f32[256,2048]{1,0:T(8,128)} async-done(((f32[256,2048]{1,0:T(8,128)}), f32[256,2048]{1,0:T(8,128)}) %all-reduce.10.cloned.1.call-update) | async-done | bytes 2097168 | tf_op jit(solution)/shard_map/psum | solution.py:198
  275.9 103.9 %all-gather.24.cloned.1.call-done = bf16[2048,4096]{1,0:T(8,128)(2,1)} async-done(((bf16[512,4096]{1,0:T(8,128)(2,1)}), bf16[2048,4096]{1,0:T(8,128)(2,1)}) %all-gather.24.cloned.1.call-update) | async-done | bytes 16777232 | tf_op jit(solution)/shard_map/all_gather | solution.py:135
  379.9 12.8 fusion.84
  392.7 94.8 %all-gather.26.cloned.1.call-done = bf16[2048,4096]{1,0:T(8,128)(2,1)} async-done(((bf16[512,4096]{1,0:T(8,128)(2,1)}), bf16[2048,4096]{1,0:T(8,128)(2,1)}) %all-gather.26.cloned.1.call-update) | async-done | bytes 16777232 | tf_op jit(solution)/shard_map/all_gather | solution.py:136
  487.5 15.2 multiply_convert_fusion.4
  502.7 92.2 %all-gather.28.cloned.1.call-done = bf16[4096,2048]{1,0:T(8,128)(2,1)} async-done(((bf16[4096,512]{1,0:T(8,128)(2,1)}), bf16[4096,2048]{1,0:T(8,128)(2,1)}) %all-gather.28.cloned.1.call-update) | async-done | bytes 16777232 | tf_op jit(solution)/shard_map/all_gather | solution.py:137
  594.9 11.9 convolution_convert_fusion.10
  607.1 5.2 all-gather.1
  612.2 3.4 fusion.8
  618.2 28.9 %all-reduce.12.cloned.1.call-done = bf16[256,2048]{1,0:T(8,128)(2,1)} async-done(((bf16[256,2048]{1,0:T(8,128)(2,1)}), bf16[256,2048]{1,0:T(8,128)(2,1)}) %all-reduce.12.cloned.1.call-update) | async-done | bytes 1048592 | tf_op jit(solution)/shard_map/psum | solution.py:210
  648.7 3.7 fusion.18
  653.1 12.8 multiply_convert_fusion.2
  665.9 12.2 fusion.85
  678.1 12.8 convolution_add_fusion.2
  691.0 63.0 %all-reduce.14.cloned.1.call-done = f32[256,2048]{1,0:T(8,128)} async-done(((f32[256,2048]{1,0:T(8,128)}), f32[256,2048]{1,0:T(8,128)}) %all-reduce.14.cloned.1.call-update) | async-done | bytes 2097168 | tf_op jit(solution)/shard_map/psum | solution.py:235
  754.0 5.2 multiply_reduce_fusion.3
  766.4 3.9 multiply_reduce_fusion
  773.8 6.2 copy.178
  780.0 3.6 copy.191
  784.8 10.5 convolution_convert_fusion.2
  795.3 9.8 convolution_convert_fusion.1
  805.1 12.3 convolution_convert_fusion
  817.5 4.3 fusion.28
  821.8 3.9 copy.157
  827.0 4.4 convolution_convert_fusion.3
  831.3 6.7 copy.168
  852.0 4.9 all-reduce.2
  859.3 3.3 convolution_convert_fusion.5
  862.6 6.5 copy.165
  870.2 3.3 convolution_convert_fusion.4
  873.5 6.5 copy.166
  880.0 4.5 bitcast_convert_fusion
  884.5 6.5 copy.167
  891.7 154.4 %concatenate.26 = bf16[2048,16512]{1,0:T(8,128)(2,1)} concatenate(bf16[2048,1024]{1,0:T(8,128)(2,1)} %copy.165, bf16[2048,1024]{1,0:T(8,128)(2,1)} %copy.166, bf16[2048,1024]{1,0:T(8,128)(2,1)} %copy.167, bf16[2048,1024]{1,0:T(8,128)(2,1)} %copy.168, bf16[2048,4096]{1,0:T(8,128)(2,1)} %convolution_convert_fusion.2, bf16[2048,4096]{1,0:T(8,128)(2,1)} %convolution_convert_fusion.1, ...), dimensions={1} | concatenate | bytes 135266304 | tf_op jit(solution)/shard_map/concatenate | solution.py:312
  1047.1 3.6 fusion.86
  1056.1 446.0 %reduce-scatter.12.cloned.1.call-done = bf16[512,16512]{1,0:T(8,128)(2,1)} async-done(((bf16[2048,16512]{1,0:T(8,128)(2,1)}), bf16[512,16512]{1,0:T(8,128)(2,1)}) %reduce-scatter.12.cloned.1.call-update) | async-done | bytes 16908304
  1507.7 4.7 all-to-all-start.1
  1512.4 32.5 %all-reduce.16.cloned.1.call-done = bf16[256,2048]{1,0:T(8,128)(2,1)} async-done(((bf16[256,2048]{1,0:T(8,128)(2,1)}), bf16[256,2048]{1,0:T(8,128)(2,1)}) %all-reduce.16.cloned.1.call-update) | async-done | bytes 1048592 | tf_op jit(solution)/shard_map/psum | solution.py:293
  1550.8 27.5 %all-to-all-done.1 = bf16[4,128,2048]{2,1,0:T(8,128)(2,1)} async-done(((bf16[4,128,2048]{2,1,0:T(8,128)(2,1)}), bf16[4,128,2048]{2,1,0:T(8,128)(2,1)}, u32[]{:S(2)}, u32[]{:S(2)}) %all-to-all-start.1) | async-done | bytes 2097184 | tf_op jit(solution)/shard_map/all_to_all | solution.py:340
  1578.3 6.5 all-to-all-start.3
  1584.9 3.4 convolution_convert_fusion.13
  1589.7 93.7 %all-to-all-done.3 = bf16[4,128,2048]{2,1,0:T(8,128)(2,1)S(1)} async-done(((bf16[4,128,2048]{2,1,0:T(8,128)(2,1)}), bf16[4,128,2048]{2,1,0:T(8,128)(2,1)S(1)}, u32[]{:S(2)}, u32[]{:S(2)}) %all-to-all-start.3) | async-done | bytes 2097184 | tf_op jit(solution)/shard_map/all_to_all | solution.py:349
  1686.5 475.7 %all-reduce.18.cloned.1.call-done = bf16[512,16512]{1,0:T(8,128)(2,1)} async-done(((bf16[512,16512]{1,0:T(8,128)(2,1)}), bf16[512,16512]{1,0:T(8,128)(2,1)}) %all-reduce.18.cloned.1.call-update) | async-done | bytes 16908304 | tf_op jit(solution)/shard_map/psum | solution.py:330
  2162.2 8.6 convert_element_type.256
  2171.1 10.9 copy-done.4
  2182.8 7.8 slice_bitcast_fusion
  2194.2 8.9 copy.172
  2203.9 4.8 fusion.78
  2208.7 12.0 fusion.77
  (273 shorter events, 98.1 us)
Async XLA Ops:
  7.2 2.4 copy-start
  7.2 2.2 copy-start.60
  7.2 66.9 %all-gather.12.cloned.1.call-start = ((), (), s32[]{:S(2)}) async-start(), calls=%async_computation.7 | async-start | bytes 5242880 | tf_op jit(solution)/shard_map/all_gather | solution.py:132
  7.9 75.0 %all-gather.16.cloned.1.call-start = ((), (), s32[]{:S(2)}) async-start(), calls=%async_computation.9 | async-start | bytes 5242880 | tf_op jit(solution)/shard_map/all_gather | solution.py:130
  8.7 110.3 %all-gather.18.cloned.1.call-start = ((), (), s32[]{:S(2)}) async-start(), calls=%async_computation.10 | async-start | bytes 5242880 | tf_op jit(solution)/shard_map/all_gather | solution.py:131
  9.5 201.8 %copy-start.62 = (s32[2]{0:T(128)}, s32[2]{0:T(128)S(1)}, u32[]{:S(2)}) copy-start(s32[2]{0:T(128)S(1)} %and_select_fusion.2) | copy-start | bytes 28
  13.9 6.7 copy-start.58
  13.9 7.1 copy-start.49
  13.9 7.1 copy-start.50
  13.9 54.6 %all-to-all-start = ((bf16[4,128,2048]{2,1,0:T(8,128)(2,1)}), bf16[4,128,2048]{2,1,0:T(8,128)(2,1)S(1)}, u32[]{:S(2)}, u32[]{:S(2)}) async-start(bf16[4,128,2048]{2,1,0:T(8,128)(2,1)} %copy.130), calls=%async_computation | async-start | bytes 4194304 | tf_op jit(solution)/shard_map/all_to_all | solution.py:99
  20.3 123.3 %all-gather.14.cloned.1.call-start = ((), (), s32[]{:S(2)}) async-start(), calls=%async_computation.8 | async-start | bytes 2621440 | tf_op jit(solution)/shard_map/all_gather | solution.py:166
  21.0 106.5 %copy-start.43 = (f32[1024]{0:T(1024)}, f32[1024]{0:T(1024)S(1)}, u32[]{:S(2)}) copy-start(f32[1024]{0:T(1024)S(1)} %convert_element_type.210) | copy-start | bytes 12292
  21.0 107.1 %copy-start.41 = (f32[1024]{0:T(1024)}, f32[1024]{0:T(1024)S(1)}, u32[]{:S(2)}) copy-start(f32[1024]{0:T(1024)S(1)} %convert_element_type.213) | copy-start | bytes 12292
  21.0 591.2 %copy-start.53 = (s32[2]{0:T(128)}, s32[2]{0:T(128)S(1)}, u32[]{:S(2)}) copy-start(s32[2]{0:T(128)S(1)} %and_select_fusion.1) | copy-start | bytes 28
  74.1 44.9 %copy-start.9 = (bf16[256,2048]{1,0:T(8,128)(2,1)}, bf16[256,2048]{1,0:T(8,128)(2,1)S(1)}, u32[]{:S(2)}) copy-start(bf16[256,2048]{1,0:T(8,128)(2,1)S(1)} %bitcast_multiply_fusion.5) | copy-start | bytes 3145732
  78.8 89.7 %all-gather.20.cloned.1.call-start = ((), (), s32[]{:S(2)}) async-start(), calls=%async_computation.11 | async-start | bytes 2621440 | tf_op jit(solution)/shard_map/all_gather | solution.py:165
  86.4 41.0 %copy-start.18 = (f32[256,1024]{1,0:T(8,128)}, f32[256,1024]{1,0:T(8,128)S(1)}, u32[]{:S(2)}) copy-start(f32[256,1024]{1,0:T(8,128)S(1)} %get-tuple-element.126) | copy-start | bytes 3145732
  122.5 5.5 copy-start.15
  130.1 38.3 %copy-start.25 = (bf16[2,128,8,64]{3,1,2,0:T(8,128)(2,1)}, bf16[2,128,8,64]{3,1,2,0:T(8,128)(2,1)S(1)}, u32[]{:S(2)}) copy-start(bf16[2,128,8,64]{3,1,2,0:T(8,128)(2,1)S(1)} %get-tuple-element.100) | copy-start | bytes 786436
  130.2 38.3 %copy-start.27 = (bf16[2,128,8,64]{3,1,2,0:T(8,128)(2,1)}, bf16[2,128,8,64]{3,1,2,0:T(8,128)(2,1)S(1)}, u32[]{:S(2)}) copy-start(bf16[2,128,8,64]{3,1,2,0:T(8,128)(2,1)S(1)} %get-tuple-element.101) | copy-start | bytes 786436
  131.5 72.9 %all-gather.22.cloned.1.call-start = ((), (), s32[]{:S(2)}) async-start(), calls=%async_computation.12 | async-start | bytes 5242880 | tf_op jit(solution)/shard_map/all_gather | solution.py:133
  132.1 140.2 %all-reduce.10.cloned.1.call-start = ((), (), s32[]{:S(2)}) async-start(), calls=%async_computation.13 | async-start | bytes 4194304 | tf_op jit(solution)/shard_map/psum | solution.py:198
  146.5 25.9 %copy-start.20 = (bf16[2,512,1024]{1,2,0:T(8,128)(2,1)}, bf16[2,512,1024]{1,2,0:T(8,128)(2,1)S(1)}, u32[]{:S(2)}) copy-start(bf16[2,512,1024]{1,2,0:T(8,128)(2,1)S(1)} %copy.133) | copy-start | bytes 6291460
  171.2 2.0 copy-start.2
  175.1 34.1 %copy-start.36 = (bf16[2,128,8,128]{3,2,1,0:T(8,128)(2,1)}, bf16[2,128,8,128]{3,2,1,0:T(8,128)(2,1)S(1)}, u32[]{:S(2)}) copy-start(bf16[2,128,8,128]{3,2,1,0:T(8,128)(2,1)S(1)} %copy.140) | copy-start | bytes 1572868
  209.2 170.7 %all-gather.24.cloned.1.call-start = ((), (), s32[]{:S(2)}) async-start(), calls=%async_computation.14 | async-start | bytes 20971520 | tf_op jit(solution)/shard_map/all_gather | solution.py:135
  209.9 277.5 %all-gather.26.cloned.1.call-start = ((), (), s32[]{:S(2)}) async-start(), calls=%async_computation.15 | async-start | bytes 20971520 | tf_op jit(solution)/shard_map/all_gather | solution.py:136
  210.7 384.2 %all-gather.28.cloned.1.call-start = ((), (), s32[]{:S(2)}) async-start(), calls=%async_computation.16 | async-start | bytes 20971520 | tf_op jit(solution)/shard_map/all_gather | solution.py:137
  216.3 4.7 copy-start.51
  216.3 58.0 %copy-start.12 = (bf16[2,128,2048]{2,1,0:T(8,128)(2,1)S(1)}, bf16[2,128,2048]{2,1,0:T(8,128)(2,1)}, u32[]{:S(2)}) copy-start(bf16[2,128,2048]{2,1,0:T(8,128)(2,1)} %copy-done.11) | copy-start | bytes 3145732
  216.3 396.0 %all-to-all-start.2 = ((bf16[4,128,2048]{2,1,0:T(8,128)(2,1)}), bf16[4,128,2048]{2,1,0:T(8,128)(2,1)}, u32[]{:S(2)}, u32[]{:S(2)}) async-start(bf16[4,128,2048]{2,1,0:T(8,128)(2,1)} %copy.145), calls=%async_computation.2 | async-start | bytes 4194304 | tf_op jit(solution)/shard_map/all_to_all | solution.py:100
  221.0 426.0 %all-reduce.12.cloned.1.call-start = ((), (), s32[]{:S(2)}) async-start(), calls=%async_computation.17 | async-start | bytes 2097152 | tf_op jit(solution)/shard_map/psum | solution.py:210
  272.3 2.2 copy-start.5
  594.9 12.1 copy-start.52
  606.8 147.2 %all-reduce.14.cloned.1.call-start = ((), (), s32[]{:S(2)}) async-start(), calls=%async_computation.18 | async-start | bytes 4194304 | tf_op jit(solution)/shard_map/psum | solution.py:235
  647.0 5.4 copy-start.6
  647.0 5.4 copy-start.13
  653.0 12.8 copy-start.24
  690.9 152.7 %reduce-scatter.10.cloned.1.call-start = ((), (), s32[]{:S(2)}) async-start(), calls=%async_computation.22 | async-start | bytes 2621440
  759.2 1.3 copy-start.7
  760.5 2.2 copy-start.56
  764.0 2.3 copy-start.21
  766.3 3.9 copy-start.31
  766.4 3.9 copy-start.3
  783.6 96.4 %reduce-scatter.8.cloned.1.call-start = ((), (), s32[]{:S(2)}) async-start(), calls=%async_computation.19 | async-start | bytes 2621440 | tf_op jit(solution)/shard_map/reduce_scatter | solution.py:269
  805.1 12.3 copy-start.32
  825.8 676.3 %reduce-scatter.12.cloned.1.call-start = ((), (), s32[]{:S(2)}) async-start(), calls=%async_computation.23 | async-start | bytes 84541440
  851.6 7.7 copy-start.10
  862.6 6.5 copy-start.17
  873.5 6.5 copy-start.34
  884.5 7.2 copy-start.35
  1046.1 4.6 copy-start.30
  1046.1 498.8 %all-reduce.16.cloned.1.call-start = ((), (), s32[]{:S(2)}) async-start(), calls=%async_computation.20 | async-start | bytes 2097152 | tf_op jit(solution)/shard_map/psum | solution.py:293
  1047.1 3.6 copy-start.33
  1050.7 3.0 copy-start.55
  1056.1 1106.1 %all-reduce.18.cloned.1.call-start = ((), (), s32[]{:S(2)}) async-start(), calls=%async_computation.21 | async-start | bytes 33816576 | tf_op jit(solution)/shard_map/psum | solution.py:330
  1507.7 37.2 %copy-start.8 = (f32[256,2048]{1,0:T(8,128)S(1)}, f32[256,2048]{1,0:T(8,128)}, u32[]{:S(2)}) copy-start(f32[256,2048]{1,0:T(8,128)} %copy-done.7) | copy-start | bytes 6291460
  1507.7 70.6 %all-to-all-start.1 = ((bf16[4,128,2048]{2,1,0:T(8,128)(2,1)}), bf16[4,128,2048]{2,1,0:T(8,128)(2,1)}, u32[]{:S(2)}, u32[]{:S(2)}) async-start(bf16[4,128,2048]{2,1,0:T(8,128)(2,1)} %copy.142), calls=%async_computation.1 | async-start | bytes 4194304 | tf_op jit(solution)/shard_map/all_to_all | solution.py:340
  1550.8 34.0 %copy-start.59 = (s32[8]{0:T(128)S(1)}, s32[8]{0:T(128)}, u32[]{:S(2)}) copy-start(s32[8]{0:T(128)} %param.17) | copy-start | bytes 100
  1550.8 34.0 %copy-start.61 = (s32[8]{0:T(128)S(1)}, s32[8]{0:T(128)}, u32[]{:S(2)}) copy-start(s32[8]{0:T(128)} %param.18) | copy-start | bytes 100
  1550.8 34.2 %copy-start.63 = (s32[2]{0:T(128)S(1)}, s32[2]{0:T(128)}, u32[]{:S(2)}) copy-start(s32[2]{0:T(128)} %copy-done.62) | copy-start | bytes 28
  1578.3 105.1 %all-to-all-start.3 = ((bf16[4,128,2048]{2,1,0:T(8,128)(2,1)}), bf16[4,128,2048]{2,1,0:T(8,128)(2,1)S(1)}, u32[]{:S(2)}, u32[]{:S(2)}) async-start(bf16[4,128,2048]{2,1,0:T(8,128)(2,1)} %copy.159), calls=%async_computation.4 | async-start | bytes 4194304 | tf_op jit(solution)/shard_map/all_to_all | solution.py:349
  2170.8 11.1 copy-start.4
  2208.7 12.0 copy-start.1
  (21 other events, 23.3 us)
Sparse Core Ops, SparseCore 0:
  9.6 37.1 all-gather.11
  48.4 34.5 all-gather.15
  84.5 34.4 all-gather.17
  121.0 22.5 all-gather.13
  145.6 22.8 all-gather.19
  169.9 34.4 all-gather.21
  209.3 62.9 all-reduce.9
  273.9 105.9 all-gather.23
  381.5 105.9 all-gather.25
  488.9 105.9 all-gather.27
  606.9 40.0 all-reduce.11
  691.0 62.9 all-reduce.13
  783.7 31.3 reduce-scatter.9
  825.9 31.6 reduce-scatter.7
  1046.2 455.8 reduce-scatter.11
  1504.8 40.0 all-reduce.15
  1547.4 614.7 all-reduce.17
where the time goes:
time: 2250 us; the launch traced here: 2230 us
  waiting for transfers between devices  1650 us (73%)
  local copies, waits for them, and re-layouts  288 us (13%)
  matrix products  188 us (8%)
  other arithmetic  37 us (2%)
  starting transfers between devices  23.6 us (1%)
    psum x1, waiting for transfers between devices, shards(): lax.psum(lax.psum_scatter(grad_term(jnp.int32(0), per_rows * lax.axis_siz...  476 us
    unnamed x19, waiting for transfers between devices  451 us
    concatenate x1, local copies, waits for them, and re-layouts, grad_term(): jnp.concatenate([against(input_side, d_query), against(input_side, d_key)...  154 us
    all_gather x1, waiting for transfers between devices, shards(): lax.all_gather(gate_weight, 'row', axis=0, tiled=True)  104 us
    all_gather x1, waiting for transfers between devices, shards(): lax.all_gather(up_weight, 'row', axis=0, tiled=True)  94.8 us
    all_to_all x1, waiting for transfers between devices, shards(): lax.all_to_all(jnp.einsum('jp,jtd->ptd', take_pick, grad_in_low, preferre...  93.7 us
    all_gather x1, waiting for transfers between devices, shards(): lax.all_gather(down_weight, 'row', axis=1, tiled=True)  92.2 us
    psum x1, waiting for transfers between devices, shards(): lax.psum(through(d_gate_low, full_gate) + through(d_up_low, full_up), 'col')  63 us
  transfers between devices with their start and end apart: 21, of which 17 were waited for; matrix products, arithmetic and copies ran while one was open for 9% of the time, Pallas kernels for 0%

commit v1 on v0

v1 whole, which is shorter than its diff:
```python
import jax
import jax.numpy as jnp
from jax import lax
from jax.sharding import PartitionSpec as P

HD = 128
EPSILON = 1e-06
ROPE_THETA = 500000.0
MASK_VALUE = 1e30
BF = jnp.bfloat16
F32 = jnp.float32


def rms_scale(matrix):
    return lax.rsqrt(jnp.mean(matrix * matrix, axis=-1, keepdims=True) + EPSILON)


def rotate_pairs(matrix, cos_table, sin_table):
    half_size = matrix.shape[-1] // 2
    first_half = matrix[..., :half_size]
    second_half = matrix[..., half_size:]
    return jnp.concatenate(
        [
            first_half * cos_table - second_half * sin_table,
            second_half * cos_table + first_half * sin_table,
        ],
        axis=-1,
    )


def dot(left_side, right_side):
    return jnp.dot(left_side, right_side, preferred_element_type=F32)


def against(left_side, right_side):
    return lax.dot_general(
        left_side, right_side, (((0,), (0,)), ((), ())), preferred_element_type=F32
    )


def through(left_side, weight):
    return lax.dot_general(
        left_side, weight, (((1,), (1,)), ((), ())), preferred_element_type=F32
    )


class Plane:
    def __init__(self, width):
        self.rows = lax.axis_size("row")
        self.cols = lax.axis_size("col")
        self.row = lax.axis_index("row")
        self.col = lax.axis_index("col")
        self.part = width // self.rows

    def hop(self, array, row_xor, col_xor=0):
        if row_xor and col_xor:
            pairs = [
                (a * self.cols + b, (a ^ row_xor) * self.cols + (b ^ col_xor))
                for a in range(self.rows)
                for b in range(self.cols)
            ]
            return lax.ppermute(array, ("row", "col"), pairs)
        if row_xor:
            return lax.ppermute(array, "row", [(a, a ^ row_xor) for a in range(self.rows)])
        if col_xor:
            return lax.ppermute(array, "col", [(a, a ^ col_xor) for a in range(self.cols)])
        return array

    def slot(self, array, index):
        return array[..., index * self.part : (index + 1) * self.part]

    def turn(self, array, row_xor):
        if row_xor == 0:
            return array
        return jnp.concatenate(
            [self.slot(array, index ^ row_xor) for index in range(self.rows)], axis=-1
        )

    def relative(self, array):
        return jnp.concatenate(
            [
                lax.dynamic_slice_in_dim(
                    array, (self.row ^ index) * self.part, self.part, axis=array.ndim - 1
                )
                for index in range(self.rows)
            ],
            axis=-1,
        )

    def gather(self, own):
        blocks = {(0, 0): own}
        if self.rows == 4 and self.cols == 2:
            half = own.shape[0] // 2
            blocks[0, 2] = self.hop(self.turn(own, 2), 2)
            blocks[1, 0] = self.hop(own, 0, 1)
            blocks[1, 2] = jnp.concatenate(
                [
                    self.hop(blocks[0, 2][:half], 0, 1),
                    self.hop(self.turn(blocks[1, 0][half:], 2), 2),
                ],
                axis=0,
            )
        else:
            for col_xor in reversed(range(self.cols)):
                for row_xor in reversed(range(0, self.rows, 2)):
                    blocks[col_xor, row_xor] = self.hop(self.turn(own, row_xor), row_xor, col_xor)
        return self.over_cores(blocks)

    def over_cores(self, blocks):
        for col_xor in range(self.cols):
            for row_xor in range(0, self.rows, 2):
                blocks[col_xor, row_xor + 1] = self.hop(
                    self.turn(blocks[col_xor, row_xor], 1), 1
                )
        return jnp.concatenate(
            [blocks[b, a] for b in range(self.cols) for a in range(self.rows)], axis=0
        )

    def gather_columns(self, own):
        blocks = {}
        for row_xor in range(0, self.rows, 2):
            arrived = self.hop(self.turn(own[0], row_xor), row_xor)
            for col_xor in range(self.cols):
                if row_xor:
                    blocks[col_xor, row_xor] = self.hop(arrived, 0, col_xor)
                else:
                    blocks[col_xor, row_xor] = own[col_xor]
        return self.over_cores(blocks)

    def scatter(self, partial):
        tokens = partial.shape[0] // (self.rows * self.cols)
        blocks = partial.reshape(self.cols, self.rows, tokens, -1)
        if self.rows == 4 and self.cols == 2:
            half = tokens // 2
            away = self.hop(self.turn(jnp.stack([blocks[:, 1], blocks[:, 3]]), 1), 1)
            near = [blocks[:, 2 * k].astype(F32) + away[k].astype(F32) for k in range(2)]
            by_row = self.hop(self.turn(near[1][:, :half].astype(BF), 2), 2).astype(F32)
            far = jnp.stack([near[0][1, half:], near[1][1, half:]]).astype(BF)
            by_col = self.hop(far, 0, 1).astype(F32)
            first = [near[0][k, :half] + by_row[k] for k in range(2)]
            second = [near[k][0, half:] + by_col[k] for k in range(2)]
            last_col = self.hop(first[1].astype(BF), 0, 1).astype(F32)
            last_row = self.hop(self.turn(second[1].astype(BF), 2), 2).astype(F32)
            return jnp.concatenate([first[0] + last_col, second[0] + last_row], axis=0)
        sums = {}
        for col_xor in reversed(range(self.cols)):
            for row_xor in reversed(range(0, self.rows, 2)):
                arrived = self.hop(self.turn(blocks[col_xor, row_xor + 1], 1), 1)
                sums[col_xor, row_xor] = blocks[col_xor, row_xor].astype(F32) + arrived.astype(F32)
        total = sums[0, 0]
        for col_xor in reversed(range(self.cols)):
            for row_xor in reversed(range(0, self.rows, 2)):
                if col_xor or row_xor:
                    sent = self.turn(sums[col_xor, row_xor].astype(BF), row_xor)
                    total = total + self.hop(sent, row_xor, col_xor).astype(F32)
        return total

    def total(self, array):
        blocks = array.reshape(array.shape[:-1] + (self.cols, self.rows, -1))
        row_xor = 1
        while row_xor < self.rows:
            order = [index ^ row_xor for index in range(self.rows)]
            arrived = self.hop(blocks, row_xor)
            blocks = blocks + jnp.stack([arrived[..., k, :] for k in order], axis=-2)
            row_xor *= 2
        col_xor = 1
        while col_xor < self.cols:
            order = [index ^ col_xor for index in range(self.cols)]
            arrived = self.hop(blocks, 0, col_xor)
            blocks = blocks + jnp.stack([arrived[..., k, :, :] for k in order], axis=-3)
            col_xor *= 2
        return blocks.reshape(array.shape)


ENDS = [(0, 1), (1, 0), (2, 3), (3, 2)]
MIDDLE = [(1, 2), (2, 1)]


def plus(one, other):
    return (one.astype(F32) + other.astype(F32)).astype(BF)


def group_sums(arrays, lag=3):
    if lax.axis_size("dp") != 4:
        return [lax.psum(array, "dp") for array in arrays]
    place = lax.axis_index("dp")
    inner = (place == 1) | (place == 2)
    count = len(arrays)
    arrived, full, result = {}, {}, {}
    for step in range(count + lag):
        back = step - lag
        array = arrays[step] if step < count else None
        if back >= 0 and array is not None and full[back].shape == array.shape:
            sent = jnp.where(inner, full[back], array)
            arrived[step] = lax.ppermute(sent, "dp", ENDS)
            result[back] = jnp.where(inner, sent, arrived[step])
        else:
            if back >= 0 and array is not None:
                full[back], array = lax.optimization_barrier((full[back], array))
            if array is not None:
                arrived[step] = lax.ppermute(array, "dp", [(0, 1), (3, 2)])
            if back >= 0:
                again = lax.ppermute(full[back], "dp", [(1, 0), (2, 3)])
                result[back] = jnp.where(inner, full[back], again)
        if array is not None:
            pair = plus(array, arrived[step])
            full[step] = plus(pair, lax.ppermute(pair, "dp", MIDDLE))
    return [result[k] for k in range(count)]


def group_total(vector):
    if lax.axis_size("dp") != 4:
        return lax.psum(vector, "dp")
    place = lax.axis_index("dp")
    inner = (place == 1) | (place == 2)
    vector = vector + lax.ppermute(vector, "dp", [(0, 1), (3, 2)])
    vector = vector + lax.ppermute(vector, "dp", MIDDLE)
    return jnp.where(inner, vector, lax.ppermute(vector, "dp", [(1, 0), (2, 3)]))


def shards(
    layer_input,
    cotangent,
    lengths,
    deal_slot,
    query_weight,
    key_weight,
    value_weight,
    out_weight,
    query_gain,
    key_gain,
    attn_gain,
    gate_weight,
    up_weight,
    down_weight,
    mlp_gain,
):
    groups = lax.axis_size("dp")
    my_group = lax.axis_index("dp")
    seq_grp, tok_seq, width = layer_input.shape
    seq_count = lengths.shape[0]
    plane = Plane(width)
    rows, cols, row, col, part = plane.rows, plane.cols, plane.row, plane.col, plane.part
    seq_own = seq_grp // cols
    tok_own = seq_own * tok_seq
    seq_len = tok_seq * rows
    tok_all = seq_grp * seq_len
    heads_cols = query_weight.shape[1]
    head_part = heads_cols // rows
    heads_here = head_part // HD
    ff_part = gate_weight.shape[1] // rows

    first_own = col * seq_own
    all_input = plane.relative(layer_input)
    own_cot = plane.relative(
        lax.dynamic_slice_in_dim(cotangent, first_own, seq_own, axis=0).reshape(tok_own, width)
    )
    own_places = row * tok_seq + jnp.arange(tok_seq, dtype=jnp.int32)
    group_len = lax.dynamic_slice_in_dim(lengths, my_group * seq_grp, seq_grp)
    valid_all = (own_places[None, :] < group_len[:, None]).astype(BF)
    all_input = (all_input * valid_all[:, :, None]).reshape(cols, tok_own, width)
    all_input = jnp.stack(
        [
            lax.dynamic_index_in_dim(all_input, col ^ index, axis=0, keepdims=False)
            for index in range(cols)
        ]
    )
    inputs_low = all_input[0]
    own_len = lax.dynamic_slice_in_dim(lengths, my_group * seq_grp + first_own, seq_own)
    valid_rows = (own_places[None, :] < own_len[:, None]).astype(F32).reshape(tok_own, 1)
    inputs = inputs_low.astype(F32)
    d_full = own_cot.astype(F32) * valid_rows
    inputs_all = plane.gather_columns(all_input)

    def pieces_of(weight, axis):
        size = weight.shape[axis] // rows
        return [
            lax.dynamic_slice_in_dim(weight, (row ^ k) * size, size, axis=axis)
            for k in range(rows)
        ]

    def shared(weight, axis):
        pieces = pieces_of(weight, axis)
        size = pieces[0].shape[0] // groups
        parts = [
            plane.hop(lax.dynamic_slice_in_dim(piece, my_group * size, size, axis=0), k)
            for k, piece in enumerate(pieces)
            if k >= 2
        ]
        far = lax.all_gather(jnp.concatenate(parts, axis=1), "dp", axis=0, tiled=True)
        far = jnp.split(far, rows - 2, axis=1)
        return pieces[:1] + [plane.hop(pieces[1], 1)] + far

    trios = zip(
        pieces_of(query_weight, 1), pieces_of(key_weight, 1), pieces_of(value_weight, 1), strict=True
    )
    trios = [plane.hop(jnp.stack(trio), k) for k, trio in enumerate(trios)]
    w_query, w_key, w_value = (
        jnp.concatenate([trio[k] for trio in trios], axis=0) for k in range(3)
    )
    w_gate = jnp.concatenate(shared(gate_weight, 1), axis=0)
    w_out = jnp.concatenate(
        [plane.hop(piece, k) for k, piece in enumerate(pieces_of(out_weight, 0))], axis=1
    )
    w_up = jnp.concatenate(shared(up_weight, 1), axis=0)
    w_down = jnp.concatenate(shared(down_weight, 0), axis=1)
    gains = jnp.stack([attn_gain, mlp_gain])
    gains = jnp.concatenate([plane.hop(gains, k) for k in range(rows)], axis=1).astype(F32)
    attn_gain_f, mlp_gain_f = gains[0:1], gains[1:2]
    q_gain_f = lax.dynamic_slice_in_dim(query_gain, row * head_part, head_part).astype(F32)
    k_gain_f = lax.dynamic_slice_in_dim(key_gain, row * head_part, head_part).astype(F32)

    def by_sequence(array):
        shape = (cols, rows, seq_own, tok_seq) + array.shape[1:]
        return jnp.swapaxes(array.reshape(shape), 1, 2).reshape(
            (seq_grp, seq_len) + array.shape[1:]
        )

    def by_block(array):
        shape = (cols, seq_own, rows, tok_seq) + array.shape[2:]
        return jnp.swapaxes(array.reshape(shape), 1, 2).reshape((tok_all,) + array.shape[2:])

    query_raw = dot(inputs_all, w_query)
    key_raw = dot(inputs_all, w_key)
    value_low = dot(inputs_all, w_value).astype(BF)
    squares = jnp.stack(
        [jnp.sum(query_raw * query_raw, axis=1), jnp.sum(key_raw * key_raw, axis=1)]
    )
    scales = lax.rsqrt(plane.total(squares) / width + EPSILON)
    q_scale = scales[0][:, None]
    k_scale = scales[1][:, None]
    q_unit = query_raw * q_scale
    k_unit = key_raw * k_scale
    block_rows = row ^ jnp.arange(rows, dtype=jnp.int32)
    places = (
        block_rows[:, None] * tok_seq + jnp.arange(tok_seq, dtype=jnp.int32)[None, :]
    ).reshape(seq_len)
    block_cols = col ^ jnp.arange(cols, dtype=jnp.int32)
    seq_ids = (
        my_group * seq_grp
        + block_cols[:, None] * seq_own
        + jnp.arange(seq_own, dtype=jnp.int32)[None, :]
    ).reshape(seq_grp)
    live_len = jnp.sum(
        jnp.where(
            seq_ids[:, None] == jnp.arange(seq_count, dtype=jnp.int32)[None, :], lengths[None, :], 0
        ),
        axis=1,
    )
    frequency = ROPE_THETA ** (-(jnp.arange(HD // 2).astype(F32) * 2.0 / HD))
    angles = places.astype(F32)[:, None] * frequency[None, :]
    cos_table = jnp.cos(angles)[None, :, None, :]
    sin_table = jnp.sin(angles)[None, :, None, :]
    head_shape = (seq_grp, seq_len, heads_here, HD)

    def heads_of(array):
        return by_sequence(array).reshape(head_shape)

    def joined(array):
        return by_block(array.reshape(seq_grp, seq_len, head_part))

    q_rot = rotate_pairs(heads_of(q_unit * q_gain_f), cos_table, sin_table).astype(BF)
    k_rot = rotate_pairs(heads_of(k_unit * k_gain_f), cos_table, sin_table).astype(BF)
    values = heads_of(value_low)
    allowed = (places[None, None, :] <= places[None, :, None]) & (
        places[None, None, :] < live_len[:, None, None]
    )
    score_scale = HD ** (-0.5)
    scores = (
        jnp.einsum("sqhd,skhd->shqk", q_rot, k_rot, preferred_element_type=F32) * score_scale
    )
    scores = jnp.where(allowed[:, None], scores, -MASK_VALUE)
    exponent = jnp.exp(scores - jnp.max(scores, axis=-1, keepdims=True))
    prob = exponent / jnp.sum(exponent, axis=-1, keepdims=True)
    prob_low = prob.astype(BF)
    attn_mix = joined(
        jnp.einsum("shqk,skhd->sqhd", prob_low, values, preferred_element_type=F32).astype(BF)
    )
    attn_raw = plane.scatter(dot(attn_mix, w_out).astype(BF))
    a_scale = rms_scale(attn_raw)
    a_unit = attn_raw * a_scale
    branch_a = a_unit * attn_gain_f
    hidden = inputs + branch_a
    hidden_all = plane.gather(hidden.astype(BF))
    gate_pre = dot(hidden_all, w_gate)
    up_pre = dot(hidden_all, w_up)
    gate_sig = jax.nn.sigmoid(gate_pre)
    gate_act = gate_pre * gate_sig
    inner_low = (gate_act * up_pre).astype(BF)
    mlp_raw = plane.scatter(dot(inner_low, w_down).astype(BF))
    m_scale = rms_scale(mlp_raw)
    m_unit = mlp_raw * m_scale
    branch_m = m_unit * mlp_gain_f
    result = (hidden + branch_m) * valid_rows

    d_m_unit = d_full * mlp_gain_f
    d_mlp = m_scale * (d_m_unit - m_unit * jnp.mean(d_m_unit * m_unit, axis=-1, keepdims=True))
    d_mlp_all = plane.gather(d_mlp.astype(BF))
    grads_down = [against(inner_low, plane.slot(d_mlp_all, k)).astype(BF) for k in range(rows)]
    d_inner = through(d_mlp_all, w_down)
    d_gate_low = (d_inner * up_pre * (gate_sig * (1.0 + gate_pre * (1.0 - gate_sig)))).astype(BF)
    d_up_low = (d_inner * gate_act).astype(BF)
    grads_gate = [against(plane.slot(hidden_all, k), d_gate_low).astype(BF) for k in range(rows)]
    grads_up = [against(plane.slot(hidden_all, k), d_up_low).astype(BF) for k in range(rows)]
    d_hidden = d_full + plane.scatter(
        (through(d_gate_low, w_gate) + through(d_up_low, w_up)).astype(BF)
    )
    d_a_unit = d_hidden * attn_gain_f
    d_attn = a_scale * (d_a_unit - a_unit * jnp.mean(d_a_unit * a_unit, axis=-1, keepdims=True))
    d_attn_all = plane.gather(d_attn.astype(BF))
    grads_out = against(attn_mix, d_attn_all).astype(BF)
    d_mix = heads_of(through(d_attn_all, w_out).astype(BF))
    d_prob = jnp.einsum("sqhd,skhd->shqk", d_mix, values, preferred_element_type=F32)
    row_delta = jnp.sum(prob * d_prob, axis=-1, keepdims=True)
    d_scores = (prob * (d_prob - row_delta)).astype(BF)
    d_qrot = (
        jnp.einsum("shqk,skhd->sqhd", d_scores, k_rot, preferred_element_type=F32) * score_scale
    )
    d_krot = (
        jnp.einsum("shqk,sqhd->skhd", d_scores, q_rot, preferred_element_type=F32) * score_scale
    )
    d_value = jnp.einsum("shqk,sqhd->skhd", prob_low, d_mix, preferred_element_type=F32)
    d_qn = joined(rotate_pairs(d_qrot, cos_table, -sin_table))
    d_kn = joined(rotate_pairs(d_krot, cos_table, -sin_table))
    d_q_hat = d_qn * q_gain_f
    d_k_hat = d_kn * k_gain_f
    inners = plane.total(
        jnp.stack([jnp.sum(d_q_hat * q_unit, axis=1), jnp.sum(d_k_hat * k_unit, axis=1)])
    )
    d_query = q_scale * (d_q_hat - q_unit * (inners[0] / width)[:, None])
    d_key = k_scale * (d_k_hat - k_unit * (inners[1] / width)[:, None])
    d_query = d_query.astype(BF)
    d_key = d_key.astype(BF)
    d_value = joined(d_value.astype(BF))
    d_qkv = jnp.concatenate([d_query, d_key, d_value], axis=1)
    grads_qkv = [against(plane.slot(inputs_all, k), d_qkv).astype(BF) for k in range(rows)]
    d_inputs = d_hidden + plane.scatter(
        (through(d_query, w_query) + through(d_key, w_key) + through(d_value, w_value)).astype(BF)
    )

    def home(array):
        own = plane.relative((array).astype(BF)).reshape(seq_own, tok_seq, width)
        pieces = [own] + [plane.hop(own, 0, k) for k in range(1, cols)]
        out = jnp.zeros((seq_grp, tok_seq, width), BF)
        for k in range(cols):
            out = lax.dynamic_update_slice_in_dim(out, pieces[k], (col ^ k) * seq_own, axis=0)
        return out

    output = home(result)
    grad_input = home(d_inputs * valid_rows)

    def finish(blocks, axis):
        size = blocks[0].shape[axis]
        shape = list(blocks[0].shape)
        shape[axis] = size * rows
        out = jnp.zeros(shape, F32)
        for k in reversed(range(rows)):
            start = [0, 0]
            start[axis] = (row ^ k) * size
            out = lax.dynamic_update_slice(out, blocks[k].astype(F32), start)
        return out

    order = [k for k in range(2, rows)] + [1, 0]
    chunks = [grads[k] for grads in (grads_down, grads_gate, grads_up) for k in order]
    chunks += [grads_out] + [grads_qkv[k] for k in order]
    summed = group_sums(chunks)

    def arrived_at(blocks):
        placed = [plane.hop(block, k) for k, block in zip(order, blocks, strict=True)]
        return [placed[order.index(k)] for k in range(rows)]

    grad_down = finish(arrived_at(summed[:rows]), 0)
    grad_gate = finish(arrived_at(summed[rows : 2 * rows]), 1)
    grad_up = finish(arrived_at(summed[2 * rows : 3 * rows]), 1)
    grad_out = finish(arrived_at([plane.slot(summed[3 * rows], k) for k in order]), 0)
    qkv_blocks = arrived_at(summed[3 * rows + 1 :])
    grad_query = finish([b[:, :head_part] for b in qkv_blocks], 1)
    grad_key = finish([b[:, head_part : 2 * head_part] for b in qkv_blocks], 1)
    grad_value = finish([b[:, 2 * head_part :] for b in qkv_blocks], 1)

    def sums_of(array):
        return jnp.sum(array.reshape(seq_own, tok_seq * width), axis=1)

    own_sums = jnp.stack(
        [
            sums_of(result * result),
            sums_of(branch_a * branch_a * valid_rows),
            sums_of(branch_m * branch_m * valid_rows),
        ],
        axis=1,
    )
    own_ids = my_group * seq_grp + first_own + jnp.arange(seq_own, dtype=jnp.int32)
    seq_sums = jnp.sum(
        jnp.where(
            own_ids[:, None, None] == jnp.arange(seq_count, dtype=jnp.int32)[None, :, None],
            own_sums[:, None, :],
            0.0,
        ),
        axis=0,
    )
    gain_sums = plane.relative(
        jnp.stack([jnp.sum(d_hidden * a_unit, axis=0), jnp.sum(d_full * m_unit, axis=0)])
    )
    head_sums = jnp.stack([jnp.sum(d_qn * q_unit, axis=0), jnp.sum(d_kn * k_unit, axis=0)])
    mine = (
        (jnp.arange(cols)[:, None] == col) & (jnp.arange(rows)[None, :] == row)
    ).astype(F32)
    head_sums = (head_sums[:, None, None, :] * mine[None, :, :, None]).reshape(2, cols, heads_cols)
    vector = jnp.concatenate([gain_sums.reshape(-1), head_sums.reshape(-1), seq_sums.reshape(-1)])
    vector = jnp.pad(vector, (0, -vector.shape[0] % 1024)).reshape(-1, 1024)
    row_xor = 1
    while row_xor < rows:
        vector = vector + plane.hop(vector, row_xor)
        row_xor *= 2
    col_xor = 1
    while col_xor < cols:
        vector = vector + plane.hop(vector, 0, col_xor)
        col_xor *= 2
    vector = group_total(vector).reshape(-1)
    gain_sums = lax.dynamic_slice_in_dim(
        vector[: 2 * width].reshape(2, width), row * part, part, axis=1
    )
    head_end = 2 * width + 2 * cols * heads_cols
    head_sums = lax.dynamic_slice_in_dim(
        vector[2 * width : head_end].reshape(2, cols, heads_cols), col, 1, axis=1
    )
    seq_sums = vector[head_end : head_end + 3 * seq_count].reshape(seq_count, 3)
    member = (
        (deal_slot // seq_grp)[:, None] == jnp.arange(groups, dtype=jnp.int32)[None, :]
    ).astype(F32)
    counts = jnp.sum(member * lengths.astype(F32)[:, None], axis=0)
    stat_sums = jnp.sum(member[:, :, None] * seq_sums[:, None, :], axis=0)
    rms_stats = jnp.sqrt(stat_sums / (counts[:, None] * width))
    return (
        output,
        grad_input,
        grad_query,
        grad_key,
        grad_value,
        grad_out,
        head_sums[0, 0],
        head_sums[1, 0],
        gain_sums[0],
        grad_gate,
        grad_up,
        grad_down,
        gain_sums[1],
        rms_stats,
    )


def solution(mesh):
    tokens = P("dp", "row", None)
    inward = P("row", "col")
    outward = P("col", "row")
    in_specs = (
        (tokens, tokens, P(), P())
        + (inward, inward, inward, outward)
        + (P("col"), P("col"), P("row"))
        + (inward, inward, outward, P("row"))
    )
    out_specs = (
        (tokens, tokens)
        + (inward, inward, inward, outward)
        + (P("col"), P("col"), P("row"))
        + (inward, inward, outward, P("row"))
        + (P(),)
    )
    return jax.shard_map(shards, mesh=mesh, in_specs=in_specs, out_specs=out_specs, check_vma=False)
```

time: 2250 us -> 1070 us (0.48)
  waiting for transfers between devices: 1650 us -> 404 us
  starting transfers between devices: 23.6 us -> 289 us
  local copies, waits for them, and re-layouts: 288 us -> 113 us
  other arithmetic: 37 us -> 116 us
  matrix products: 188 us -> 128 us
    psum x5 -> x0, waiting for transfers between devices: 646 us -> none  [the longest x1 476 us: shards(): lax.psum(lax.psum_scatter(grad_term(jnp.int32(0), per_rows * lax.axis_siz...]
    unnamed x19 -> x3, waiting for transfers between devices: 451 us -> 0.05 us
    ppermute x0 -> x141, waiting for transfers between devices: none -> 374 us  [the longest x74 120 us: hop(): lax.ppermute(array, 'row', [(a, a ^ row_xor) for a in range(self.rows)])]
    all_gather x9 -> x3, waiting for transfers between devices: 390 us -> 30.2 us  [shared(): lax.all_gather(jnp.concatenate(parts, axis=1), 'dp', axis=0, tiled=True)]
    ppermute x0 -> x141, starting transfers between devices: none -> 289 us  [the longest x7 104 us: group_sums(): arrived[step] = lax.ppermute(sent, 'dp', ENDS)]
    all_to_all x4 -> x0, waiting for transfers between devices: 169 us -> none  [the longest x1 93.7 us: shards(): lax.all_to_all(jnp.einsum('jp,jtd->ptd', take_pick, grad_in_low, preferre...]
    concatenate x3 -> x7, local copies, waits for them, and re-layouts: 156 us -> 4.75 us  [the longest x4 3.21 us: over_cores(): jnp.concatenate([blocks[b, a] for b in range(self.cols) for a in range(se...]
    dot_general x21 -> x12, matrix products: 93.5 us -> 41.5 us  [the longest x7 32.2 us: dot(): return jnp.dot(left_side, right_side, preferred_element_type=F32)]
  transfers between devices with their start and end apart: 21 -> 144, of which waited for: 17 -> 56; matrix products, arithmetic and copies ran while one was open for 9% -> 25% of each run, Pallas kernels for 0% -> 0%
where the time goes in v1:
time: 1070 us
  waiting for transfers between devices  404 us (38%)
  starting transfers between devices  289 us (27%)
  matrix products  128 us (12%)
  other arithmetic  116 us (11%)
  local copies, waits for them, and re-layouts  113 us (11%)
  between operations  18.4 us (2%)
    ppermute x74, waiting for transfers between devices, hop(): lax.ppermute(array, 'row', [(a, a ^ row_xor) for a in range(self.rows)])  120 us
    ppermute x10, waiting for transfers between devices, group_sums(): again = lax.ppermute(full[back], 'dp', [(1, 0), (2, 3)])  105 us
    ppermute x7, starting transfers between devices, group_sums(): arrived[step] = lax.ppermute(sent, 'dp', ENDS)  104 us
    ppermute x10, starting transfers between devices, group_sums(): arrived[step] = lax.ppermute(array, 'dp', [(0, 1), (3, 2)])  71.7 us
    ppermute x10, waiting for transfers between devices, group_sums(): arrived[step] = lax.ppermute(array, 'dp', [(0, 1), (3, 2)])  70.2 us
    ppermute x74, starting transfers between devices, hop(): lax.ppermute(array, 'row', [(a, a ^ row_xor) for a in range(self.rows)])  52 us
    unnamed x339, local copies, waits for them, and re-layouts  46.5 us
    dot_general x17, matrix products, against(): lax.dot_general(left_side, right_side, (((0,), (0,)), ((), ())), preferre...  43.7 us
  transfers between devices with their start and end apart: 144, of which 56 were waited for; matrix products, arithmetic and copies ran while one was open for 25% of the time, Pallas kernels for 0%

profile of v1, /device:TPU:0, one launch (start us, length us, event | category | flops | bytes accessed | tf_op | source)
XLA Modules:
  0.0 1068.2 jit_solution(13619734738345499054)
XLA Ops:
  33.3 11.6 %collective-permute-done.8 = bf16[3,512,256]{2,1,0:T(8,128)(2,1)} collective-permute-done((bf16[3,512,256]{2,1,0:T(8,128)(2,1)}, bf16[3,512,256]{2,1,0:T(8,128)(2,1)}, u32[]{:S(2)}, u32[]{:S(2)}) %collective-permute-start.8) | collective-permute-done | bytes 786464 | tf_op jit(solution)/shard_map/ppermute | solution.py:64
  47.7 14.5 %collective-permute-done.7 = bf16[3,512,256]{2,1,0:T(8,128)(2,1)} collective-permute-done((bf16[3,512,256]{2,1,0:T(8,128)(2,1)}, bf16[3,512,256]{2,1,0:T(8,128)(2,1)}, u32[]{:S(2)}, u32[]{:S(2)}) %collective-permute-start.7) | collective-permute-done | bytes 786464 | tf_op jit(solution)/shard_map/ppermute | solution.py:64
  67.3 10.7 %collective-permute-done.4 = bf16[128,2048]{1,0:T(8,128)(2,1)S(1)} collective-permute-done((bf16[128,2048]{1,0:T(8,128)(2,1)S(1)}, bf16[128,2048]{1,0:T(8,128)(2,1)S(1)}, u32[]{:S(2)}, u32[]{:S(2)}) %collective-permute-start.4) | collective-permute-done | bytes 524320 | tf_op jit(solution)/shard_map/ppermute | solution.py:66
  108.7 3.1 subtract_convert_fusion.1
  111.8 6.3 fusion.207
  131.1 6.1 collective-permute-done.33
  137.2 6.0 collective-permute-done.32
  146.1 3.0 constant_dynamic-slice_fusion.26
  152.6 3.3 constant_dynamic-slice_fusion.24
  158.8 3.8 convert_add_fusion.6
  167.2 4.7 collective-permute-done.35
  173.8 9.3 collective-permute-done.16
  188.0 4.2 collective-permute-done.17
  202.9 8.0 collective-permute-done.24
  228.5 3.0 fusion.161
  231.5 5.7 all-gather.6.cloned.1.call-done
  241.4 7.1 fusion.66
  248.6 11.0 %multiply_convert_fusion.3 = (bf16[1024,1024]{1,0:T(8,128)(2,1)}, f32[1024,1024]{1,0:T(8,128)}) fusion(f32[1024,1024]{1,0:T(8,128)S(1)} %fusion.66, bf16[1024,2048]{1,0:T(8,128)(2,1)} %constant_dynamic-update-slice_fusion.10, bf16[512,1024]{1,0:T(8,128)(2,1)S(1)} %get-tuple-element.131, bf16[512,1024]{1,0:T(8,128)(2,1)S(1)} %get-tuple-element.130, ...), kind=kOutput, calls=%fused_computation.19 | convolution fusion | flops 4318035968 | bytes 18874368 | tf_op jit(solution)/shard_map/dot_general | solution.py:32
  259.5 24.5 %all-gather.8.cloned.1.call-done = bf16[1024,1024]{1,0:T(8,128)(2,1)} async-done(((bf16[256,1024]{1,0:T(8,128)(2,1)}), bf16[1024,1024]{1,0:T(8,128)(2,1)}) %all-gather.8.cloned.1.call-update) | async-done | bytes 2097168 | tf_op jit(solution)/shard_map/all_gather | solution.py:290
  284.0 7.0 convolution_convert_fusion.1
  292.7 3.1 collective-permute-done.40
  307.0 6.8 collective-permute-done.41
  334.1 9.3 collective-permute-done.47
  351.7 3.5 collective-permute-done.52
  362.7 10.5 multiply_convert_fusion.2
  375.9 3.6 convolution_convert_fusion.13
  381.8 3.5 convolution_convert_fusion.11
  390.1 3.6 convolution_convert_fusion.7
  393.7 9.2 fusion.64
  403.0 9.1 add_convert_fusion.1
  417.1 3.5 convolution_convert_fusion.6
  421.9 3.5 convolution_convert_fusion.3
  426.7 12.3 %collective-permute-done.76 = bf16[1024,512]{1,0:T(8,128)(2,1)S(1)} collective-permute-done((bf16[1024,512]{1,0:T(8,128)(2,1)S(1)}, bf16[1024,512]{1,0:T(8,128)(2,1)S(1)}, u32[]{:S(2)}, u32[]{:S(2)}) %collective-permute-start.76) | collective-permute-done | bytes 1048608 | tf_op jit(solution)/shard_map/ppermute | solution.py:201
  440.1 3.5 convolution_convert_fusion.10
  445.0 16.6 %collective-permute-done.88 = bf16[1024,512]{1,0:T(8,128)(2,1)S(1)} collective-permute-done((bf16[1024,512]{1,0:T(8,128)(2,1)S(1)}, bf16[1024,512]{1,0:T(8,128)(2,1)S(1)}, u32[]{:S(2)}, u32[]{:S(2)}) %collective-permute-start.88) | collective-permute-done | bytes 1048608 | tf_op jit(solution)/shard_map/ppermute | solution.py:201
  462.6 21.2 %collective-permute-done.100 = bf16[1024,512]{1,0:T(8,128)(2,1)S(1)} collective-permute-done((bf16[1024,512]{1,0:T(8,128)(2,1)S(1)}, bf16[1024,512]{1,0:T(8,128)(2,1)S(1)}, u32[]{:S(2)}, u32[]{:S(2)}) %collective-permute-start.100) | collective-permute-done | bytes 1048608 | tf_op jit(solution)/shard_map/ppermute | solution.py:201
  486.1 8.2 collective-permute-start.78
  501.5 6.7 collective-permute-done.55
  527.9 32.6 %collective-permute-done.102 = bf16[1024,512]{1,0:T(8,128)(2,1)} collective-permute-done((bf16[1024,512]{1,0:T(8,128)(2,1)}, bf16[1024,512]{1,0:T(8,128)(2,1)}, u32[]{:S(2)}, u32[]{:S(2)}) %collective-permute-start.102) | collective-permute-done | bytes 1048608 | tf_op jit(solution)/shard_map/ppermute | solution.py:195
  572.1 10.4 collective-permute-done.138
  590.1 5.8 collective-permute-done.64
  601.7 44.4 %collective-permute-start.80 = (bf16[512,1024]{1,0:T(8,128)(2,1)}, bf16[512,1024]{1,0:T(8,128)(2,1)}, u32[]{:S(2)}, u32[]{:S(2)}) collective-permute-start(bf16[512,1024]{1,0:T(8,128)(2,1)} %fusion.27), channel_id=1, source_target_pairs={{0,8},{8,0},{16,24},{24,16},{1,9},{9,1},{17,25},{25,17},{2,10},{10... | collective-permute-start | bytes 3145736 | tf_op jit(solution)/shard_map/ppermute | solution.py:195
  647.8 4.5 broadcast_in_dim.65
  653.9 4.9 collective-permute-start.104
  669.3 3.0 multiply_reduce_fusion
  696.1 3.3 collective-permute-done.68
  724.7 5.5 collective-permute-start.123
  738.7 5.7 collective-permute-done.125
  757.0 2.9 convert_dynamic-update-slice_fusion
  762.7 35.9 %collective-permute-start.82 = (bf16[512,1024]{1,0:T(8,128)(2,1)S(1)}, bf16[512,1024]{1,0:T(8,128)(2,1)S(1)}, u32[]{:S(2)}, u32[]{:S(2)}) collective-permute-start(bf16[512,1024]{1,0:T(8,128)(2,1)S(1)} %fusion.28), channel_id=1, source_target_pairs={{0,8},{8,0},{16,24},{24,16},{1,9},{9,1},{17,25},{25,17},{2,10},{10... | collective-permute-start | bytes 3145736 | tf_op jit(solution)/shard_map/ppermute | solution.py:195
  799.3 21.4 %collective-permute-start.106 = (bf16[512,1024]{1,0:T(8,128)(2,1)S(1)}, bf16[512,1024]{1,0:T(8,128)(2,1)S(1)}, u32[]{:S(2)}, u32[]{:S(2)}) collective-permute-start(bf16[512,1024]{1,0:T(8,128)(2,1)S(1)} %fusion.32), channel_id=1, source_target_pairs={{0,8},{8,0},{16,24},{24,16},{1,9},{9,1},{17,25},{25,17},{2,10},{10... | collective-permute-start | bytes 3145736 | tf_op jit(solution)/shard_map/ppermute | solution.py:195
  828.7 10.8 %collective-permute-done.71 = bf16[2,64,2048]{2,1,0:T(8,128)(2,1)S(1)} collective-permute-done((bf16[2,64,2048]{2,1,0:T(8,128)(2,1)S(1)}, bf16[2,64,2048]{2,1,0:T(8,128)(2,1)S(1)}, u32[]{:S(2)}, u32[]{:S(2)}) %collective-permute-start.71) | collective-permute-done | bytes 524320 | tf_op jit(solution)/shard_map/ppermute | solution.py:64
  852.2 24.5 %collective-permute-start.84 = (bf16[512,768]{1,0:T(8,128)(2,1)S(1)}, bf16[512,768]{1,0:T(8,128)(2,1)S(1)}, u32[]{:S(2)}, u32[]{:S(2)}) collective-permute-start(bf16[512,768]{1,0:T(8,128)(2,1)S(1)} %copy-done.97), channel_id=1, source_target_pairs={{0,8},{24,16},{1,9},{25,17},{2,10},{26,18},{3,11},{27,19},{4,12},{... | collective-permute-start | bytes 2359304 | tf_op jit(solution)/shard_map/ppermute | solution.py:201
  879.8 17.3 %collective-permute-start.108 = (bf16[256,2048]{1,0:T(8,128)(2,1)S(1)}, bf16[256,2048]{1,0:T(8,128)(2,1)S(1)}, u32[]{:S(2)}, u32[]{:S(2)}) collective-permute-start(bf16[256,2048]{1,0:T(8,128)(2,1)S(1)} %copy-done.65), channel_id=1, source_target_pairs={{0,8},{24,16},{1,9},{25,17},{2,10},{26,18},{3,11},{27,19},{4,12},{... | collective-permute-start | bytes 3145736 | tf_op jit(solution)/shard_map/ppermute | solution.py:201
  902.1 11.0 %collective-permute-done.108 = bf16[256,2048]{1,0:T(8,128)(2,1)S(1)} collective-permute-done((bf16[256,2048]{1,0:T(8,128)(2,1)S(1)}, bf16[256,2048]{1,0:T(8,128)(2,1)S(1)}, u32[]{:S(2)}, u32[]{:S(2)}) %collective-permute-start.108) | collective-permute-done | bytes 1048608 | tf_op jit(solution)/shard_map/ppermute | solution.py:201
  913.1 5.6 collective-permute-start.96
  923.0 9.1 collective-permute-done.96
  934.1 36.4 %collective-permute-done.132 = bf16[512,1024]{1,0:T(8,128)(2,1)S(1)} collective-permute-done((bf16[512,1024]{1,0:T(8,128)(2,1)S(1)}, bf16[512,1024]{1,0:T(8,128)(2,1)S(1)}, u32[]{:S(2)}, u32[]{:S(2)}) %collective-permute-start.132) | collective-permute-done | bytes 1048608 | tf_op jit(solution)/shard_map/ppermute | solution.py:203
  971.3 4.2 collective-permute-start.110
  978.5 8.9 collective-permute-done.86
  989.8 20.0 %collective-permute-done.116 = bf16[256,2048]{1,0:T(8,128)(2,1)S(1)} collective-permute-done((bf16[256,2048]{1,0:T(8,128)(2,1)S(1)}, bf16[256,2048]{1,0:T(8,128)(2,1)S(1)}, u32[]{:S(2)}, u32[]{:S(2)}) %collective-permute-start.116) | collective-permute-done | bytes 1048608 | tf_op jit(solution)/shard_map/ppermute | solution.py:203
  1014.4 7.4 collective-permute-done.98
  1028.1 17.3 %collective-permute-done.112 = bf16[512,768]{1,0:T(8,128)(2,1)S(1)} collective-permute-done((bf16[512,768]{1,0:T(8,128)(2,1)S(1)}, bf16[512,768]{1,0:T(8,128)(2,1)S(1)}, u32[]{:S(2)}, u32[]{:S(2)}) %collective-permute-start.112) | collective-permute-done | bytes 786464 | tf_op jit(solution)/shard_map/ppermute | solution.py:203
  1045.8 12.1 %collective-permute-done.115 = bf16[512,768]{1,0:T(8,128)(2,1)S(1)} collective-permute-done((bf16[512,768]{1,0:T(8,128)(2,1)S(1)}, bf16[512,768]{1,0:T(8,128)(2,1)S(1)}, u32[]{:S(2)}, u32[]{:S(2)}) %collective-permute-start.115) | collective-permute-done | bytes 786464 | tf_op jit(solution)/shard_map/ppermute | solution.py:203
  (947 shorter events, 394.4 us)
Async XLA Ops:
  7.2 221.3 %all-gather.4.cloned.1.call-start = ((), (), s32[]{:S(2)}) async-start(), calls=%async_computation | async-start | bytes 2621440 | tf_op jit(solution)/shard_map/all_gather | solution.py:290
  20.0 25.0 %collective-permute-start.8 = (bf16[3,512,256]{2,1,0:T(8,128)(2,1)}, bf16[3,512,256]{2,1,0:T(8,128)(2,1)}, u32[]{:S(2)}, u32[]{:S(2)}) collective-permute-start(bf16[3,512,256]{2,1,0:T(8,128)(2,1)} %pad_maximum_fusion.16), channel_id=1, source_target_pairs={{0,6},{2,4},{4,2},{6,0},{1,7},{3,5},{5,3},{7,1},{8,14},{10,12},{12... | collective-permute-start | bytes 2359304 | tf_op jit(solution)/shard_map/ppermute | solution.py:64
  21.0 41.1 %collective-permute-start.7 = (bf16[3,512,256]{2,1,0:T(8,128)(2,1)}, bf16[3,512,256]{2,1,0:T(8,128)(2,1)}, u32[]{:S(2)}, u32[]{:S(2)}) collective-permute-start(bf16[3,512,256]{2,1,0:T(8,128)(2,1)} %pad_maximum_fusion.15), channel_id=1, source_target_pairs={{0,4},{2,6},{4,0},{6,2},{1,5},{3,7},{5,1},{7,3},{8,12},{10,14},{12... | collective-permute-start | bytes 2359304 | tf_op jit(solution)/shard_map/ppermute | solution.py:64
  23.8 54.4 %collective-permute-start.6 = (bf16[3,512,256]{2,1,0:T(8,128)(2,1)}, bf16[3,512,256]{2,1,0:T(8,128)(2,1)}, u32[]{:S(2)}, u32[]{:S(2)}) collective-permute-start(bf16[3,512,256]{2,1,0:T(8,128)(2,1)} %pad_maximum_fusion.14), channel_id=1, source_target_pairs={{0,2},{2,0},{4,6},{6,4},{1,3},{3,1},{5,7},{7,5},{8,10},{10,8},{12,... | collective-permute-start | bytes 2359304 | tf_op jit(solution)/shard_map/ppermute | solution.py:64
  28.5 92.8 %collective-permute-start.14 = (bf16[256,512]{1,0:T(8,128)(2,1)}, bf16[256,512]{1,0:T(8,128)(2,1)}, u32[]{:S(2)}, u32[]{:S(2)}) collective-permute-start(bf16[256,512]{1,0:T(8,128)(2,1)} %get-tuple-element.162), channel_id=1, source_target_pairs={{0,6},{2,4},{4,2},{6,0},{1,7},{3,5},{5,3},{7,1},{8,14},{10,12},{12... | collective-permute-start | bytes 786440 | tf_op jit(solution)/shard_map/ppermute | solution.py:64
  29.4 34.0 %collective-permute-start.2 = (bf16[128,2048]{1,0:T(8,128)(2,1)S(1)}, bf16[128,2048]{1,0:T(8,128)(2,1)S(1)}, u32[]{:S(2)}, u32[]{:S(2)}) collective-permute-start(bf16[128,2048]{1,0:T(8,128)(2,1)S(1)} %pad_maximum_fusion.23), channel_id=1, source_target_pairs={{0,2},{2,0},{4,6},{6,4},{1,3},{3,1},{5,7},{7,5},{8,10},{10,8},{12,... | collective-permute-start | bytes 1572872 | tf_op jit(solution)/shard_map/ppermute | solution.py:64
  45.0 76.4 %collective-permute-start.13 = (bf16[256,512]{1,0:T(8,128)(2,1)}, bf16[256,512]{1,0:T(8,128)(2,1)}, u32[]{:S(2)}, u32[]{:S(2)}) collective-permute-start(bf16[256,512]{1,0:T(8,128)(2,1)} %get-tuple-element.163), channel_id=1, source_target_pairs={{0,4},{2,6},{4,0},{6,2},{1,5},{3,7},{5,1},{7,3},{8,12},{10,14},{12... | collective-permute-start | bytes 786440 | tf_op jit(solution)/shard_map/ppermute | solution.py:64
  62.2 59.2 %collective-permute-start.12 = (bf16[256,512]{1,0:T(8,128)(2,1)}, bf16[256,512]{1,0:T(8,128)(2,1)}, u32[]{:S(2)}, u32[]{:S(2)}) collective-permute-start(bf16[256,512]{1,0:T(8,128)(2,1)} %get-tuple-element.161), channel_id=1, source_target_pairs={{0,2},{2,0},{4,6},{6,4},{1,3},{3,1},{5,7},{7,5},{8,10},{10,8},{12,... | collective-permute-start | bytes 786440 | tf_op jit(solution)/shard_map/ppermute | solution.py:64
  127.5 29.8 %collective-permute-start.15 = (bf16[2,2,128,2048]{3,2,1,0:T(8,128)(2,1)}, bf16[2,2,128,2048]{3,2,1,0:T(8,128)(2,1)}, u32[]{:S(2)}, u32[]{:S(2)}) collective-permute-start(bf16[2,2,128,2048]{3,2,1,0:T(8,128)(2,1)} %fusion.12), channel_id=1, source_target_pairs={{0,2},{2,0},{4,6},{6,4},{1,3},{3,1},{5,7},{7,5},{8,10},{10,8},{12,... | collective-permute-start | bytes 6291464 | tf_op jit(solution)/shard_map/ppermute | solution.py:64
  144.0 93.2 %all-gather.6.cloned.1.call-start = ((), (), s32[]{:S(2)}) async-start(), calls=%async_computation.1 | async-start | bytes 2621440 | tf_op jit(solution)/shard_map/all_gather | solution.py:290
  149.1 92.3 %collective-permute-start.31 = (bf16[512,1024]{1,0:T(8,128)(2,1)}, bf16[512,1024]{1,0:T(8,128)(2,1)}, u32[]{:S(2)}, u32[]{:S(2)}) collective-permute-start(bf16[512,1024]{1,0:T(8,128)(2,1)} %get-tuple-element.100), channel_id=1, source_target_pairs={{0,2},{2,0},{4,6},{6,4},{1,3},{3,1},{5,7},{7,5},{8,10},{10,8},{12,... | collective-permute-start | bytes 3145736 | tf_op jit(solution)/shard_map/ppermute | solution.py:64
  164.1 84.4 %collective-permute-start.34 = (bf16[512,1024]{1,0:T(8,128)(2,1)}, bf16[512,1024]{1,0:T(8,128)(2,1)}, u32[]{:S(2)}, u32[]{:S(2)}) collective-permute-start(bf16[512,1024]{1,0:T(8,128)(2,1)} %get-tuple-element.104), channel_id=1, source_target_pairs={{0,2},{2,0},{4,6},{6,4},{1,3},{3,1},{5,7},{7,5},{8,10},{10,8},{12,... | collective-permute-start | bytes 3145736 | tf_op jit(solution)/shard_map/ppermute | solution.py:64
  165.5 30.5 %collective-permute-start.39 = (bf16[256,512]{1,0:T(8,128)(2,1)}, bf16[256,512]{1,0:T(8,128)(2,1)}, u32[]{:S(2)}, u32[]{:S(2)}) collective-permute-start(bf16[256,512]{1,0:T(8,128)(2,1)} %get-tuple-element.98), channel_id=1, source_target_pairs={{0,6},{2,4},{4,2},{6,0},{1,7},{3,5},{5,3},{7,1},{8,14},{10,12},{12... | collective-permute-start | bytes 786440 | tf_op jit(solution)/shard_map/ppermute | solution.py:64
  173.7 110.3 %all-gather.8.cloned.1.call-start = ((), (), s32[]{:S(2)}) async-start(), calls=%async_computation.2 | async-start | bytes 2621440 | tf_op jit(solution)/shard_map/all_gather | solution.py:290
  194.5 65.0 %collective-permute-start.37 = (bf16[1024,512]{1,0:T(8,128)(2,1)}, bf16[1024,512]{1,0:T(8,128)(2,1)}, u32[]{:S(2)}, u32[]{:S(2)}) collective-permute-start(bf16[1024,512]{1,0:T(8,128)(2,1)} %get-tuple-element.96), channel_id=1, source_target_pairs={{0,2},{2,0},{4,6},{6,4},{1,3},{3,1},{5,7},{7,5},{8,10},{10,8},{12,... | collective-permute-start | bytes 3145736 | tf_op jit(solution)/shard_map/ppermute | solution.py:64
  412.8 81.5 %collective-permute-start.54 = (bf16[2,2,128,2048]{3,2,1,0:T(8,128)(2,1)S(1)}, bf16[2,2,128,2048]{3,2,1,0:T(8,128)(2,1)S(1)}, u32[]{:S(2)}, u32[]{:S(2)}) collective-permute-start(bf16[2,2,128,2048]{3,2,1,0:T(8,128)(2,1)S(1)} %fusion.16), channel_id=1, source_target_pairs={{0,2},{2,0},{4,6},{6,4},{1,3},{3,1},{5,7},{7,5},{8,10},{10,8},{12,... | collective-permute-start | bytes 6291464 | tf_op jit(solution)/shard_map/ppermute | solution.py:64
  413.7 25.4 %collective-permute-start.76 = (bf16[1024,512]{1,0:T(8,128)(2,1)S(1)}, bf16[1024,512]{1,0:T(8,128)(2,1)S(1)}, u32[]{:S(2)}, u32[]{:S(2)}) collective-permute-start(bf16[1024,512]{1,0:T(8,128)(2,1)S(1)} %copy-done.67), channel_id=1, source_target_pairs={{0,8},{24,16},{1,9},{25,17},{2,10},{26,18},{3,11},{27,19},{4,12},{... | collective-permute-start | bytes 3145736 | tf_op jit(solution)/shard_map/ppermute | solution.py:201
  415.7 45.8 %collective-permute-start.88 = (bf16[1024,512]{1,0:T(8,128)(2,1)S(1)}, bf16[1024,512]{1,0:T(8,128)(2,1)S(1)}, u32[]{:S(2)}, u32[]{:S(2)}) collective-permute-start(bf16[1024,512]{1,0:T(8,128)(2,1)S(1)} %copy-done.66), channel_id=1, source_target_pairs={{0,8},{24,16},{1,9},{25,17},{2,10},{26,18},{3,11},{27,19},{4,12},{... | collective-permute-start | bytes 3145736 | tf_op jit(solution)/shard_map/ppermute | solution.py:201
  425.4 58.4 %collective-permute-start.100 = (bf16[1024,512]{1,0:T(8,128)(2,1)S(1)}, bf16[1024,512]{1,0:T(8,128)(2,1)S(1)}, u32[]{:S(2)}, u32[]{:S(2)}) collective-permute-start(bf16[1024,512]{1,0:T(8,128)(2,1)S(1)} %convolution_convert_fusion.4), channel_id=1, source_target_pairs={{0,8},{24,16},{1,9},{25,17},{2,10},{26,18},{3,11},{27,19},{4,12},{... | collective-permute-start | bytes 3145736 | tf_op jit(solution)/shard_map/ppermute | solution.py:201
  439.4 45.4 %collective-permute-start.77 = (bf16[1024,512]{1,0:T(8,128)(2,1)S(1)}, bf16[1024,512]{1,0:T(8,128)(2,1)S(1)}, u32[]{:S(2)}, u32[]{:S(2)}) collective-permute-start(bf16[1024,512]{1,0:T(8,128)(2,1)S(1)} %add_convert_fusion.27), channel_id=1, source_target_pairs={{8,16},{16,8},{9,17},{17,9},{10,18},{18,10},{11,19},{19,11},{12,20... | collective-permute-start | bytes 3145736 | tf_op jit(solution)/shard_map/ppermute | solution.py:207
  461.9 36.1 %collective-permute-start.89 = (bf16[1024,512]{1,0:T(8,128)(2,1)S(1)}, bf16[1024,512]{1,0:T(8,128)(2,1)S(1)}, u32[]{:S(2)}, u32[]{:S(2)}) collective-permute-start(bf16[1024,512]{1,0:T(8,128)(2,1)S(1)} %add_convert_fusion.19), channel_id=1, source_target_pairs={{8,16},{16,8},{9,17},{17,9},{10,18},{18,10},{11,19},{19,11},{12,20... | collective-permute-start | bytes 3145736 | tf_op jit(solution)/shard_map/ppermute | solution.py:207
  484.1 27.3 %collective-permute-start.101 = (bf16[1024,512]{1,0:T(8,128)(2,1)S(1)}, bf16[1024,512]{1,0:T(8,128)(2,1)S(1)}, u32[]{:S(2)}, u32[]{:S(2)}) collective-permute-start(bf16[1024,512]{1,0:T(8,128)(2,1)S(1)} %add_convert_fusion.11), channel_id=1, source_target_pairs={{8,16},{16,8},{9,17},{17,9},{10,18},{18,10},{11,19},{19,11},{12,20... | collective-permute-start | bytes 3145736 | tf_op jit(solution)/shard_map/ppermute | solution.py:207
  486.1 78.1 %collective-permute-start.78 = (bf16[512,1024]{1,0:T(8,128)(2,1)}, bf16[512,1024]{1,0:T(8,128)(2,1)}, u32[]{:S(2)}, u32[]{:S(2)}) collective-permute-start(bf16[512,1024]{1,0:T(8,128)(2,1)} %convolution_convert_fusion.11), channel_id=1, source_target_pairs={{0,8},{24,16},{1,9},{25,17},{2,10},{26,18},{3,11},{27,19},{4,12},{... | collective-permute-start | bytes 3145736 | tf_op jit(solution)/shard_map/ppermute | solution.py:201
  499.2 68.7 %collective-permute-start.90 = (bf16[512,1024]{1,0:T(8,128)(2,1)}, bf16[512,1024]{1,0:T(8,128)(2,1)}, u32[]{:S(2)}, u32[]{:S(2)}) collective-permute-start(bf16[512,1024]{1,0:T(8,128)(2,1)} %convolution_convert_fusion.7), channel_id=1, source_target_pairs={{0,8},{24,16},{1,9},{25,17},{2,10},{26,18},{3,11},{27,19},{4,12},{... | collective-permute-start | bytes 3145736 | tf_op jit(solution)/shard_map/ppermute | solution.py:201
  512.8 47.7 %collective-permute-start.102 = (bf16[1024,512]{1,0:T(8,128)(2,1)}, bf16[1024,512]{1,0:T(8,128)(2,1)}, u32[]{:S(2)}, u32[]{:S(2)}) collective-permute-start(bf16[1024,512]{1,0:T(8,128)(2,1)} %fusion.31), channel_id=1, source_target_pairs={{0,8},{8,0},{16,24},{24,16},{1,9},{9,1},{17,25},{25,17},{2,10},{10... | collective-permute-start | bytes 3145736 | tf_op jit(solution)/shard_map/ppermute | solution.py:195
  514.9 55.0 %collective-permute-start.135 = (bf16[1024,512]{1,0:T(8,128)(2,1)}, bf16[1024,512]{1,0:T(8,128)(2,1)}, u32[]{:S(2)}, u32[]{:S(2)}) collective-permute-start(bf16[1024,512]{1,0:T(8,128)(2,1)} %add_convert_fusion.18), channel_id=1, source_target_pairs={{8,0},{16,24},{9,1},{17,25},{10,2},{18,26},{11,3},{19,27},{12,4},{... | collective-permute-start | bytes 3145736 | tf_op jit(solution)/shard_map/ppermute | solution.py:203
  516.2 66.2 %collective-permute-start.138 = (bf16[1024,512]{1,0:T(8,128)(2,1)}, bf16[1024,512]{1,0:T(8,128)(2,1)}, u32[]{:S(2)}, u32[]{:S(2)}) collective-permute-start(bf16[1024,512]{1,0:T(8,128)(2,1)} %add_convert_fusion.26), channel_id=1, source_target_pairs={{8,0},{16,24},{9,1},{17,25},{10,2},{18,26},{11,3},{19,27},{12,4},{... | collective-permute-start | bytes 3145736 | tf_op jit(solution)/shard_map/ppermute | solution.py:203
  560.5 25.1 %collective-permute-start.62 = (bf16[128,2048]{1,0:T(8,128)(2,1)S(1)}, bf16[128,2048]{1,0:T(8,128)(2,1)S(1)}, u32[]{:S(2)}, u32[]{:S(2)}) collective-permute-start(bf16[128,2048]{1,0:T(8,128)(2,1)S(1)} %copy-done.26), channel_id=1, source_target_pairs={{0,1},{1,0},{2,3},{3,2},{4,5},{5,4},{6,7},{7,6},{8,9},{9,8},{10,11... | collective-permute-start | bytes 1572872 | tf_op jit(solution)/shard_map/ppermute | solution.py:66
  570.0 28.3 %collective-permute-start.79 = (bf16[512,1024]{1,0:T(8,128)(2,1)S(1)}, bf16[512,1024]{1,0:T(8,128)(2,1)S(1)}, u32[]{:S(2)}, u32[]{:S(2)}) collective-permute-start(bf16[512,1024]{1,0:T(8,128)(2,1)S(1)} %add_convert_fusion.25), channel_id=1, source_target_pairs={{8,16},{16,8},{9,17},{17,9},{10,18},{18,10},{11,19},{19,11},{12,20... | collective-permute-start | bytes 3145736 | tf_op jit(solution)/shard_map/ppermute | solution.py:207
  595.9 51.9 %collective-permute-start.136 = (bf16[1024,512]{1,0:T(8,128)(2,1)S(1)}, bf16[1024,512]{1,0:T(8,128)(2,1)S(1)}, u32[]{:S(2)}, u32[]{:S(2)}) collective-permute-start(bf16[1024,512]{1,0:T(8,128)(2,1)S(1)} %broadcast_select_fusion.3), channel_id=1, source_target_pairs={{0,6},{2,4},{4,2},{6,0},{1,7},{3,5},{5,3},{7,1},{8,14},{10,12},{12... | collective-permute-start | bytes 3145736 | tf_op jit(solution)/shard_map/ppermute | solution.py:64
  596.6 57.2 %collective-permute-start.137 = (bf16[1024,512]{1,0:T(8,128)(2,1)S(1)}, bf16[1024,512]{1,0:T(8,128)(2,1)S(1)}, u32[]{:S(2)}, u32[]{:S(2)}) collective-permute-start(bf16[1024,512]{1,0:T(8,128)(2,1)S(1)} %broadcast_select_fusion.2), channel_id=1, source_target_pairs={{0,4},{2,6},{4,0},{6,2},{1,5},{3,7},{5,1},{7,3},{8,12},{10,14},{12... | collective-permute-start | bytes 3145736 | tf_op jit(solution)/shard_map/ppermute | solution.py:64
  598.3 62.1 %collective-permute-start.139 = (bf16[1024,512]{1,0:T(8,128)(2,1)S(1)}, bf16[1024,512]{1,0:T(8,128)(2,1)S(1)}, u32[]{:S(2)}, u32[]{:S(2)}) collective-permute-start(bf16[1024,512]{1,0:T(8,128)(2,1)S(1)} %broadcast_select_fusion.1), channel_id=1, source_target_pairs={{0,2},{2,0},{4,6},{6,4},{1,3},{3,1},{5,7},{7,5},{8,10},{10,8},{12,... | collective-permute-start | bytes 3145736 | tf_op jit(solution)/shard_map/ppermute | solution.py:64
  600.0 63.8 %collective-permute-start.66 = (bf16[128,2048]{1,0:T(8,128)(2,1)S(1)}, bf16[128,2048]{1,0:T(8,128)(2,1)S(1)}, u32[]{:S(2)}, u32[]{:S(2)}) collective-permute-start(bf16[128,2048]{1,0:T(8,128)(2,1)S(1)} %pad_maximum_fusion.52), channel_id=1, source_target_pairs={{0,2},{2,0},{4,6},{6,4},{1,3},{3,1},{5,7},{7,5},{8,10},{10,8},{12,... | collective-permute-start | bytes 1572872 | tf_op jit(solution)/shard_map/ppermute | solution.py:64
  601.7 145.0 %collective-permute-start.80 = (bf16[512,1024]{1,0:T(8,128)(2,1)}, bf16[512,1024]{1,0:T(8,128)(2,1)}, u32[]{:S(2)}, u32[]{:S(2)}) collective-permute-start(bf16[512,1024]{1,0:T(8,128)(2,1)} %fusion.27), channel_id=1, source_target_pairs={{0,8},{8,0},{16,24},{24,16},{1,9},{9,1},{17,25},{25,17},{2,10},{10... | collective-permute-start | bytes 3145736 | tf_op jit(solution)/shard_map/ppermute | solution.py:195
  647.8 106.1 %collective-permute-start.92 = (bf16[512,1024]{1,0:T(8,128)(2,1)}, bf16[512,1024]{1,0:T(8,128)(2,1)}, u32[]{:S(2)}, u32[]{:S(2)}) collective-permute-start(bf16[512,1024]{1,0:T(8,128)(2,1)} %fusion.29), channel_id=1, source_target_pairs={{0,8},{8,0},{16,24},{24,16},{1,9},{9,1},{17,25},{25,17},{2,10},{10... | collective-permute-start | bytes 3145736 | tf_op jit(solution)/shard_map/ppermute | solution.py:195
  653.9 96.6 %collective-permute-start.104 = (bf16[512,1024]{1,0:T(8,128)(2,1)}, bf16[512,1024]{1,0:T(8,128)(2,1)}, u32[]{:S(2)}, u32[]{:S(2)}) collective-permute-start(bf16[512,1024]{1,0:T(8,128)(2,1)} %convolution_convert_fusion.3), channel_id=1, source_target_pairs={{0,8},{24,16},{1,9},{25,17},{2,10},{26,18},{3,11},{27,19},{4,12},{... | collective-permute-start | bytes 3145736 | tf_op jit(solution)/shard_map/ppermute | solution.py:201
  660.4 95.9 %collective-permute-start.140 = (bf16[1024,512]{1,0:T(8,128)(2,1)}, bf16[1024,512]{1,0:T(8,128)(2,1)}, u32[]{:S(2)}, u32[]{:S(2)}) collective-permute-start(bf16[1024,512]{1,0:T(8,128)(2,1)} %add_convert_fusion.8), channel_id=1, source_target_pairs={{8,0},{16,24},{9,1},{17,25},{10,2},{18,26},{11,3},{19,27},{12,4},{... | collective-permute-start | bytes 3145736 | tf_op jit(solution)/shard_map/ppermute | solution.py:203
  744.4 78.3 %collective-permute-start.70 = (bf16[2,2,128,2048]{3,2,1,0:T(8,128)(2,1)}, bf16[2,2,128,2048]{3,2,1,0:T(8,128)(2,1)}, u32[]{:S(2)}, u32[]{:S(2)}) collective-permute-start(bf16[2,2,128,2048]{3,2,1,0:T(8,128)(2,1)} %fusion.18), channel_id=1, source_target_pairs={{0,2},{2,0},{4,6},{6,4},{1,3},{3,1},{5,7},{7,5},{8,10},{10,8},{12,... | collective-permute-start | bytes 6291464 | tf_op jit(solution)/shard_map/ppermute | solution.py:64
  750.4 70.9 %collective-permute-start.126 = (bf16[512,1024]{1,0:T(8,128)(2,1)S(1)}, bf16[512,1024]{1,0:T(8,128)(2,1)S(1)}, u32[]{:S(2)}, u32[]{:S(2)}) collective-permute-start(bf16[512,1024]{1,0:T(8,128)(2,1)S(1)} %broadcast_select_fusion.9), channel_id=1, source_target_pairs={{0,6},{2,4},{4,2},{6,0},{1,7},{3,5},{5,3},{7,1},{8,14},{10,12},{12... | collective-permute-start | bytes 3145736 | tf_op jit(solution)/shard_map/ppermute | solution.py:64
  756.3 43.0 %collective-permute-start.93 = (bf16[512,1024]{1,0:T(8,128)(2,1)S(1)}, bf16[512,1024]{1,0:T(8,128)(2,1)S(1)}, u32[]{:S(2)}, u32[]{:S(2)}) collective-permute-start(bf16[512,1024]{1,0:T(8,128)(2,1)S(1)} %add_convert_fusion.15), channel_id=1, source_target_pairs={{8,16},{16,8},{9,17},{17,9},{10,18},{18,10},{11,19},{19,11},{12,20... | collective-permute-start | bytes 3145736 | tf_op jit(solution)/shard_map/ppermute | solution.py:207
  761.2 66.4 %collective-permute-start.127 = (bf16[512,1024]{1,0:T(8,128)(2,1)S(1)}, bf16[512,1024]{1,0:T(8,128)(2,1)S(1)}, u32[]{:S(2)}, u32[]{:S(2)}) collective-permute-start(bf16[512,1024]{1,0:T(8,128)(2,1)S(1)} %broadcast_select_fusion.8), channel_id=1, source_target_pairs={{0,4},{2,6},{4,0},{6,2},{1,5},{3,7},{5,1},{7,3},{8,12},{10,14},{12... | collective-permute-start | bytes 3145736 | tf_op jit(solution)/shard_map/ppermute | solution.py:64
  762.7 79.5 %collective-permute-start.82 = (bf16[512,1024]{1,0:T(8,128)(2,1)S(1)}, bf16[512,1024]{1,0:T(8,128)(2,1)S(1)}, u32[]{:S(2)}, u32[]{:S(2)}) collective-permute-start(bf16[512,1024]{1,0:T(8,128)(2,1)S(1)} %fusion.28), channel_id=1, source_target_pairs={{0,8},{8,0},{16,24},{24,16},{1,9},{9,1},{17,25},{25,17},{2,10},{10... | collective-permute-start | bytes 3145736 | tf_op jit(solution)/shard_map/ppermute | solution.py:195
  799.3 45.4 %collective-permute-start.106 = (bf16[512,1024]{1,0:T(8,128)(2,1)S(1)}, bf16[512,1024]{1,0:T(8,128)(2,1)S(1)}, u32[]{:S(2)}, u32[]{:S(2)}) collective-permute-start(bf16[512,1024]{1,0:T(8,128)(2,1)S(1)} %fusion.32), channel_id=1, source_target_pairs={{0,8},{8,0},{16,24},{24,16},{1,9},{9,1},{17,25},{25,17},{2,10},{10... | collective-permute-start | bytes 3145736 | tf_op jit(solution)/shard_map/ppermute | solution.py:195
  821.3 55.7 %collective-permute-start.94 = (bf16[512,1024]{1,0:T(8,128)(2,1)S(1)}, bf16[512,1024]{1,0:T(8,128)(2,1)S(1)}, u32[]{:S(2)}, u32[]{:S(2)}) collective-permute-start(bf16[512,1024]{1,0:T(8,128)(2,1)S(1)} %fusion.30), channel_id=1, source_target_pairs={{0,8},{8,0},{16,24},{24,16},{1,9},{9,1},{17,25},{25,17},{2,10},{10... | collective-permute-start | bytes 3145736 | tf_op jit(solution)/shard_map/ppermute | solution.py:195
  846.5 32.2 %collective-permute-start.107 = (bf16[512,1024]{1,0:T(8,128)(2,1)S(1)}, bf16[512,1024]{1,0:T(8,128)(2,1)S(1)}, u32[]{:S(2)}, u32[]{:S(2)}) collective-permute-start(bf16[512,1024]{1,0:T(8,128)(2,1)S(1)} %add_convert_fusion.5), channel_id=1, source_target_pairs={{8,16},{16,8},{9,17},{17,9},{10,18},{18,10},{11,19},{19,11},{12,20... | collective-permute-start | bytes 3145736 | tf_op jit(solution)/shard_map/ppermute | solution.py:207
  848.3 128.5 %collective-permute-start.131 = (bf16[512,1024]{1,0:T(8,128)(2,1)S(1)}, bf16[512,1024]{1,0:T(8,128)(2,1)S(1)}, u32[]{:S(2)}, u32[]{:S(2)}) collective-permute-start(bf16[512,1024]{1,0:T(8,128)(2,1)S(1)} %broadcast_select_fusion.5), channel_id=1, source_target_pairs={{0,4},{2,6},{4,0},{6,2},{1,5},{3,7},{5,1},{7,3},{8,12},{10,14},{12... | collective-permute-start | bytes 3145736 | tf_op jit(solution)/shard_map/ppermute | solution.py:64
  850.3 47.1 %collective-permute-start.45 = (bf16[1,128,2048]{2,1,0:T(8,128)(2,1)S(1)}, bf16[1,128,2048]{2,1,0:T(8,128)(2,1)S(1)}, u32[]{:S(2)}, u32[]{:S(2)}) collective-permute-start(bf16[1,128,2048]{2,1,0:T(8,128)(2,1)S(1)} %maximum_bitcast_fusion), channel_id=1, source_target_pairs={{0,1},{1,0},{2,3},{3,2},{4,5},{5,4},{6,7},{7,6},{8,9},{9,8},{10,11... | collective-permute-start | bytes 1572872 | tf_op jit(solution)/shard_map/ppermute | solution.py:66
  852.2 47.1 %collective-permute-start.84 = (bf16[512,768]{1,0:T(8,128)(2,1)S(1)}, bf16[512,768]{1,0:T(8,128)(2,1)S(1)}, u32[]{:S(2)}, u32[]{:S(2)}) collective-permute-start(bf16[512,768]{1,0:T(8,128)(2,1)S(1)} %copy-done.97), channel_id=1, source_target_pairs={{0,8},{24,16},{1,9},{25,17},{2,10},{26,18},{3,11},{27,19},{4,12},{... | collective-permute-start | bytes 2359304 | tf_op jit(solution)/shard_map/ppermute | solution.py:201
  877.8 23.0 %collective-permute-start.95 = (bf16[512,1024]{1,0:T(8,128)(2,1)S(1)}, bf16[512,1024]{1,0:T(8,128)(2,1)S(1)}, u32[]{:S(2)}, u32[]{:S(2)}) collective-permute-start(bf16[512,1024]{1,0:T(8,128)(2,1)S(1)} %get-tuple-element.144), channel_id=1, source_target_pairs={{8,16},{16,8},{9,17},{17,9},{10,18},{18,10},{11,19},{19,11},{12,20... | collective-permute-start | bytes 3145736 | tf_op jit(solution)/shard_map/ppermute | solution.py:207
  879.8 33.3 %collective-permute-start.108 = (bf16[256,2048]{1,0:T(8,128)(2,1)S(1)}, bf16[256,2048]{1,0:T(8,128)(2,1)S(1)}, u32[]{:S(2)}, u32[]{:S(2)}) collective-permute-start(bf16[256,2048]{1,0:T(8,128)(2,1)S(1)} %copy-done.65), channel_id=1, source_target_pairs={{0,8},{24,16},{1,9},{25,17},{2,10},{26,18},{3,11},{27,19},{4,12},{... | collective-permute-start | bytes 3145736 | tf_op jit(solution)/shard_map/ppermute | solution.py:201
  897.3 21.9 %collective-permute-start.75 = (bf16[1,128,2048]{2,1,0:T(8,128)(2,1)S(1)}, bf16[1,128,2048]{2,1,0:T(8,128)(2,1)S(1)}, u32[]{:S(2)}, u32[]{:S(2)}) collective-permute-start(bf16[1,128,2048]{2,1,0:T(8,128)(2,1)S(1)} %maximum_bitcast_fusion.1), channel_id=1, source_target_pairs={{0,1},{1,0},{2,3},{3,2},{4,5},{5,4},{6,7},{7,6},{8,9},{9,8},{10,11... | collective-permute-start | bytes 1572872 | tf_op jit(solution)/shard_map/ppermute | solution.py:66
  899.3 20.7 %collective-permute-start.129 = (bf16[512,1024]{1,0:T(8,128)(2,1)S(1)}, bf16[512,1024]{1,0:T(8,128)(2,1)S(1)}, u32[]{:S(2)}, u32[]{:S(2)}) collective-permute-start(bf16[512,1024]{1,0:T(8,128)(2,1)S(1)} %add_convert_fusion.4), channel_id=1, source_target_pairs={{8,0},{16,24},{9,1},{17,25},{10,2},{18,26},{11,3},{19,27},{12,4},{... | collective-permute-start | bytes 3145736 | tf_op jit(solution)/shard_map/ppermute | solution.py:203
  900.9 20.6 %collective-permute-start.85 = (bf16[512,768]{1,0:T(8,128)(2,1)S(1)}, bf16[512,768]{1,0:T(8,128)(2,1)S(1)}, u32[]{:S(2)}, u32[]{:S(2)}) collective-permute-start(bf16[512,768]{1,0:T(8,128)(2,1)S(1)} %add_convert_fusion.35), channel_id=1, source_target_pairs={{8,16},{16,8},{9,17},{17,9},{10,18},{18,10},{11,19},{19,11},{12,20... | collective-permute-start | bytes 2359304 | tf_op jit(solution)/shard_map/ppermute | solution.py:207
  920.0 93.4 %collective-permute-start.134 = (bf16[512,1024]{1,0:T(8,128)(2,1)S(1)}, bf16[512,1024]{1,0:T(8,128)(2,1)S(1)}, u32[]{:S(2)}, u32[]{:S(2)}) collective-permute-start(bf16[512,1024]{1,0:T(8,128)(2,1)S(1)} %add_convert_fusion.20), channel_id=1, source_target_pairs={{8,0},{16,24},{9,1},{17,25},{10,2},{18,26},{11,3},{19,27},{12,4},{... | collective-permute-start | bytes 3145736 | tf_op jit(solution)/shard_map/ppermute | solution.py:203
  921.5 49.0 %collective-permute-start.132 = (bf16[512,1024]{1,0:T(8,128)(2,1)S(1)}, bf16[512,1024]{1,0:T(8,128)(2,1)S(1)}, u32[]{:S(2)}, u32[]{:S(2)}) collective-permute-start(bf16[512,1024]{1,0:T(8,128)(2,1)S(1)} %add_convert_fusion.12), channel_id=1, source_target_pairs={{8,0},{16,24},{9,1},{17,25},{10,2},{18,26},{11,3},{19,27},{12,4},{... | collective-permute-start | bytes 3145736 | tf_op jit(solution)/shard_map/ppermute | solution.py:203
  932.1 39.2 %collective-permute-start.130 = (bf16[512,1024]{1,0:T(8,128)(2,1)S(1)}, bf16[512,1024]{1,0:T(8,128)(2,1)S(1)}, u32[]{:S(2)}, u32[]{:S(2)}) collective-permute-start(bf16[512,1024]{1,0:T(8,128)(2,1)S(1)} %broadcast_select_fusion.6), channel_id=1, source_target_pairs={{0,6},{2,4},{4,2},{6,0},{1,7},{3,5},{5,3},{7,1},{8,14},{10,12},{12... | collective-permute-start | bytes 3145736 | tf_op jit(solution)/shard_map/ppermute | solution.py:64
  932.3 55.0 %collective-permute-start.86 = (bf16[512,768]{1,0:T(8,128)(2,1)S(1)}, bf16[512,768]{1,0:T(8,128)(2,1)S(1)}, u32[]{:S(2)}, u32[]{:S(2)}) collective-permute-start(bf16[512,768]{1,0:T(8,128)(2,1)S(1)} %add_convert_fusion.34), channel_id=1, source_target_pairs={{8,0},{16,24},{9,1},{17,25},{10,2},{18,26},{11,3},{19,27},{12,4},{... | collective-permute-start | bytes 2359304 | tf_op jit(solution)/shard_map/ppermute | solution.py:203
  976.8 33.0 %collective-permute-start.116 = (bf16[256,2048]{1,0:T(8,128)(2,1)S(1)}, bf16[256,2048]{1,0:T(8,128)(2,1)S(1)}, u32[]{:S(2)}, u32[]{:S(2)}) collective-permute-start(bf16[256,2048]{1,0:T(8,128)(2,1)S(1)} %add_convert_fusion.2), channel_id=1, source_target_pairs={{8,0},{16,24},{9,1},{17,25},{10,2},{18,26},{11,3},{19,27},{12,4},{... | collective-permute-start | bytes 3145736 | tf_op jit(solution)/shard_map/ppermute | solution.py:203
  987.3 23.8 %collective-permute-start.133 = (bf16[512,1024]{1,0:T(8,128)(2,1)S(1)}, bf16[512,1024]{1,0:T(8,128)(2,1)S(1)}, u32[]{:S(2)}, u32[]{:S(2)}) collective-permute-start(bf16[512,1024]{1,0:T(8,128)(2,1)S(1)} %broadcast_select_fusion.4), channel_id=1, source_target_pairs={{0,2},{2,0},{4,6},{6,4},{1,3},{3,1},{5,7},{7,5},{8,10},{10,8},{12,... | collective-permute-start | bytes 3145736 | tf_op jit(solution)/shard_map/ppermute | solution.py:64
  987.4 23.3 %collective-permute-start.87 = (bf16[512,768]{1,0:T(8,128)(2,1)S(1)}, bf16[512,768]{1,0:T(8,128)(2,1)S(1)}, u32[]{:S(2)}, u32[]{:S(2)}) collective-permute-start(bf16[512,768]{1,0:T(8,128)(2,1)S(1)} %broadcast_select_fusion.13), channel_id=1, source_target_pairs={{0,6},{2,4},{4,2},{6,0},{1,7},{3,5},{5,3},{7,1},{8,14},{10,12},{12... | collective-permute-start | bytes 2359304 | tf_op jit(solution)/shard_map/ppermute | solution.py:64
  989.6 32.3 %collective-permute-start.98 = (bf16[512,768]{1,0:T(8,128)(2,1)S(1)}, bf16[512,768]{1,0:T(8,128)(2,1)S(1)}, u32[]{:S(2)}, u32[]{:S(2)}) collective-permute-start(bf16[512,768]{1,0:T(8,128)(2,1)S(1)} %fusion.63), channel_id=1, source_target_pairs={{0,8},{8,0},{16,24},{24,16},{1,9},{9,1},{17,25},{25,17},{2,10},{10... | collective-permute-start | bytes 2359304 | tf_op jit(solution)/shard_map/ppermute | solution.py:195
  1021.9 23.7 %collective-permute-start.99 = (bf16[512,768]{1,0:T(8,128)(2,1)S(1)}, bf16[512,768]{1,0:T(8,128)(2,1)S(1)}, u32[]{:S(2)}, u32[]{:S(2)}) collective-permute-start(bf16[512,768]{1,0:T(8,128)(2,1)S(1)} %broadcast_select_fusion.12), channel_id=1, source_target_pairs={{0,4},{2,6},{4,0},{6,2},{1,5},{3,7},{5,1},{7,3},{8,12},{10,14},{12... | collective-permute-start | bytes 2359304 | tf_op jit(solution)/shard_map/ppermute | solution.py:64
  1024.8 20.6 %collective-permute-start.112 = (bf16[512,768]{1,0:T(8,128)(2,1)S(1)}, bf16[512,768]{1,0:T(8,128)(2,1)S(1)}, u32[]{:S(2)}, u32[]{:S(2)}) collective-permute-start(bf16[512,768]{1,0:T(8,128)(2,1)S(1)} %add_convert_fusion.30), channel_id=1, source_target_pairs={{8,0},{16,24},{9,1},{17,25},{10,2},{18,26},{11,3},{19,27},{12,4},{... | collective-permute-start | bytes 2359304 | tf_op jit(solution)/shard_map/ppermute | solution.py:203
  1026.8 31.2 %collective-permute-start.115 = (bf16[512,768]{1,0:T(8,128)(2,1)S(1)}, bf16[512,768]{1,0:T(8,128)(2,1)S(1)}, u32[]{:S(2)}, u32[]{:S(2)}) collective-permute-start(bf16[512,768]{1,0:T(8,128)(2,1)S(1)} %add_convert_fusion.28), channel_id=1, source_target_pairs={{8,0},{16,24},{9,1},{17,25},{10,2},{18,26},{11,3},{19,27},{12,4},{... | collective-permute-start | bytes 2359304 | tf_op jit(solution)/shard_map/ppermute | solution.py:203
  (232 other events, 2509.2 us)
Sparse Core Ops, SparseCore 0:
  144.1 46.2 all-gather.3
  192.5 44.6 all-gather.5
  239.4 44.5 all-gather.7

commit v2 on v1

--- a/solution.py
+++ b/solution.py
@@ -42,6 +42,14 @@
     return lax.dot_general(
         left_side, weight, (((1,), (1,)), ((), ())), preferred_element_type=F32
     )
+
+
+def together(*values):
+    return lax.optimization_barrier(values)
+
+
+def unchanged(value):
+    return value
 
 
 class Plane:
@@ -87,12 +95,13 @@
             axis=-1,
         )
 
-    def gather(self, own):
+    def gather(self, own, step=unchanged):
         blocks = {(0, 0): own}
         if self.rows == 4 and self.cols == 2:
             half = own.shape[0] // 2
             blocks[0, 2] = self.hop(self.turn(own, 2), 2)
             blocks[1, 0] = self.hop(own, 0, 1)
+            blocks = step(blocks)
             blocks[1, 2] = jnp.concatenate(
                 [
                     self.hop(blocks[0, 2][:half], 0, 1),
@@ -104,7 +113,7 @@
             for col_xor in reversed(range(self.cols)):
                 for row_xor in reversed(range(0, self.rows, 2)):
                     blocks[col_xor, row_xor] = self.hop(self.turn(own, row_xor), row_xor, col_xor)
-        return self.over_cores(blocks)
+        return step(self.over_cores(blocks))
 
     def over_cores(self, blocks):
         for col_xor in range(self.cols):
@@ -127,21 +136,23 @@
                     blocks[col_xor, row_xor] = own[col_xor]
         return self.over_cores(blocks)
 
-    def scatter(self, partial):
+    def scatter(self, partial, step=unchanged):
         tokens = partial.shape[0] // (self.rows * self.cols)
         blocks = partial.reshape(self.cols, self.rows, tokens, -1)
         if self.rows == 4 and self.cols == 2:
             half = tokens // 2
             away = self.hop(self.turn(jnp.stack([blocks[:, 1], blocks[:, 3]]), 1), 1)
+            away, blocks = step((away, blocks))
             near = [blocks[:, 2 * k].astype(F32) + away[k].astype(F32) for k in range(2)]
-            by_row = self.hop(self.turn(near[1][:, :half].astype(BF), 2), 2).astype(F32)
+            by_row = self.hop(self.turn(near[1][:, :half].astype(BF), 2), 2)
             far = jnp.stack([near[0][1, half:], near[1][1, half:]]).astype(BF)
-            by_col = self.hop(far, 0, 1).astype(F32)
-            first = [near[0][k, :half] + by_row[k] for k in range(2)]
-            second = [near[k][0, half:] + by_col[k] for k in range(2)]
+            by_col = self.hop(far, 0, 1)
+            by_row, by_col, near = step((by_row, by_col, near))
+            first = [near[0][k, :half] + by_row[k].astype(F32) for k in range(2)]
+            second = [near[k][0, half:] + by_col[k].astype(F32) for k in range(2)]
             last_col = self.hop(first[1].astype(BF), 0, 1).astype(F32)
             last_row = self.hop(self.turn(second[1].astype(BF), 2), 2).astype(F32)
-            return jnp.concatenate([first[0] + last_col, second[0] + last_row], axis=0)
+            return step(jnp.concatenate([first[0] + last_col, second[0] + last_row], axis=0))
         sums = {}
         for col_xor in reversed(range(self.cols)):
             for row_xor in reversed(range(0, self.rows, 2)):
@@ -180,32 +191,69 @@
     return (one.astype(F32) + other.astype(F32)).astype(BF)
 
 
-def group_sums(arrays, lag=3):
-    if lax.axis_size("dp") != 4:
-        return [lax.psum(array, "dp") for array in arrays]
-    place = lax.axis_index("dp")
-    inner = (place == 1) | (place == 2)
-    count = len(arrays)
-    arrived, full, result = {}, {}, {}
-    for step in range(count + lag):
-        back = step - lag
-        array = arrays[step] if step < count else None
-        if back >= 0 and array is not None and full[back].shape == array.shape:
-            sent = jnp.where(inner, full[back], array)
-            arrived[step] = lax.ppermute(sent, "dp", ENDS)
-            result[back] = jnp.where(inner, sent, arrived[step])
+class Line:
+    depth = 2
+
+    def __init__(self, move):
+        self.line = lax.axis_size("dp") == 4
+        place = lax.axis_index("dp")
+        self.inner = (place == 1) | (place == 2)
+        self.move = move
+        self.arrays, self.pairs, self.full, self.placed = [], [], [], []
+        self.pending = [{}] * self.depth
+        self.moving = [[]] * (self.depth + 1)
+        self.sent_back = 0
+
+    def step(self, values, array=None):
+        if not self.line:
+            if array is not None:
+                self.arrays.append(array)
+            return values
+        pending, moving, array, values = lax.optimization_barrier(
+            (self.pending.pop(0), self.moving.pop(0), array, values)
+        )
+        self.advance(pending, moving, array)
+        return values
+
+    def advance(self, pending, moving, array):
+        self.placed += moving
+        current, moved = {}, []
+        if "back" in pending:
+            total = jnp.where(self.inner, pending["full"], pending["back"])
+            moved.append(self.move(len(self.placed) + sum(map(len, self.moving)), total))
+        self.moving.append(moved)
+        if "across" in pending:
+            self.full.append(plus(self.pairs[len(self.full)], pending["across"]))
+        if "inward" in pending:
+            pair = plus(self.arrays[len(self.pairs)], pending["inward"])
+            self.pairs.append(pair)
+            current["across"] = lax.ppermute(pair, "dp", MIDDLE)
+        back = None
+        if len(self.full) > self.sent_back:
+            back = self.full[self.sent_back]
+            self.sent_back += 1
+        if array is not None:
+            self.arrays.append(array)
+        if back is not None and array is not None and back.shape == array.shape:
+            sent = jnp.where(self.inner, back, array)
+            current["full"] = sent
+            current["inward"] = lax.ppermute(sent, "dp", ENDS)
+            current["back"] = current["inward"]
         else:
-            if back >= 0 and array is not None:
-                full[back], array = lax.optimization_barrier((full[back], array))
             if array is not None:
-                arrived[step] = lax.ppermute(array, "dp", [(0, 1), (3, 2)])
-            if back >= 0:
-                again = lax.ppermute(full[back], "dp", [(1, 0), (2, 3)])
-                result[back] = jnp.where(inner, full[back], again)
-        if array is not None:
-            pair = plus(array, arrived[step])
-            full[step] = plus(pair, lax.ppermute(pair, "dp", MIDDLE))
-    return [result[k] for k in range(count)]
+                current["inward"] = lax.ppermute(array, "dp", [(0, 1), (3, 2)])
+            if back is not None:
+                current["full"] = back
+                current["back"] = lax.ppermute(back, "dp", [(1, 0), (2, 3)])
+        self.pending.append(current)
+
+    def finish(self):
+        if not self.line:
+            totals = [lax.psum(array, "dp") for array in self.arrays]
+            return [self.move(index, total) for index, total in enumerate(totals)]
+        while len(self.placed) < len(self.arrays):
+            self.advance(self.pending.pop(0), self.moving.pop(0), None)
+        return self.placed
 
 
 def group_total(vector):
@@ -287,23 +335,36 @@
             for k, piece in enumerate(pieces)
             if k >= 2
         ]
-        far = lax.all_gather(jnp.concatenate(parts, axis=1), "dp", axis=0, tiled=True)
-        far = jnp.split(far, rows - 2, axis=1)
-        return pieces[:1] + [plane.hop(pieces[1], 1)] + far
-
-    trios = zip(
-        pieces_of(query_weight, 1), pieces_of(key_weight, 1), pieces_of(value_weight, 1), strict=True
-    )
-    trios = [plane.hop(jnp.stack(trio), k) for k, trio in enumerate(trios)]
+        return pieces[:1] + [plane.hop(pieces[1], 1)], jnp.concatenate(parts, axis=1)
+
+    def whole(pieces, far, axis):
+        return jnp.concatenate(pieces + jnp.split(far, rows - 2, axis=1), axis=axis)
+
+    def over_groups(part):
+        return lax.all_gather(part, "dp", axis=0, tiled=True)
+
+    gate_pieces, gate_far = shared(gate_weight, 1)
+    trios = [
+        jnp.stack(trio)
+        for trio in zip(
+            pieces_of(query_weight, 1),
+            pieces_of(key_weight, 1),
+            pieces_of(value_weight, 1),
+            strict=True,
+        )
+    ]
+    gate_far, trios[2:] = together(gate_far, trios[2:])
+    gate_far = over_groups(gate_far)
+    trios = [plane.hop(trio, k) for k, trio in enumerate(trios)]
+    gate_far, trios, inputs_all = together(gate_far, trios, inputs_all)
+    up_pieces, up_far = shared(up_weight, 1)
+    down_pieces, down_far = shared(down_weight, 0)
     w_query, w_key, w_value = (
         jnp.concatenate([trio[k] for trio in trios], axis=0) for k in range(3)
     )
-    w_gate = jnp.concatenate(shared(gate_weight, 1), axis=0)
     w_out = jnp.concatenate(
         [plane.hop(piece, k) for k, piece in enumerate(pieces_of(out_weight, 0))], axis=1
     )
-    w_up = jnp.concatenate(shared(up_weight, 1), axis=0)
-    w_down = jnp.concatenate(shared(down_weight, 0), axis=1)
     gains = jnp.stack([attn_gain, mlp_gain])
     gains = jnp.concatenate([plane.hop(gains, k) for k in range(rows)], axis=1).astype(F32)
     attn_gain_f, mlp_gain_f = gains[0:1], gains[1:2]
@@ -362,6 +423,8 @@
     q_rot = rotate_pairs(heads_of(q_unit * q_gain_f), cos_table, sin_table).astype(BF)
     k_rot = rotate_pairs(heads_of(k_unit * k_gain_f), cos_table, sin_table).astype(BF)
     values = heads_of(value_low)
+    up_far, q_rot = together(up_far, q_rot)
+    up_far = over_groups(up_far)
     allowed = (places[None, None, :] <= places[None, :, None]) & (
         places[None, None, :] < live_len[:, None, None]
     )
@@ -376,7 +439,13 @@
     attn_mix = joined(
         jnp.einsum("shqk,skhd->sqhd", prob_low, values, preferred_element_type=F32).astype(BF)
     )
+    up_far, down_far, attn_mix = together(up_far, down_far, attn_mix)
+    down_far = over_groups(down_far)
     attn_raw = plane.scatter(dot(attn_mix, w_out).astype(BF))
+    down_far, attn_raw = together(down_far, attn_raw)
+    w_gate = whole(gate_pieces, gate_far, 0)
+    w_up = whole(up_pieces, up_far, 0)
+    w_down = whole(down_pieces, down_far, 1)
     a_scale = rms_scale(attn_raw)
     a_unit = attn_raw * a_scale
     branch_a = a_unit * attn_gain_f
@@ -396,23 +465,39 @@
     d_m_unit = d_full * mlp_gain_f
     d_mlp = m_scale * (d_m_unit - m_unit * jnp.mean(d_m_unit * m_unit, axis=-1, keepdims=True))
     d_mlp_all = plane.gather(d_mlp.astype(BF))
-    grads_down = [against(inner_low, plane.slot(d_mlp_all, k)).astype(BF) for k in range(rows)]
+    order = [k for k in range(2, rows)] + [1, 0]
+    waiting = []
+
+    def move(index, total):
+        if index < 3 * rows:
+            return plane.hop(total, order[index % rows])
+        if index == 3 * rows:
+            return [plane.hop(plane.slot(total, k), k) for k in order]
+        return plane.hop(total, order[(index - 3 * rows - 1) % rows])
+
+    line = Line(move)
+
+    def step(values):
+        return line.step(values, waiting.pop(0) if waiting else None)
+
+    waiting += [against(inner_low, plane.slot(d_mlp_all, k)).astype(BF) for k in order]
+    d_mlp_all = step(d_mlp_all)
     d_inner = through(d_mlp_all, w_down)
     d_gate_low = (d_inner * up_pre * (gate_sig * (1.0 + gate_pre * (1.0 - gate_sig)))).astype(BF)
     d_up_low = (d_inner * gate_act).astype(BF)
-    grads_gate = [against(plane.slot(hidden_all, k), d_gate_low).astype(BF) for k in range(rows)]
-    grads_up = [against(plane.slot(hidden_all, k), d_up_low).astype(BF) for k in range(rows)]
-    d_hidden = d_full + plane.scatter(
-        (through(d_gate_low, w_gate) + through(d_up_low, w_up)).astype(BF)
-    )
+    d_gate_low, d_up_low = step((d_gate_low, d_up_low))
+    waiting += [against(plane.slot(hidden_all, k), d_gate_low).astype(BF) for k in order]
+    waiting += [against(plane.slot(hidden_all, k), d_up_low).astype(BF) for k in order]
+    partial = step((through(d_gate_low, w_gate) + through(d_up_low, w_up)).astype(BF))
+    d_hidden = d_full + plane.scatter(partial, step)
     d_a_unit = d_hidden * attn_gain_f
     d_attn = a_scale * (d_a_unit - a_unit * jnp.mean(d_a_unit * a_unit, axis=-1, keepdims=True))
-    d_attn_all = plane.gather(d_attn.astype(BF))
-    grads_out = against(attn_mix, d_attn_all).astype(BF)
+    d_attn_all = plane.gather(d_attn.astype(BF), step)
+    waiting += [against(attn_mix, d_attn_all).astype(BF)]
     d_mix = heads_of(through(d_attn_all, w_out).astype(BF))
     d_prob = jnp.einsum("sqhd,skhd->shqk", d_mix, values, preferred_element_type=F32)
     row_delta = jnp.sum(prob * d_prob, axis=-1, keepdims=True)
-    d_scores = (prob * (d_prob - row_delta)).astype(BF)
+    d_scores = step((prob * (d_prob - row_delta)).astype(BF))
     d_qrot = (
         jnp.einsum("shqk,skhd->sqhd", d_scores, k_rot, preferred_element_type=F32) * score_scale
     )
@@ -422,32 +507,26 @@
     d_value = jnp.einsum("shqk,sqhd->skhd", prob_low, d_mix, preferred_element_type=F32)
     d_qn = joined(rotate_pairs(d_qrot, cos_table, -sin_table))
     d_kn = joined(rotate_pairs(d_krot, cos_table, -sin_table))
+    d_value = joined(d_value.astype(BF))
     d_q_hat = d_qn * q_gain_f
     d_k_hat = d_kn * k_gain_f
+    d_q_hat, d_k_hat, d_value = step((d_q_hat, d_k_hat, d_value))
     inners = plane.total(
         jnp.stack([jnp.sum(d_q_hat * q_unit, axis=1), jnp.sum(d_k_hat * k_unit, axis=1)])
     )
+    inners = step(inners)
     d_query = q_scale * (d_q_hat - q_unit * (inners[0] / width)[:, None])
     d_key = k_scale * (d_k_hat - k_unit * (inners[1] / width)[:, None])
     d_query = d_query.astype(BF)
     d_key = d_key.astype(BF)
-    d_value = joined(d_value.astype(BF))
     d_qkv = jnp.concatenate([d_query, d_key, d_value], axis=1)
-    grads_qkv = [against(plane.slot(inputs_all, k), d_qkv).astype(BF) for k in range(rows)]
-    d_inputs = d_hidden + plane.scatter(
+    waiting += [against(plane.slot(inputs_all, k), d_qkv).astype(BF) for k in order]
+    partial = step(
         (through(d_query, w_query) + through(d_key, w_key) + through(d_value, w_value)).astype(BF)
     )
-
-    def home(array):
-        own = plane.relative((array).astype(BF)).reshape(seq_own, tok_seq, width)
-        pieces = [own] + [plane.hop(own, 0, k) for k in range(1, cols)]
-        out = jnp.zeros((seq_grp, tok_seq, width), BF)
-        for k in range(cols):
-            out = lax.dynamic_update_slice_in_dim(out, pieces[k], (col ^ k) * seq_own, axis=0)
-        return out
-
-    output = home(result)
-    grad_input = home(d_inputs * valid_rows)
+    d_inputs = d_hidden + plane.scatter(partial, step)
+    while waiting:
+        d_inputs = step(d_inputs)
 
     def finish(blocks, axis):
         size = blocks[0].shape[axis]
@@ -460,23 +539,31 @@
             out = lax.dynamic_update_slice(out, blocks[k].astype(F32), start)
         return out
 
-    order = [k for k in range(2, rows)] + [1, 0]
-    chunks = [grads[k] for grads in (grads_down, grads_gate, grads_up) for k in order]
-    chunks += [grads_out] + [grads_qkv[k] for k in order]
-    summed = group_sums(chunks)
+    line.placed, d_inputs = lax.optimization_barrier((line.placed, d_inputs))
+    placed = line.finish()
 
     def arrived_at(blocks):
-        placed = [plane.hop(block, k) for k, block in zip(order, blocks, strict=True)]
-        return [placed[order.index(k)] for k in range(rows)]
-
-    grad_down = finish(arrived_at(summed[:rows]), 0)
-    grad_gate = finish(arrived_at(summed[rows : 2 * rows]), 1)
-    grad_up = finish(arrived_at(summed[2 * rows : 3 * rows]), 1)
-    grad_out = finish(arrived_at([plane.slot(summed[3 * rows], k) for k in order]), 0)
-    qkv_blocks = arrived_at(summed[3 * rows + 1 :])
+        return [blocks[order.index(k)] for k in range(rows)]
+
+    grad_down = finish(arrived_at(placed[:rows]), 0)
+    grad_gate = finish(arrived_at(placed[rows : 2 * rows]), 1)
+    grad_up = finish(arrived_at(placed[2 * rows : 3 * rows]), 1)
+    grad_out = finish(arrived_at(placed[3 * rows]), 0)
+    qkv_blocks = arrived_at(placed[3 * rows + 1 :])
     grad_query = finish([b[:, :head_part] for b in qkv_blocks], 1)
     grad_key = finish([b[:, head_part : 2 * head_part] for b in qkv_blocks], 1)
     grad_value = finish([b[:, 2 * head_part :] for b in qkv_blocks], 1)
+
+    def home(array):
+        own = plane.relative((array).astype(BF)).reshape(seq_own, tok_seq, width)
+        pieces = [own] + [plane.hop(own, 0, k) for k in range(1, cols)]
+        out = jnp.zeros((seq_grp, tok_seq, width), BF)
+        for k in range(cols):
+            out = lax.dynamic_update_slice_in_dim(out, pieces[k], (col ^ k) * seq_own, axis=0)
+        return out
+
+    output = home(result)
+    grad_input = home(d_inputs * valid_rows)
 
     def sums_of(array):
         return jnp.sum(array.reshape(seq_own, tok_seq * width), axis=1)

time: 1070 us -> 964 us (0.901)
  starting transfers between devices: 289 us -> 196 us
  waiting for transfers between devices: 404 us -> 367 us
  other arithmetic: 116 us -> 137 us
    ppermute x44 -> x47, waiting for transfers between devices: 217 us -> 132 us  [the longest x13 75.2 us: advance(): current['back'] = lax.ppermute(back, 'dp', [(1, 0), (2, 3)])]
    ppermute x44 -> x47, starting transfers between devices: 202 us -> 123 us  [the longest x13 80.7 us: advance(): current['inward'] = lax.ppermute(array, 'dp', [(0, 1), (3, 2)])]
    ppermute x20, waiting for transfers between devices: 31.2 us -> 100 us  [hop(): lax.ppermute(array, 'col', [(a, a ^ col_xor) for a in range(self.cols)])]
    ppermute x74, waiting for transfers between devices: 120 us -> 78.2 us  [hop(): lax.ppermute(array, 'row', [(a, a ^ row_xor) for a in range(self.rows)])]
    ppermute x1, waiting for transfers between devices: 0.01 us -> 15.6 us  [group_total(): vector = vector + lax.ppermute(vector, 'dp', [(0, 1), (3, 2)])]
    convert_element_type x26 -> x30, other arithmetic: 19.5 us -> 30 us  [plus(): return (one.astype(F32) + other.astype(F32)).astype(BF)]
    select_n x21 -> x20, other arithmetic: 14.5 us -> 23.4 us  [the longest x16 13.5 us: advance(): total = jnp.where(self.inner, pending['full'], pending['back'])]
    unnamed x339 -> x371, local copies, waits for them, and re-layouts: 46.5 us -> 44.3 us
  transfers between devices with their start and end apart: 144 -> 147, of which waited for: 56 -> 60; matrix products, arithmetic and copies ran while one was open for 25% -> 30% of each run, Pallas kernels for 0% -> 0%
where the time goes in v2:
time: 964 us; the launch traced here: 958 us
  waiting for transfers between devices  367 us (38%)
  starting transfers between devices  196 us (20%)
  other arithmetic  137 us (14%)
  matrix products  123 us (13%)
  local copies, waits for them, and re-layouts  117 us (12%)
  between operations  18.3 us (2%)
    ppermute x20, waiting for transfers between devices, hop(): lax.ppermute(array, 'col', [(a, a ^ col_xor) for a in range(self.cols)])  100 us
    ppermute x13, starting transfers between devices, advance(): current['inward'] = lax.ppermute(array, 'dp', [(0, 1), (3, 2)])  80.7 us
    ppermute x74, waiting for transfers between devices, hop(): lax.ppermute(array, 'row', [(a, a ^ row_xor) for a in range(self.rows)])  78.2 us
    ppermute x13, waiting for transfers between devices, advance(): current['back'] = lax.ppermute(back, 'dp', [(1, 0), (2, 3)])  75.2 us
    ppermute x13, waiting for transfers between devices, advance(): current['inward'] = lax.ppermute(array, 'dp', [(0, 1), (3, 2)])  48.2 us
    unnamed x371, local copies, waits for them, and re-layouts  44.3 us
    ppermute x74, starting transfers between devices, hop(): lax.ppermute(array, 'row', [(a, a ^ row_xor) for a in range(self.rows)])  42 us
    dot_general x7, matrix products, through(): lax.dot_general(left_side, weight, (((1,), (1,)), ((), ())), preferred_el...  40.2 us
  transfers between devices with their start and end apart: 147, of which 60 were waited for; matrix products, arithmetic and copies ran while one was open for 30% of the time, Pallas kernels for 0%

profile of v2, /device:TPU:0, one launch (start us, length us, event | category | flops | bytes accessed | tf_op | source)
XLA Modules:
  0.0 957.5 jit_solution(9730471628658433982)
XLA Ops:
  11.4 2.9 collective-permute-start.8
  24.3 8.7 collective-permute-done.2
  33.1 4.0 collective-permute-done.3
  52.5 6.6 collective-permute-done.11
  63.8 16.1 %collective-permute-done.6 = bf16[3,512,256]{2,1,0:T(8,128)(2,1)} collective-permute-done((bf16[3,512,256]{2,1,0:T(8,128)(2,1)}, bf16[3,512,256]{2,1,0:T(8,128)(2,1)}, u32[]{:S(2)}, u32[]{:S(2)}) %collective-permute-start.6) | collective-permute-done | bytes 786464 | tf_op jit(solution)/shard_map/ppermute | solution.py:72
  79.9 6.9 all-gather.4.cloned.1.call-done
  122.9 2.9 subtract_convert_fusion
  136.9 4.6 collective-permute-done.17
  142.3 4.3 convolution_convert_fusion.22
  147.9 5.1 fusion.188
  156.3 14.7 %all-gather.6.cloned.1.call-done = bf16[512,2048]{1,0:T(8,128)(2,1)} async-done(((bf16[128,2048]{1,0:T(8,128)(2,1)}), bf16[512,2048]{1,0:T(8,128)(2,1)}) %all-gather.6.cloned.1.call-update) | async-done | bytes 2097168 | tf_op jit(solution)/shard_map/all_gather | solution.py:344
  179.1 3.2 constant_dynamic-slice_fusion.24
  194.2 11.2 %collective-permute-done.24 = bf16[2,64,2048]{2,1,0:T(8,128)(2,1)S(1)} collective-permute-done((bf16[2,64,2048]{2,1,0:T(8,128)(2,1)S(1)}, bf16[2,64,2048]{2,1,0:T(8,128)(2,1)S(1)}, u32[]{:S(2)}, u32[]{:S(2)}) %collective-permute-start.24) | collective-permute-done | bytes 524320 | tf_op jit(solution)/shard_map/ppermute | solution.py:74
  208.6 5.0 collective-permute-done.25
  215.2 16.7 %all-gather.8.cloned.1.call-done = bf16[1024,1024]{1,0:T(8,128)(2,1)} async-done(((bf16[256,1024]{1,0:T(8,128)(2,1)}), bf16[1024,1024]{1,0:T(8,128)(2,1)}) %all-gather.8.cloned.1.call-update) | async-done | bytes 2097168 | tf_op jit(solution)/shard_map/all_gather | solution.py:344
  235.5 10.5 %collective-permute-done.32 = bf16[128,2048]{1,0:T(8,128)(2,1)S(1)} collective-permute-done((bf16[128,2048]{1,0:T(8,128)(2,1)S(1)}, bf16[128,2048]{1,0:T(8,128)(2,1)S(1)}, u32[]{:S(2)}, u32[]{:S(2)}) %collective-permute-start.32) | collective-permute-done | bytes 524320 | tf_op jit(solution)/shard_map/ppermute | solution.py:74
  252.9 5.4 collective-permute-done.34
  263.2 6.6 fusion.58
  269.9 9.6 %multiply_convert_fusion.3 = (bf16[1024,1024]{1,0:T(8,128)(2,1)S(1)}, f32[1024,1024]{1,0:T(8,128)}) fusion(f32[1024,1024]{1,0:T(8,128)S(1)} %fusion.58, bf16[1024,2048]{1,0:T(8,128)(2,1)S(1)} %constant_dynamic-update-slice_fusion.10, bf16[512,1024]{1,0:T(8,128)(2,1)S(1)} %get-tuple-element.364, bf16[512,1024]{1,0:T(8,128)(2,1)S(1)} %get-tuple-element.363, ...), kind=kOutput, calls=%fused_computation.21 | convolution fusion | flops 4318035968 | bytes 18874368 | tf_op jit(solution)/shard_map/dot_general | solution.py:32
  279.5 6.5 convolution_convert_fusion.1
  294.1 5.1 fusion.135
  304.6 10.8 %collective-permute-done.43 = bf16[2,64,2048]{2,1,0:T(8,128)(2,1)} collective-permute-done((bf16[2,64,2048]{2,1,0:T(8,128)(2,1)}, bf16[2,64,2048]{2,1,0:T(8,128)(2,1)}, u32[]{:S(2)}, u32[]{:S(2)}) %collective-permute-start.43) | collective-permute-done | bytes 524320 | tf_op jit(solution)/shard_map/ppermute | solution.py:74
  332.0 10.3 %collective-permute-done.49 = bf16[128,2048]{1,0:T(8,128)(2,1)S(1)} collective-permute-done((bf16[128,2048]{1,0:T(8,128)(2,1)S(1)}, bf16[128,2048]{1,0:T(8,128)(2,1)S(1)}, u32[]{:S(2)}, u32[]{:S(2)}) %collective-permute-start.49) | collective-permute-done | bytes 524320 | tf_op jit(solution)/shard_map/ppermute | solution.py:74
  346.6 6.2 collective-permute-done.51
  362.0 8.8 multiply_convert_fusion.1
  382.6 9.2 fusion.56
  391.8 10.9 %add_convert_fusion.1 = bf16[1024,2048]{1,0:T(8,128)(2,1)} fusion(f32[1024,2048]{1,0:T(8,128)} %fusion.56, bf16[1024,1024]{1,0:T(8,128)(2,1)S(1)} %get-tuple-element.163, bf16[512,1024]{1,0:T(8,128)(2,1)} %copy-done.110, bf16[512,1024]{1,0:T(8,128)(2,1)} %copy-done.109, bf16[512,1024]{1,0:T(8,128)(2,1)} %collective-permute-done.37, ...), kind=kOutput, calls=%fused_computation.3 | convolution fusion | flops 4315938816 | bytes 18874368 | tf_op jit(solution)/shard_map/dot_general | solution.py:42
  420.1 7.6 collective-permute-start.60
  436.2 15.5 %collective-permute-start.58 = (bf16[1024,512]{1,0:T(8,128)(2,1)S(1)}, bf16[1024,512]{1,0:T(8,128)(2,1)S(1)}, u32[]{:S(2)}, u32[]{:S(2)}) collective-permute-start(bf16[1024,512]{1,0:T(8,128)(2,1)S(1)} %convolution_convert_fusion.12), channel_id=1, source_target_pairs={{0,8},{24,16},{1,9},{25,17},{2,10},{26,18},{3,11},{27,19},{4,12},{... | collective-permute-start | bytes 3145736 | tf_op jit(solution)/shard_map/ppermute | solution.py:244
  461.3 7.7 collective-permute-start.70
  469.3 6.0 collective-permute-done.58
  476.5 3.1 multiply_reduce_fusion.3
  489.1 4.6 collective-permute-done.71
  495.8 7.9 collective-permute-start.67
  514.1 7.4 collective-permute-done.76
  523.3 11.8 %collective-permute-done.45 = bf16[1,128,2048]{2,1,0:T(8,128)(2,1)S(1)} collective-permute-done((bf16[1,128,2048]{2,1,0:T(8,128)(2,1)S(1)}, bf16[1,128,2048]{2,1,0:T(8,128)(2,1)S(1)}, u32[]{:S(2)}, u32[]{:S(2)}) %collective-permute-start.45) | collective-permute-done | bytes 524320 | tf_op jit(solution)/shard_map/ppermute | solution.py:74
  544.0 3.2 convolution_convert_fusion.21
  551.2 3.3 fusion.30
  557.9 6.7 collective-permute-done.85
  586.7 7.3 collective-permute-start.81
  595.1 2.9 add_convert_fusion.17
  605.7 4.5 collective-permute-done.80
  611.9 5.2 collective-permute-done.81
  623.3 3.1 collective-permute-done.90
  657.8 3.1 fusion.33
  665.0 5.5 add_convert_fusion
  670.5 15.6 %collective-permute-done.137 = f32[9,1024]{1,0:T(8,128)S(1)} collective-permute-done((f32[9,1024]{1,0:T(8,128)S(1)}, f32[9,1024]{1,0:T(8,128)S(1)}, u32[]{:S(2)}, u32[]{:S(2)}) %collective-permute-start.137) | collective-permute-done | bytes 36896 | tf_op jit(solution)/shard_map/ppermute | solution.py:264
  714.6 4.4 collective-permute-start.99
  733.9 8.7 collective-permute-done.99
  744.6 8.4 collective-permute-start.105
  755.5 13.3 %collective-permute-done.108 = bf16[64,2048]{1,0:T(8,128)(2,1)S(1)} collective-permute-done((bf16[64,2048]{1,0:T(8,128)(2,1)S(1)}, bf16[64,2048]{1,0:T(8,128)(2,1)S(1)}, u32[]{:S(2)}, u32[]{:S(2)}) %collective-permute-start.108) | collective-permute-done | bytes 262176 | tf_op jit(solution)/shard_map/ppermute | solution.py:72
  769.4 6.3 collective-permute-done.107
  778.0 6.7 collective-permute-start.111
  788.2 13.4 %collective-permute-done.111 = bf16[512,768]{1,0:T(8,128)(2,1)S(1)} collective-permute-done((bf16[512,768]{1,0:T(8,128)(2,1)S(1)}, bf16[512,768]{1,0:T(8,128)(2,1)S(1)}, u32[]{:S(2)}, u32[]{:S(2)}) %collective-permute-start.111) | collective-permute-done | bytes 786464 | tf_op jit(solution)/shard_map/ppermute | solution.py:244
  801.6 4.4 collective-permute-start.115
  809.7 12.4 %collective-permute-done.115 = bf16[512,768]{1,0:T(8,128)(2,1)S(1)} collective-permute-done((bf16[512,768]{1,0:T(8,128)(2,1)S(1)}, bf16[512,768]{1,0:T(8,128)(2,1)S(1)}, u32[]{:S(2)}, u32[]{:S(2)}) %collective-permute-start.115) | collective-permute-done | bytes 786464 | tf_op jit(solution)/shard_map/ppermute | solution.py:244
  822.1 4.2 collective-permute-done.114
  841.4 3.6 collective-permute-done.123
  846.5 5.8 collective-permute-start.127
  856.6 9.9 %collective-permute-done.116 = bf16[1,128,2048]{2,1,0:T(8,128)(2,1)S(1)} collective-permute-done((bf16[1,128,2048]{2,1,0:T(8,128)(2,1)S(1)}, bf16[1,128,2048]{2,1,0:T(8,128)(2,1)S(1)}, u32[]{:S(2)}, u32[]{:S(2)}) %collective-permute-start.116) | collective-permute-done | bytes 524320 | tf_op jit(solution)/shard_map/ppermute | solution.py:74
  874.8 19.0 %collective-permute-done.121 = bf16[512,768]{1,0:T(8,128)(2,1)S(1)} collective-permute-done((bf16[512,768]{1,0:T(8,128)(2,1)S(1)}, bf16[512,768]{1,0:T(8,128)(2,1)S(1)}, u32[]{:S(2)}, u32[]{:S(2)}) %collective-permute-start.121) | collective-permute-done | bytes 786464 | tf_op jit(solution)/shard_map/ppermute | solution.py:247
  896.3 19.5 %collective-permute-done.118 = bf16[512,768]{1,0:T(8,128)(2,1)S(1)} collective-permute-done((bf16[512,768]{1,0:T(8,128)(2,1)S(1)}, bf16[512,768]{1,0:T(8,128)(2,1)S(1)}, u32[]{:S(2)}, u32[]{:S(2)}) %collective-permute-start.118) | collective-permute-done | bytes 786464 | tf_op jit(solution)/shard_map/ppermute | solution.py:247
  917.6 15.1 %collective-permute-done.125 = bf16[512,768]{1,0:T(8,128)(2,1)S(1)} collective-permute-done((bf16[512,768]{1,0:T(8,128)(2,1)S(1)}, bf16[512,768]{1,0:T(8,128)(2,1)S(1)}, u32[]{:S(2)}, u32[]{:S(2)}) %collective-permute-start.125) | collective-permute-done | bytes 786464 | tf_op jit(solution)/shard_map/ppermute | solution.py:247
  935.9 11.6 %collective-permute-done.129 = bf16[512,768]{1,0:T(8,128)(2,1)S(1)} collective-permute-done((bf16[512,768]{1,0:T(8,128)(2,1)S(1)}, bf16[512,768]{1,0:T(8,128)(2,1)S(1)}, u32[]{:S(2)}, u32[]{:S(2)}) %collective-permute-start.129) | collective-permute-done | bytes 786464 | tf_op jit(solution)/shard_map/ppermute | solution.py:247
  (991 shorter events, 427.7 us)
Async XLA Ops:
  7.2 79.6 %all-gather.4.cloned.1.call-start = ((), (), s32[]{:S(2)}) async-start(), calls=%async_computation | async-start | bytes 2621440 | tf_op jit(solution)/shard_map/all_gather | solution.py:344
  11.4 28.0 %collective-permute-start.8 = (bf16[128,2048]{1,0:T(8,128)(2,1)}, bf16[128,2048]{1,0:T(8,128)(2,1)S(1)}, u32[]{:S(2)}, u32[]{:S(2)}) collective-permute-start(bf16[128,2048]{1,0:T(8,128)(2,1)} %pad_maximum_fusion.27), channel_id=1, source_target_pairs={{0,4},{2,6},{4,0},{6,2},{1,5},{3,7},{5,1},{7,3},{8,12},{10,14},{12... | collective-permute-start | bytes 1572872 | tf_op jit(solution)/shard_map/ppermute | solution.py:72
  15.3 29.5 %collective-permute-start.7 = (bf16[128,2048]{1,0:T(8,128)(2,1)}, bf16[128,2048]{1,0:T(8,128)(2,1)}, u32[]{:S(2)}, u32[]{:S(2)}) collective-permute-start(bf16[128,2048]{1,0:T(8,128)(2,1)} %pad_maximum_fusion.26), channel_id=1, source_target_pairs={{0,2},{2,0},{4,6},{6,4},{1,3},{3,1},{5,7},{7,5},{8,10},{10,8},{12,... | collective-permute-start | bytes 1572872 | tf_op jit(solution)/shard_map/ppermute | solution.py:72
  21.9 41.7 %collective-permute-start.4 = (bf16[3,512,256]{2,1,0:T(8,128)(2,1)}, bf16[3,512,256]{2,1,0:T(8,128)(2,1)}, u32[]{:S(2)}, u32[]{:S(2)}) collective-permute-start(bf16[3,512,256]{2,1,0:T(8,128)(2,1)} %pad_maximum_fusion.19), channel_id=1, source_target_pairs={{0,2},{2,0},{4,6},{6,4},{1,3},{3,1},{5,7},{7,5},{8,10},{10,8},{12,... | collective-permute-start | bytes 2359304 | tf_op jit(solution)/shard_map/ppermute | solution.py:72
  38.9 132.1 %all-gather.6.cloned.1.call-start = ((), (), s32[]{:S(2)}) async-start(), calls=%async_computation.1 | async-start | bytes 2621440 | tf_op jit(solution)/shard_map/all_gather | solution.py:344
  44.8 35.1 %collective-permute-start.6 = (bf16[3,512,256]{2,1,0:T(8,128)(2,1)}, bf16[3,512,256]{2,1,0:T(8,128)(2,1)}, u32[]{:S(2)}, u32[]{:S(2)}) collective-permute-start(bf16[3,512,256]{2,1,0:T(8,128)(2,1)} %pad_maximum_fusion.17), channel_id=1, source_target_pairs={{0,6},{2,4},{4,2},{6,0},{1,7},{3,5},{5,3},{7,1},{8,14},{10,12},{12... | collective-permute-start | bytes 2359304 | tf_op jit(solution)/shard_map/ppermute | solution.py:72
  59.3 44.5 %collective-permute-start = (bf16[128,1024]{1,0:T(8,128)(2,1)}, bf16[128,1024]{1,0:T(8,128)(2,1)S(1)}, u32[]{:S(2)}, u32[]{:S(2)}) collective-permute-start(bf16[128,1024]{1,0:T(8,128)(2,1)} %get-tuple-element.340), channel_id=1, source_target_pairs={{0,4},{2,6},{4,0},{6,2},{1,5},{3,7},{5,1},{7,3},{8,12},{10,14},{12... | collective-permute-start | bytes 786440 | tf_op jit(solution)/shard_map/ppermute | solution.py:72
  62.8 41.0 %collective-permute-start.1 = (bf16[128,1024]{1,0:T(8,128)(2,1)S(1)}, bf16[128,1024]{1,0:T(8,128)(2,1)}, u32[]{:S(2)}, u32[]{:S(2)}) collective-permute-start(bf16[128,1024]{1,0:T(8,128)(2,1)S(1)} %get-tuple-element.341), channel_id=1, source_target_pairs={{0,6},{2,4},{4,2},{6,0},{1,7},{3,5},{5,3},{7,1},{8,14},{10,12},{12... | collective-permute-start | bytes 786440 | tf_op jit(solution)/shard_map/ppermute | solution.py:72
  126.1 105.7 %all-gather.8.cloned.1.call-start = ((), (), s32[]{:S(2)}) async-start(), calls=%async_computation.2 | async-start | bytes 2621440 | tf_op jit(solution)/shard_map/all_gather | solution.py:344
  131.4 39.5 %collective-permute-start.18 = (bf16[256,512]{1,0:T(8,128)(2,1)}, bf16[256,512]{1,0:T(8,128)(2,1)}, u32[]{:S(2)}, u32[]{:S(2)}) collective-permute-start(bf16[256,512]{1,0:T(8,128)(2,1)} %get-tuple-element.391), channel_id=1, source_target_pairs={{0,2},{2,0},{4,6},{6,4},{1,3},{3,1},{5,7},{7,5},{8,10},{10,8},{12,... | collective-permute-start | bytes 786440 | tf_op jit(solution)/shard_map/ppermute | solution.py:72
  132.0 39.0 %collective-permute-start.19 = (bf16[256,512]{1,0:T(8,128)(2,1)}, bf16[256,512]{1,0:T(8,128)(2,1)}, u32[]{:S(2)}, u32[]{:S(2)}) collective-permute-start(bf16[256,512]{1,0:T(8,128)(2,1)} %get-tuple-element.393), channel_id=1, source_target_pairs={{0,4},{2,6},{4,0},{6,2},{1,5},{3,7},{5,1},{7,3},{8,12},{10,14},{12... | collective-permute-start | bytes 786440 | tf_op jit(solution)/shard_map/ppermute | solution.py:72
  133.5 37.5 %collective-permute-start.20 = (bf16[256,512]{1,0:T(8,128)(2,1)}, bf16[256,512]{1,0:T(8,128)(2,1)}, u32[]{:S(2)}, u32[]{:S(2)}) collective-permute-start(bf16[256,512]{1,0:T(8,128)(2,1)} %get-tuple-element.392), channel_id=1, source_target_pairs={{0,6},{2,4},{4,2},{6,0},{1,7},{3,5},{5,3},{7,1},{8,14},{10,12},{12... | collective-permute-start | bytes 786440 | tf_op jit(solution)/shard_map/ppermute | solution.py:72
  182.3 79.4 %collective-permute-start.37 = (bf16[512,1024]{1,0:T(8,128)(2,1)}, bf16[512,1024]{1,0:T(8,128)(2,1)}, u32[]{:S(2)}, u32[]{:S(2)}) collective-permute-start(bf16[512,1024]{1,0:T(8,128)(2,1)} %get-tuple-element.331), channel_id=1, source_target_pairs={{0,2},{2,0},{4,6},{6,4},{1,3},{3,1},{5,7},{7,5},{8,10},{10,8},{12,... | collective-permute-start | bytes 3145736 | tf_op jit(solution)/shard_map/ppermute | solution.py:72
  186.7 83.1 %collective-permute-start.38 = (bf16[512,1024]{1,0:T(8,128)(2,1)}, bf16[512,1024]{1,0:T(8,128)(2,1)}, u32[]{:S(2)}, u32[]{:S(2)}) collective-permute-start(bf16[512,1024]{1,0:T(8,128)(2,1)} %get-tuple-element.333), channel_id=1, source_target_pairs={{0,2},{2,0},{4,6},{6,4},{1,3},{3,1},{5,7},{7,5},{8,10},{10,8},{12,... | collective-permute-start | bytes 3145736 | tf_op jit(solution)/shard_map/ppermute | solution.py:72
  191.0 88.4 %collective-permute-start.39 = (bf16[1024,512]{1,0:T(8,128)(2,1)S(1)}, bf16[1024,512]{1,0:T(8,128)(2,1)}, u32[]{:S(2)}, u32[]{:S(2)}) collective-permute-start(bf16[1024,512]{1,0:T(8,128)(2,1)S(1)} %copy-done.75), channel_id=1, source_target_pairs={{0,2},{2,0},{4,6},{6,4},{1,3},{3,1},{5,7},{7,5},{8,10},{10,8},{12,... | collective-permute-start | bytes 3145736 | tf_op jit(solution)/shard_map/ppermute | solution.py:72
  377.6 25.5 %collective-permute-start.55 = (bf16[1024,512]{1,0:T(8,128)(2,1)}, bf16[1024,512]{1,0:T(8,128)(2,1)}, u32[]{:S(2)}, u32[]{:S(2)}) collective-permute-start(bf16[1024,512]{1,0:T(8,128)(2,1)} %convolution_convert_fusion.13), channel_id=1, source_target_pairs={{0,8},{24,16},{1,9},{25,17},{2,10},{26,18},{3,11},{27,19},{4,12},{... | collective-permute-start | bytes 3145736 | tf_op jit(solution)/shard_map/ppermute | solution.py:244
  380.3 47.5 %collective-permute-start.54 = (bf16[1024,512]{1,0:T(8,128)(2,1)}, bf16[1024,512]{1,0:T(8,128)(2,1)}, u32[]{:S(2)}, u32[]{:S(2)}) collective-permute-start(bf16[1024,512]{1,0:T(8,128)(2,1)} %convolution_convert_fusion.14), channel_id=1, source_target_pairs={{0,8},{24,16},{1,9},{25,17},{2,10},{26,18},{3,11},{27,19},{4,12},{... | collective-permute-start | bytes 3145736 | tf_op jit(solution)/shard_map/ppermute | solution.py:244
  420.1 31.6 %collective-permute-start.60 = (bf16[1024,512]{1,0:T(8,128)(2,1)S(1)}, bf16[1024,512]{1,0:T(8,128)(2,1)S(1)}, u32[]{:S(2)}, u32[]{:S(2)}) collective-permute-start(bf16[1024,512]{1,0:T(8,128)(2,1)S(1)} %copy-done.80), channel_id=1, source_target_pairs={{0,8},{24,16},{1,9},{25,17},{2,10},{26,18},{3,11},{27,19},{4,12},{... | collective-permute-start | bytes 3145736 | tf_op jit(solution)/shard_map/ppermute | solution.py:244
  435.5 33.8 %collective-permute-start.57 = (bf16[1024,512]{1,0:T(8,128)(2,1)S(1)}, bf16[1024,512]{1,0:T(8,128)(2,1)S(1)}, u32[]{:S(2)}, u32[]{:S(2)}) collective-permute-start(bf16[1024,512]{1,0:T(8,128)(2,1)S(1)} %add_convert_fusion.27), channel_id=1, source_target_pairs={{8,16},{16,8},{9,17},{17,9},{10,18},{18,10},{11,19},{19,11},{12,20... | collective-permute-start | bytes 3145736 | tf_op jit(solution)/shard_map/ppermute | solution.py:230
  436.2 39.1 %collective-permute-start.58 = (bf16[1024,512]{1,0:T(8,128)(2,1)S(1)}, bf16[1024,512]{1,0:T(8,128)(2,1)S(1)}, u32[]{:S(2)}, u32[]{:S(2)}) collective-permute-start(bf16[1024,512]{1,0:T(8,128)(2,1)S(1)} %convolution_convert_fusion.12), channel_id=1, source_target_pairs={{0,8},{24,16},{1,9},{25,17},{2,10},{26,18},{3,11},{27,19},{4,12},{... | collective-permute-start | bytes 3145736 | tf_op jit(solution)/shard_map/ppermute | solution.py:244
  455.7 39.3 %collective-permute-start.69 = (bf16[1024,512]{1,0:T(8,128)(2,1)}, bf16[1024,512]{1,0:T(8,128)(2,1)}, u32[]{:S(2)}, u32[]{:S(2)}) collective-permute-start(bf16[1024,512]{1,0:T(8,128)(2,1)} %add_convert_fusion.22), channel_id=1, source_target_pairs={{8,0},{16,24},{9,1},{17,25},{10,2},{18,26},{11,3},{19,27},{12,4},{... | collective-permute-start | bytes 3145736 | tf_op jit(solution)/shard_map/ppermute | solution.py:247
  459.6 36.1 %collective-permute-start.68 = (bf16[1024,512]{1,0:T(8,128)(2,1)}, bf16[1024,512]{1,0:T(8,128)(2,1)}, u32[]{:S(2)}, u32[]{:S(2)}) collective-permute-start(bf16[1024,512]{1,0:T(8,128)(2,1)} %add_convert_fusion.23), channel_id=1, source_target_pairs={{8,16},{16,8},{9,17},{17,9},{10,18},{18,10},{11,19},{19,11},{12,20... | collective-permute-start | bytes 3145736 | tf_op jit(solution)/shard_map/ppermute | solution.py:230
  461.3 42.4 %collective-permute-start.70 = (bf16[512,1024]{1,0:T(8,128)(2,1)}, bf16[512,1024]{1,0:T(8,128)(2,1)}, u32[]{:S(2)}, u32[]{:S(2)}) collective-permute-start(bf16[512,1024]{1,0:T(8,128)(2,1)} %convolution_convert_fusion.9), channel_id=1, source_target_pairs={{0,8},{24,16},{1,9},{25,17},{2,10},{26,18},{3,11},{27,19},{4,12},{... | collective-permute-start | bytes 3145736 | tf_op jit(solution)/shard_map/ppermute | solution.py:244
  479.6 24.0 %collective-permute-start.72 = (bf16[128,2048]{1,0:T(8,128)(2,1)S(1)}, bf16[128,2048]{1,0:T(8,128)(2,1)S(1)}, u32[]{:S(2)}, u32[]{:S(2)}) collective-permute-start(bf16[128,2048]{1,0:T(8,128)(2,1)S(1)} %get-tuple-element.183), channel_id=1, source_target_pairs={{0,1},{1,0},{2,3},{3,2},{4,5},{5,4},{6,7},{7,6},{8,9},{9,8},{10,11... | collective-permute-start | bytes 1572872 | tf_op jit(solution)/shard_map/ppermute | solution.py:74
  493.7 45.9 %collective-permute-start.66 = (bf16[1024,512]{1,0:T(8,128)(2,1)S(1)}, bf16[1024,512]{1,0:T(8,128)(2,1)S(1)}, u32[]{:S(2)}, u32[]{:S(2)}) collective-permute-start(bf16[1024,512]{1,0:T(8,128)(2,1)S(1)} %add_convert_fusion.24), channel_id=1, source_target_pairs={{8,0},{16,24},{9,1},{17,25},{10,2},{18,26},{11,3},{19,27},{12,4},{... | collective-permute-start | bytes 3145736 | tf_op jit(solution)/shard_map/ppermute | solution.py:247
  495.0 47.5 %collective-permute-start.65 = (bf16[1024,512]{1,0:T(8,128)(2,1)S(1)}, bf16[1024,512]{1,0:T(8,128)(2,1)S(1)}, u32[]{:S(2)}, u32[]{:S(2)}) collective-permute-start(bf16[1024,512]{1,0:T(8,128)(2,1)S(1)} %add_convert_fusion.25), channel_id=1, source_target_pairs={{8,16},{16,8},{9,17},{17,9},{10,18},{18,10},{11,19},{19,11},{12,20... | collective-permute-start | bytes 3145736 | tf_op jit(solution)/shard_map/ppermute | solution.py:230
  495.8 48.2 %collective-permute-start.67 = (bf16[512,1024]{1,0:T(8,128)(2,1)S(1)}, bf16[512,1024]{1,0:T(8,128)(2,1)}, u32[]{:S(2)}, u32[]{:S(2)}) collective-permute-start(bf16[512,1024]{1,0:T(8,128)(2,1)S(1)} %copy-done.31), channel_id=1, source_target_pairs={{0,8},{24,16},{1,9},{25,17},{2,10},{26,18},{3,11},{27,19},{4,12},{... | collective-permute-start | bytes 3145736 | tf_op jit(solution)/shard_map/ppermute | solution.py:244
  521.9 36.0 %collective-permute-start.84 = (bf16[1024,512]{1,0:T(8,128)(2,1)}, bf16[1024,512]{1,0:T(8,128)(2,1)}, u32[]{:S(2)}, u32[]{:S(2)}) collective-permute-start(bf16[1024,512]{1,0:T(8,128)(2,1)} %add_convert_fusion.18), channel_id=1, source_target_pairs={{8,0},{16,24},{9,1},{17,25},{10,2},{18,26},{11,3},{19,27},{12,4},{... | collective-permute-start | bytes 3145736 | tf_op jit(solution)/shard_map/ppermute | solution.py:247
  539.7 25.0 %collective-permute-start.85 = (bf16[512,1024]{1,0:T(8,128)(2,1)}, bf16[512,1024]{1,0:T(8,128)(2,1)}, u32[]{:S(2)}, u32[]{:S(2)}) collective-permute-start(bf16[512,1024]{1,0:T(8,128)(2,1)} %convolution_convert_fusion.7), channel_id=1, source_target_pairs={{0,8},{24,16},{1,9},{25,17},{2,10},{26,18},{3,11},{27,19},{4,12},{... | collective-permute-start | bytes 3145736 | tf_op jit(solution)/shard_map/ppermute | solution.py:244
  543.5 62.2 %collective-permute-start.82 = (bf16[1024,512]{1,0:T(8,128)(2,1)}, bf16[1024,512]{1,0:T(8,128)(2,1)}, u32[]{:S(2)}, u32[]{:S(2)}) collective-permute-start(bf16[1024,512]{1,0:T(8,128)(2,1)} %broadcast_select_fusion.11), channel_id=1, source_target_pairs={{0,4},{2,6},{4,0},{6,2},{1,5},{3,7},{5,1},{7,3},{8,12},{10,14},{12... | collective-permute-start | bytes 3145736 | tf_op jit(solution)/shard_map/ppermute | solution.py:72
  582.7 27.5 %collective-permute-start.80 = (bf16[1024,512]{1,0:T(8,128)(2,1)S(1)}, bf16[1024,512]{1,0:T(8,128)(2,1)S(1)}, u32[]{:S(2)}, u32[]{:S(2)}) collective-permute-start(bf16[1024,512]{1,0:T(8,128)(2,1)S(1)} %add_convert_fusion.20), channel_id=1, source_target_pairs={{8,0},{16,24},{9,1},{17,25},{10,2},{18,26},{11,3},{19,27},{12,4},{... | collective-permute-start | bytes 3145736 | tf_op jit(solution)/shard_map/ppermute | solution.py:247
  585.9 26.0 %collective-permute-start.79 = (bf16[512,1024]{1,0:T(8,128)(2,1)S(1)}, bf16[512,1024]{1,0:T(8,128)(2,1)S(1)}, u32[]{:S(2)}, u32[]{:S(2)}) collective-permute-start(bf16[512,1024]{1,0:T(8,128)(2,1)S(1)} %add_convert_fusion.21), channel_id=1, source_target_pairs={{8,16},{16,8},{9,17},{17,9},{10,18},{18,10},{11,19},{19,11},{12,20... | collective-permute-start | bytes 3145736 | tf_op jit(solution)/shard_map/ppermute | solution.py:230
  586.7 30.5 %collective-permute-start.81 = (bf16[512,1024]{1,0:T(8,128)(2,1)S(1)}, bf16[512,1024]{1,0:T(8,128)(2,1)S(1)}, u32[]{:S(2)}, u32[]{:S(2)}) collective-permute-start(bf16[512,1024]{1,0:T(8,128)(2,1)S(1)} %copy-done.29), channel_id=1, source_target_pairs={{0,8},{24,16},{1,9},{25,17},{2,10},{26,18},{3,11},{27,19},{4,12},{... | collective-permute-start | bytes 3145736 | tf_op jit(solution)/shard_map/ppermute | solution.py:244
  595.1 42.7 %collective-permute-start.88 = (bf16[1024,512]{1,0:T(8,128)(2,1)}, bf16[1024,512]{1,0:T(8,128)(2,1)}, u32[]{:S(2)}, u32[]{:S(2)}) collective-permute-start(bf16[1024,512]{1,0:T(8,128)(2,1)} %broadcast_select_fusion.10), channel_id=1, source_target_pairs={{0,6},{2,4},{4,2},{6,0},{1,7},{3,5},{5,3},{7,1},{8,14},{10,12},{12... | collective-permute-start | bytes 3145736 | tf_op jit(solution)/shard_map/ppermute | solution.py:72
  605.7 34.0 %collective-permute-start.87 = (bf16[512,1024]{1,0:T(8,128)(2,1)}, bf16[512,1024]{1,0:T(8,128)(2,1)}, u32[]{:S(2)}, u32[]{:S(2)}) collective-permute-start(bf16[512,1024]{1,0:T(8,128)(2,1)} %fusion.31), channel_id=1, source_target_pairs={{0,8},{8,0},{16,24},{24,16},{1,9},{9,1},{17,25},{25,17},{2,10},{10... | collective-permute-start | bytes 3145736 | tf_op jit(solution)/shard_map/ppermute | solution.py:240
  610.3 29.4 %collective-permute-start.86 = (bf16[512,1024]{1,0:T(8,128)(2,1)}, bf16[512,1024]{1,0:T(8,128)(2,1)}, u32[]{:S(2)}, u32[]{:S(2)}) collective-permute-start(bf16[512,1024]{1,0:T(8,128)(2,1)} %add_convert_fusion.17), channel_id=1, source_target_pairs={{8,16},{16,8},{9,17},{17,9},{10,18},{18,10},{11,19},{19,11},{12,20... | collective-permute-start | bytes 3145736 | tf_op jit(solution)/shard_map/ppermute | solution.py:230
  611.9 79.2 %collective-permute-start.94 = (bf16[1024,512]{1,0:T(8,128)(2,1)}, bf16[1024,512]{1,0:T(8,128)(2,1)}, u32[]{:S(2)}, u32[]{:S(2)}) collective-permute-start(bf16[1024,512]{1,0:T(8,128)(2,1)} %broadcast_select_fusion.9), channel_id=1, source_target_pairs={{0,2},{2,0},{4,6},{6,4},{1,3},{3,1},{5,7},{7,5},{8,10},{10,8},{12,... | collective-permute-start | bytes 3145736 | tf_op jit(solution)/shard_map/ppermute | solution.py:72
  631.9 60.7 %collective-permute-start.93 = (bf16[512,1024]{1,0:T(8,128)(2,1)}, bf16[512,1024]{1,0:T(8,128)(2,1)}, u32[]{:S(2)}, u32[]{:S(2)}) collective-permute-start(bf16[512,1024]{1,0:T(8,128)(2,1)} %fusion.32), channel_id=1, source_target_pairs={{0,8},{8,0},{16,24},{24,16},{1,9},{9,1},{17,25},{25,17},{2,10},{10... | collective-permute-start | bytes 3145736 | tf_op jit(solution)/shard_map/ppermute | solution.py:240
  637.8 54.8 %collective-permute-start.92 = (bf16[512,1024]{1,0:T(8,128)(2,1)}, bf16[512,1024]{1,0:T(8,128)(2,1)}, u32[]{:S(2)}, u32[]{:S(2)}) collective-permute-start(bf16[512,1024]{1,0:T(8,128)(2,1)} %add_convert_fusion.15), channel_id=1, source_target_pairs={{8,16},{16,8},{9,17},{17,9},{10,18},{18,10},{11,19},{19,11},{12,20... | collective-permute-start | bytes 3145736 | tf_op jit(solution)/shard_map/ppermute | solution.py:230
  660.9 61.3 %collective-permute-start.96 = (bf16[512,1024]{1,0:T(8,128)(2,1)}, bf16[512,1024]{1,0:T(8,128)(2,1)}, u32[]{:S(2)}, u32[]{:S(2)}) collective-permute-start(bf16[512,1024]{1,0:T(8,128)(2,1)} %fusion.33), channel_id=1, source_target_pairs={{0,8},{8,0},{16,24},{24,16},{1,9},{9,1},{17,25},{25,17},{2,10},{10... | collective-permute-start | bytes 3145736 | tf_op jit(solution)/shard_map/ppermute | solution.py:240
  662.4 23.8 %collective-permute-start.137 = (f32[9,1024]{1,0:T(8,128)S(1)}, f32[9,1024]{1,0:T(8,128)S(1)}, u32[]{:S(2)}, u32[]{:S(2)}) collective-permute-start(f32[9,1024]{1,0:T(8,128)S(1)} %add.685), channel_id=1, source_target_pairs={{0,8},{24,16},{1,9},{25,17},{2,10},{26,18},{3,11},{27,19},{4,12},{... | collective-permute-start | bytes 110600 | tf_op jit(solution)/shard_map/ppermute | solution.py:264
  689.4 33.5 %collective-permute-start.95 = (bf16[512,1024]{1,0:T(8,128)(2,1)}, bf16[512,1024]{1,0:T(8,128)(2,1)}, u32[]{:S(2)}, u32[]{:S(2)}) collective-permute-start(bf16[512,1024]{1,0:T(8,128)(2,1)} %add_convert_fusion.13), channel_id=1, source_target_pairs={{8,16},{16,8},{9,17},{17,9},{10,18},{18,10},{11,19},{19,11},{12,20... | collective-permute-start | bytes 3145736 | tf_op jit(solution)/shard_map/ppermute | solution.py:230
  695.9 27.1 %collective-permute-start.97 = (bf16[2,2,128,2048]{3,2,1,0:T(8,128)(2,1)}, bf16[2,2,128,2048]{3,2,1,0:T(8,128)(2,1)}, u32[]{:S(2)}, u32[]{:S(2)}) collective-permute-start(bf16[2,2,128,2048]{3,2,1,0:T(8,128)(2,1)} %fusion.22), channel_id=1, source_target_pairs={{0,2},{2,0},{4,6},{6,4},{1,3},{3,1},{5,7},{7,5},{8,10},{10,8},{12,... | collective-permute-start | bytes 6291464 | tf_op jit(solution)/shard_map/ppermute | solution.py:72
  698.3 35.5 %collective-permute-start.100 = (bf16[512,1024]{1,0:T(8,128)(2,1)}, bf16[512,1024]{1,0:T(8,128)(2,1)}, u32[]{:S(2)}, u32[]{:S(2)}) collective-permute-start(bf16[512,1024]{1,0:T(8,128)(2,1)} %broadcast_select_fusion.7), channel_id=1, source_target_pairs={{0,4},{2,6},{4,0},{6,2},{1,5},{3,7},{5,1},{7,3},{8,12},{10,14},{12... | collective-permute-start | bytes 3145736 | tf_op jit(solution)/shard_map/ppermute | solution.py:72
  714.6 27.9 %collective-permute-start.99 = (bf16[512,1024]{1,0:T(8,128)(2,1)S(1)}, bf16[512,1024]{1,0:T(8,128)(2,1)S(1)}, u32[]{:S(2)}, u32[]{:S(2)}) collective-permute-start(bf16[512,1024]{1,0:T(8,128)(2,1)S(1)} %fusion.34), channel_id=1, source_target_pairs={{0,8},{8,0},{16,24},{24,16},{1,9},{9,1},{17,25},{25,17},{2,10},{10... | collective-permute-start | bytes 3145736 | tf_op jit(solution)/shard_map/ppermute | solution.py:240
  727.2 25.7 %collective-permute-start.101 = (bf16[2,64,2048]{2,1,0:T(8,128)(2,1)S(1)}, bf16[2,64,2048]{2,1,0:T(8,128)(2,1)S(1)}, u32[]{:S(2)}, u32[]{:S(2)}) collective-permute-start(bf16[2,64,2048]{2,1,0:T(8,128)(2,1)S(1)} %pad_maximum_fusion.56), channel_id=1, source_target_pairs={{0,4},{2,6},{4,0},{6,2},{1,5},{3,7},{5,1},{7,3},{8,12},{10,14},{12... | collective-permute-start | bytes 1572872 | tf_op jit(solution)/shard_map/ppermute | solution.py:72
  733.8 42.2 %collective-permute-start.106 = (bf16[512,1024]{1,0:T(8,128)(2,1)S(1)}, bf16[512,1024]{1,0:T(8,128)(2,1)S(1)}, u32[]{:S(2)}, u32[]{:S(2)}) collective-permute-start(bf16[512,1024]{1,0:T(8,128)(2,1)S(1)} %broadcast_select_fusion.6), channel_id=1, source_target_pairs={{0,6},{2,4},{4,2},{6,0},{1,7},{3,5},{5,3},{7,1},{8,14},{10,12},{12... | collective-permute-start | bytes 3145736 | tf_op jit(solution)/shard_map/ppermute | solution.py:72
  742.5 34.8 %collective-permute-start.104 = (bf16[512,1024]{1,0:T(8,128)(2,1)S(1)}, bf16[512,1024]{1,0:T(8,128)(2,1)S(1)}, u32[]{:S(2)}, u32[]{:S(2)}) collective-permute-start(bf16[512,1024]{1,0:T(8,128)(2,1)S(1)} %add_convert_fusion.8), channel_id=1, source_target_pairs={{8,0},{16,24},{9,1},{17,25},{10,2},{18,26},{11,3},{19,27},{12,4},{... | collective-permute-start | bytes 3145736 | tf_op jit(solution)/shard_map/ppermute | solution.py:247
  743.8 34.2 %collective-permute-start.103 = (bf16[512,1024]{1,0:T(8,128)(2,1)S(1)}, bf16[512,1024]{1,0:T(8,128)(2,1)S(1)}, u32[]{:S(2)}, u32[]{:S(2)}) collective-permute-start(bf16[512,1024]{1,0:T(8,128)(2,1)S(1)} %add_convert_fusion.9), channel_id=1, source_target_pairs={{8,16},{16,8},{9,17},{17,9},{10,18},{18,10},{11,19},{19,11},{12,20... | collective-permute-start | bytes 3145736 | tf_op jit(solution)/shard_map/ppermute | solution.py:230
  744.6 40.2 %collective-permute-start.105 = (bf16[256,2048]{1,0:T(8,128)(2,1)S(1)}, bf16[256,2048]{1,0:T(8,128)(2,1)S(1)}, u32[]{:S(2)}, u32[]{:S(2)}) collective-permute-start(bf16[256,2048]{1,0:T(8,128)(2,1)S(1)} %copy-done.74), channel_id=1, source_target_pairs={{0,8},{24,16},{1,9},{25,17},{2,10},{26,18},{3,11},{27,19},{4,12},{... | collective-permute-start | bytes 3145736 | tf_op jit(solution)/shard_map/ppermute | solution.py:244
  776.0 30.1 %collective-permute-start.110 = (bf16[512,1024]{1,0:T(8,128)(2,1)S(1)}, bf16[512,1024]{1,0:T(8,128)(2,1)S(1)}, u32[]{:S(2)}, u32[]{:S(2)}) collective-permute-start(bf16[512,1024]{1,0:T(8,128)(2,1)S(1)} %add_convert_fusion.6), channel_id=1, source_target_pairs={{8,0},{16,24},{9,1},{17,25},{10,2},{18,26},{11,3},{19,27},{12,4},{... | collective-permute-start | bytes 3145736 | tf_op jit(solution)/shard_map/ppermute | solution.py:247
  777.3 30.4 %collective-permute-start.109 = (bf16[512,1024]{1,0:T(8,128)(2,1)S(1)}, bf16[512,1024]{1,0:T(8,128)(2,1)S(1)}, u32[]{:S(2)}, u32[]{:S(2)}) collective-permute-start(bf16[512,1024]{1,0:T(8,128)(2,1)S(1)} %add_convert_fusion.7), channel_id=1, source_target_pairs={{8,16},{16,8},{9,17},{17,9},{10,18},{18,10},{11,19},{19,11},{12,20... | collective-permute-start | bytes 3145736 | tf_op jit(solution)/shard_map/ppermute | solution.py:230
  785.2 41.1 %collective-permute-start.114 = (bf16[512,1024]{1,0:T(8,128)(2,1)S(1)}, bf16[512,1024]{1,0:T(8,128)(2,1)S(1)}, u32[]{:S(2)}, u32[]{:S(2)}) collective-permute-start(bf16[512,1024]{1,0:T(8,128)(2,1)S(1)} %add_convert_fusion.4), channel_id=1, source_target_pairs={{8,0},{16,24},{9,1},{17,25},{10,2},{18,26},{11,3},{19,27},{12,4},{... | collective-permute-start | bytes 3145736 | tf_op jit(solution)/shard_map/ppermute | solution.py:247
  787.2 40.6 %collective-permute-start.113 = (bf16[256,2048]{1,0:T(8,128)(2,1)S(1)}, bf16[256,2048]{1,0:T(8,128)(2,1)S(1)}, u32[]{:S(2)}, u32[]{:S(2)}) collective-permute-start(bf16[256,2048]{1,0:T(8,128)(2,1)S(1)} %add_convert_fusion.5), channel_id=1, source_target_pairs={{8,16},{16,8},{9,17},{17,9},{10,18},{18,10},{11,19},{19,11},{12,20... | collective-permute-start | bytes 3145736 | tf_op jit(solution)/shard_map/ppermute | solution.py:230
  806.1 49.5 %collective-permute-start.141 = (bf16[512,1024]{1,0:T(8,128)(2,1)S(1)}, bf16[512,1024]{1,0:T(8,128)(2,1)S(1)}, u32[]{:S(2)}, u32[]{:S(2)}) collective-permute-start(bf16[512,1024]{1,0:T(8,128)(2,1)S(1)} %broadcast_select_fusion.2), channel_id=1, source_target_pairs={{0,4},{2,6},{4,0},{6,2},{1,5},{3,7},{5,1},{7,3},{8,12},{10,14},{12... | collective-permute-start | bytes 3145736 | tf_op jit(solution)/shard_map/ppermute | solution.py:72
  808.1 65.7 %collective-permute-start.143 = (bf16[512,1024]{1,0:T(8,128)(2,1)S(1)}, bf16[512,1024]{1,0:T(8,128)(2,1)S(1)}, u32[]{:S(2)}, u32[]{:S(2)}) collective-permute-start(bf16[512,1024]{1,0:T(8,128)(2,1)S(1)} %add_convert_fusion.2), channel_id=1, source_target_pairs={{8,0},{16,24},{9,1},{17,25},{10,2},{18,26},{11,3},{19,27},{12,4},{... | collective-permute-start | bytes 3145736 | tf_op jit(solution)/shard_map/ppermute | solution.py:247
  822.1 30.5 %collective-permute-start.140 = (bf16[512,1024]{1,0:T(8,128)(2,1)S(1)}, bf16[512,1024]{1,0:T(8,128)(2,1)S(1)}, u32[]{:S(2)}, u32[]{:S(2)}) collective-permute-start(bf16[512,1024]{1,0:T(8,128)(2,1)S(1)} %broadcast_select_fusion.3), channel_id=1, source_target_pairs={{0,6},{2,4},{4,2},{6,0},{1,7},{3,5},{5,3},{7,1},{8,14},{10,12},{12... | collective-permute-start | bytes 3145736 | tf_op jit(solution)/shard_map/ppermute | solution.py:72
  845.0 26.6 %collective-permute-start.130 = (bf16[256,2048]{1,0:T(8,128)(2,1)S(1)}, bf16[256,2048]{1,0:T(8,128)(2,1)S(1)}, u32[]{:S(2)}, u32[]{:S(2)}) collective-permute-start(bf16[256,2048]{1,0:T(8,128)(2,1)S(1)} %add_convert_fusion.3), channel_id=1, source_target_pairs={{8,0},{16,24},{9,1},{17,25},{10,2},{18,26},{11,3},{19,27},{12,4},{... | collective-permute-start | bytes 3145736 | tf_op jit(solution)/shard_map/ppermute | solution.py:247
  867.9 25.9 %collective-permute-start.121 = (bf16[512,768]{1,0:T(8,128)(2,1)S(1)}, bf16[512,768]{1,0:T(8,128)(2,1)S(1)}, u32[]{:S(2)}, u32[]{:S(2)}) collective-permute-start(bf16[512,768]{1,0:T(8,128)(2,1)S(1)} %add_convert_fusion.32), channel_id=1, source_target_pairs={{8,0},{16,24},{9,1},{17,25},{10,2},{18,26},{11,3},{19,27},{12,4},{... | collective-permute-start | bytes 2359304 | tf_op jit(solution)/shard_map/ppermute | solution.py:247
  869.4 46.6 %collective-permute-start.128 = (bf16[512,768]{1,0:T(8,128)(2,1)S(1)}, bf16[512,768]{1,0:T(8,128)(2,1)S(1)}, u32[]{:S(2)}, u32[]{:S(2)}) collective-permute-start(bf16[512,768]{1,0:T(8,128)(2,1)S(1)} %add_convert_fusion.29), channel_id=1, source_target_pairs={{8,16},{16,8},{9,17},{17,9},{10,18},{18,10},{11,19},{19,11},{12,20... | collective-permute-start | bytes 2359304 | tf_op jit(solution)/shard_map/ppermute | solution.py:230
  871.6 44.2 %collective-permute-start.118 = (bf16[512,768]{1,0:T(8,128)(2,1)S(1)}, bf16[512,768]{1,0:T(8,128)(2,1)S(1)}, u32[]{:S(2)}, u32[]{:S(2)}) collective-permute-start(bf16[512,768]{1,0:T(8,128)(2,1)S(1)} %add_convert_fusion.34), channel_id=1, source_target_pairs={{8,0},{16,24},{9,1},{17,25},{10,2},{18,26},{11,3},{19,27},{12,4},{... | collective-permute-start | bytes 2359304 | tf_op jit(solution)/shard_map/ppermute | solution.py:247
  894.0 38.7 %collective-permute-start.125 = (bf16[512,768]{1,0:T(8,128)(2,1)S(1)}, bf16[512,768]{1,0:T(8,128)(2,1)S(1)}, u32[]{:S(2)}, u32[]{:S(2)}) collective-permute-start(bf16[512,768]{1,0:T(8,128)(2,1)S(1)} %add_convert_fusion.30), channel_id=1, source_target_pairs={{8,0},{16,24},{9,1},{17,25},{10,2},{18,26},{11,3},{19,27},{12,4},{... | collective-permute-start | bytes 2359304 | tf_op jit(solution)/shard_map/ppermute | solution.py:247
  895.6 40.0 %collective-permute-start.122 = (bf16[512,768]{1,0:T(8,128)(2,1)S(1)}, bf16[512,768]{1,0:T(8,128)(2,1)S(1)}, u32[]{:S(2)}, u32[]{:S(2)}) collective-permute-start(bf16[512,768]{1,0:T(8,128)(2,1)S(1)} %broadcast_select_fusion.14), channel_id=1, source_target_pairs={{0,4},{2,6},{4,0},{6,2},{1,5},{3,7},{5,1},{7,3},{8,12},{10,14},{12... | collective-permute-start | bytes 2359304 | tf_op jit(solution)/shard_map/ppermute | solution.py:72
  916.3 31.2 %collective-permute-start.129 = (bf16[512,768]{1,0:T(8,128)(2,1)S(1)}, bf16[512,768]{1,0:T(8,128)(2,1)S(1)}, u32[]{:S(2)}, u32[]{:S(2)}) collective-permute-start(bf16[512,768]{1,0:T(8,128)(2,1)S(1)} %add_convert_fusion.28), channel_id=1, source_target_pairs={{8,0},{16,24},{9,1},{17,25},{10,2},{18,26},{11,3},{19,27},{12,4},{... | collective-permute-start | bytes 2359304 | tf_op jit(solution)/shard_map/ppermute | solution.py:247
  (250 other events, 2249.9 us)
Sparse Core Ops, SparseCore 0:
  39.0 47.7 all-gather.3
  126.3 44.6 all-gather.5
  186.8 44.9 all-gather.7

commit v3 on v2

--- a/solution.py
+++ b/solution.py
@@ -195,10 +195,10 @@
     depth = 2
 
     def __init__(self, move):
+        self.move = move
         self.line = lax.axis_size("dp") == 4
         place = lax.axis_index("dp")
         self.inner = (place == 1) | (place == 2)
-        self.move = move
         self.arrays, self.pairs, self.full, self.placed = [], [], [], []
         self.pending = [{}] * self.depth
         self.moving = [[]] * (self.depth + 1)
@@ -209,8 +209,8 @@
             if array is not None:
                 self.arrays.append(array)
             return values
-        pending, moving, array, values = lax.optimization_barrier(
-            (self.pending.pop(0), self.moving.pop(0), array, values)
+        pending, moving, array, values = together(
+            self.pending.pop(0), self.moving.pop(0), array, values
         )
         self.advance(pending, moving, array)
         return values
@@ -256,16 +256,6 @@
         return self.placed
 
 
-def group_total(vector):
-    if lax.axis_size("dp") != 4:
-        return lax.psum(vector, "dp")
-    place = lax.axis_index("dp")
-    inner = (place == 1) | (place == 2)
-    vector = vector + lax.ppermute(vector, "dp", [(0, 1), (3, 2)])
-    vector = vector + lax.ppermute(vector, "dp", MIDDLE)
-    return jnp.where(inner, vector, lax.ppermute(vector, "dp", [(1, 0), (2, 3)]))
-
-
 def shards(
     layer_input,
     cotangent,
@@ -358,13 +348,11 @@
     trios = [plane.hop(trio, k) for k, trio in enumerate(trios)]
     gate_far, trios, inputs_all = together(gate_far, trios, inputs_all)
     up_pieces, up_far = shared(up_weight, 1)
-    down_pieces, down_far = shared(down_weight, 0)
+    down_pieces = pieces_of(down_weight, 0)
     w_query, w_key, w_value = (
         jnp.concatenate([trio[k] for trio in trios], axis=0) for k in range(3)
     )
-    w_out = jnp.concatenate(
-        [plane.hop(piece, k) for k, piece in enumerate(pieces_of(out_weight, 0))], axis=1
-    )
+    out_pieces = [plane.hop(piece, k) for k, piece in enumerate(pieces_of(out_weight, 0))]
     gains = jnp.stack([attn_gain, mlp_gain])
     gains = jnp.concatenate([plane.hop(gains, k) for k in range(rows)], axis=1).astype(F32)
     attn_gain_f, mlp_gain_f = gains[0:1], gains[1:2]
@@ -423,7 +411,13 @@
     q_rot = rotate_pairs(heads_of(q_unit * q_gain_f), cos_table, sin_table).astype(BF)
     k_rot = rotate_pairs(heads_of(k_unit * k_gain_f), cos_table, sin_table).astype(BF)
     values = heads_of(value_low)
-    up_far, q_rot = together(up_far, q_rot)
+    down_half = rows // 2
+    out_pieces, down_pieces = together(out_pieces, down_pieces)
+    down_pieces = [plane.hop(piece, k) for k, piece in enumerate(down_pieces)]
+    up_far, down_pieces[: down_half + 1], q_rot = together(
+        up_far, down_pieces[: down_half + 1], q_rot
+    )
+    w_out = jnp.concatenate(out_pieces, axis=1)
     up_far = over_groups(up_far)
     allowed = (places[None, None, :] <= places[None, :, None]) & (
         places[None, None, :] < live_len[:, None, None]
@@ -439,13 +433,11 @@
     attn_mix = joined(
         jnp.einsum("shqk,skhd->sqhd", prob_low, values, preferred_element_type=F32).astype(BF)
     )
-    up_far, down_far, attn_mix = together(up_far, down_far, attn_mix)
-    down_far = over_groups(down_far)
+    up_far, down_pieces, attn_mix = together(up_far, down_pieces, attn_mix)
     attn_raw = plane.scatter(dot(attn_mix, w_out).astype(BF))
-    down_far, attn_raw = together(down_far, attn_raw)
     w_gate = whole(gate_pieces, gate_far, 0)
     w_up = whole(up_pieces, up_far, 0)
-    w_down = whole(down_pieces, down_far, 1)
+    w_down = jnp.concatenate(down_pieces, axis=1)
     a_scale = rms_scale(attn_raw)
     a_unit = attn_raw * a_scale
     branch_a = a_unit * attn_gain_f
@@ -465,35 +457,43 @@
     d_m_unit = d_full * mlp_gain_f
     d_mlp = m_scale * (d_m_unit - m_unit * jnp.mean(d_m_unit * m_unit, axis=-1, keepdims=True))
     d_mlp_all = plane.gather(d_mlp.astype(BF))
-    order = [k for k in range(2, rows)] + [1, 0]
+    order = list(range(rows // 2, rows)) + list(range(rows // 2))
+    near, far = slice(0, width // 2), slice(width // 2, width)
+    low, high = slice(0, ff_part // 2), slice(ff_part // 2, ff_part)
     waiting = []
 
     def move(index, total):
-        if index < 3 * rows:
-            return plane.hop(total, order[index % rows])
-        if index == 3 * rows:
-            return [plane.hop(plane.slot(total, k), k) for k in order]
-        return plane.hop(total, order[(index - 3 * rows - 1) % rows])
+        if index < 4:
+            first = rows // 2 if index < 2 else 0
+            blocks = jnp.split(total, rows // 2, axis=1)
+            return [plane.hop(block, first + k) for k, block in enumerate(blocks)]
+        if index == 3 + 3 * rows:
+            return plane.hop(total[:part], order[-1]), total[part:]
+        return plane.hop(total, order[index % rows])
 
     line = Line(move)
+
+    def outer(left_side, right_side):
+        return against(left_side, right_side).astype(BF)
 
     def step(values):
         return line.step(values, waiting.pop(0) if waiting else None)
 
-    waiting += [against(inner_low, plane.slot(d_mlp_all, k)).astype(BF) for k in order]
+    waiting += [outer(inner_low[:, low], d_mlp_all[:, far])]
     d_mlp_all = step(d_mlp_all)
+    waiting += [outer(inner_low[:, high], d_mlp_all[:, far])]
+    waiting += [outer(inner_low[:, half], d_mlp_all[:, near]) for half in (low, high)]
     d_inner = through(d_mlp_all, w_down)
     d_gate_low = (d_inner * up_pre * (gate_sig * (1.0 + gate_pre * (1.0 - gate_sig)))).astype(BF)
     d_up_low = (d_inner * gate_act).astype(BF)
     d_gate_low, d_up_low = step((d_gate_low, d_up_low))
-    waiting += [against(plane.slot(hidden_all, k), d_gate_low).astype(BF) for k in order]
-    waiting += [against(plane.slot(hidden_all, k), d_up_low).astype(BF) for k in order]
+    waiting += [outer(plane.slot(hidden_all, k), d_gate_low) for k in order]
+    waiting += [outer(plane.slot(hidden_all, k), d_up_low) for k in order]
     partial = step((through(d_gate_low, w_gate) + through(d_up_low, w_up)).astype(BF))
     d_hidden = d_full + plane.scatter(partial, step)
     d_a_unit = d_hidden * attn_gain_f
     d_attn = a_scale * (d_a_unit - a_unit * jnp.mean(d_a_unit * a_unit, axis=-1, keepdims=True))
     d_attn_all = plane.gather(d_attn.astype(BF), step)
-    waiting += [against(attn_mix, d_attn_all).astype(BF)]
     d_mix = heads_of(through(d_attn_all, w_out).astype(BF))
     d_prob = jnp.einsum("sqhd,skhd->shqk", d_mix, values, preferred_element_type=F32)
     row_delta = jnp.sum(prob * d_prob, axis=-1, keepdims=True)
@@ -520,13 +520,73 @@
     d_query = d_query.astype(BF)
     d_key = d_key.astype(BF)
     d_qkv = jnp.concatenate([d_query, d_key, d_value], axis=1)
-    waiting += [against(plane.slot(inputs_all, k), d_qkv).astype(BF) for k in order]
+    waiting += [
+        jnp.concatenate(
+            [
+                outer(plane.slot(inputs_all, k), d_qkv),
+                outer(plane.slot(d_attn_all, k), attn_mix),
+            ],
+            axis=1,
+        )
+        for k in order
+    ]
     partial = step(
         (through(d_query, w_query) + through(d_key, w_key) + through(d_value, w_value)).astype(BF)
     )
-    d_inputs = d_hidden + plane.scatter(partial, step)
-    while waiting:
-        d_inputs = step(d_inputs)
+    d_inputs = d_hidden + plane.scatter(partial)
+    while len(waiting) > 1:
+        step(())
+    line.placed, d_inputs, result_late = together(line.placed, d_inputs, result)
+
+    def home(array):
+        own = plane.relative((array).astype(BF)).reshape(seq_own, tok_seq, width)
+        pieces = [own] + [plane.hop(own, 0, k) for k in range(1, cols)]
+        out = jnp.zeros((seq_grp, tok_seq, width), BF)
+        for k in range(cols):
+            out = lax.dynamic_update_slice_in_dim(out, pieces[k], (col ^ k) * seq_own, axis=0)
+        return out
+
+    output = home(result_late)
+    grad_input = home(d_inputs * valid_rows)
+
+    def sums_of(array):
+        return jnp.sum(array.reshape(seq_own, tok_seq * width), axis=1)
+
+    own_sums = jnp.stack(
+        [
+            sums_of(result * result),
+            sums_of(branch_a * branch_a * valid_rows),
+            sums_of(branch_m * branch_m * valid_rows),
+        ],
+        axis=1,
+    )
+    own_ids = my_group * seq_grp + first_own + jnp.arange(seq_own, dtype=jnp.int32)
+    seq_sums = jnp.sum(
+        jnp.where(
+            own_ids[:, None, None] == jnp.arange(seq_count, dtype=jnp.int32)[None, :, None],
+            own_sums[:, None, :],
+            0.0,
+        ),
+        axis=0,
+    )
+    gain_sums = plane.relative(
+        jnp.stack([jnp.sum(d_hidden * a_unit, axis=0), jnp.sum(d_full * m_unit, axis=0)])
+    )
+    head_sums = jnp.stack([jnp.sum(d_qn * q_unit, axis=0), jnp.sum(d_kn * k_unit, axis=0)])
+    mine = (
+        (jnp.arange(cols)[:, None] == col) & (jnp.arange(rows)[None, :] == row)
+    ).astype(F32)
+    head_sums = (head_sums[:, None, None, :] * mine[None, :, :, None]).reshape(2, cols, heads_cols)
+    vector = jnp.concatenate([gain_sums.reshape(-1), head_sums.reshape(-1), seq_sums.reshape(-1)])
+    vector = jnp.pad(vector, (0, -vector.shape[0] % (ff_part * 16))).reshape(-1, ff_part)
+    row_xor = 1
+    while row_xor < rows:
+        vector = vector + plane.hop(vector, row_xor)
+        row_xor *= 2
+    col_xor = 1
+    while col_xor < cols:
+        vector = vector + plane.hop(vector, 0, col_xor)
+        col_xor *= 2
 
     def finish(blocks, axis):
         size = blocks[0].shape[axis]
@@ -539,71 +599,26 @@
             out = lax.dynamic_update_slice(out, blocks[k].astype(F32), start)
         return out
 
-    line.placed, d_inputs = lax.optimization_barrier((line.placed, d_inputs))
+    def arrived_at(placed):
+        return [placed[order.index(k)] for k in range(rows)]
+
+    line.step((), jnp.concatenate([waiting.pop(0), vector.astype(BF)], axis=0))
     placed = line.finish()
-
-    def arrived_at(blocks):
-        return [blocks[order.index(k)] for k in range(rows)]
-
-    grad_down = finish(arrived_at(placed[:rows]), 0)
-    grad_gate = finish(arrived_at(placed[rows : 2 * rows]), 1)
-    grad_up = finish(arrived_at(placed[2 * rows : 3 * rows]), 1)
-    grad_out = finish(arrived_at(placed[3 * rows]), 0)
-    qkv_blocks = arrived_at(placed[3 * rows + 1 :])
-    grad_query = finish([b[:, :head_part] for b in qkv_blocks], 1)
-    grad_key = finish([b[:, head_part : 2 * head_part] for b in qkv_blocks], 1)
-    grad_value = finish([b[:, 2 * head_part :] for b in qkv_blocks], 1)
-
-    def home(array):
-        own = plane.relative((array).astype(BF)).reshape(seq_own, tok_seq, width)
-        pieces = [own] + [plane.hop(own, 0, k) for k in range(1, cols)]
-        out = jnp.zeros((seq_grp, tok_seq, width), BF)
-        for k in range(cols):
-            out = lax.dynamic_update_slice_in_dim(out, pieces[k], (col ^ k) * seq_own, axis=0)
-        return out
-
-    output = home(result)
-    grad_input = home(d_inputs * valid_rows)
-
-    def sums_of(array):
-        return jnp.sum(array.reshape(seq_own, tok_seq * width), axis=1)
-
-    own_sums = jnp.stack(
-        [
-            sums_of(result * result),
-            sums_of(branch_a * branch_a * valid_rows),
-            sums_of(branch_m * branch_m * valid_rows),
-        ],
-        axis=1,
-    )
-    own_ids = my_group * seq_grp + first_own + jnp.arange(seq_own, dtype=jnp.int32)
-    seq_sums = jnp.sum(
-        jnp.where(
-            own_ids[:, None, None] == jnp.arange(seq_count, dtype=jnp.int32)[None, :, None],
-            own_sums[:, None, :],
-            0.0,
-        ),
-        axis=0,
-    )
-    gain_sums = plane.relative(
-        jnp.stack([jnp.sum(d_hidden * a_unit, axis=0), jnp.sum(d_full * m_unit, axis=0)])
-    )
-    head_sums = jnp.stack([jnp.sum(d_qn * q_unit, axis=0), jnp.sum(d_kn * k_unit, axis=0)])
-    mine = (
-        (jnp.arange(cols)[:, None] == col) & (jnp.arange(rows)[None, :] == row)
-    ).astype(F32)
-    head_sums = (head_sums[:, None, None, :] * mine[None, :, :, None]).reshape(2, cols, heads_cols)
-    vector = jnp.concatenate([gain_sums.reshape(-1), head_sums.reshape(-1), seq_sums.reshape(-1)])
-    vector = jnp.pad(vector, (0, -vector.shape[0] % 1024)).reshape(-1, 1024)
-    row_xor = 1
-    while row_xor < rows:
-        vector = vector + plane.hop(vector, row_xor)
-        row_xor *= 2
-    col_xor = 1
-    while col_xor < cols:
-        vector = vector + plane.hop(vector, 0, col_xor)
-        col_xor *= 2
-    vector = group_total(vector).reshape(-1)
+    placed[-1], vector = placed[-1]
+    vector = vector.astype(F32).reshape(-1)
+    grad_down = [placed[2] + placed[0], placed[3] + placed[1]]
+    grad_down = finish([jnp.concatenate(both, axis=0) for both in zip(*grad_down, strict=True)], 0)
+    grad_gate = finish(arrived_at(placed[4 : 4 + rows]), 1)
+    grad_up = finish(arrived_at(placed[4 + rows : 4 + 2 * rows]), 1)
+    attn_blocks = arrived_at(placed[4 + 2 * rows :])
+    grad_query, grad_key, grad_value, grad_out = (
+        [block[:, k * head_part : (k + 1) * head_part] for block in attn_blocks] for k in range(4)
+    )
+    grad_query, grad_key, grad_value = (
+        finish(blocks, 1) for blocks in (grad_query, grad_key, grad_value)
+    )
+    grad_out = finish([block.T for block in grad_out], 0)
+
     gain_sums = lax.dynamic_slice_in_dim(
         vector[: 2 * width].reshape(2, width), row * part, part, axis=1
     )

time: 964 us -> 933 us (0.968)
  starting transfers between devices: 196 us -> 170 us
  waiting for transfers between devices: 367 us -> 344 us
  local copies, waits for them, and re-layouts: 117 us -> 132 us
  other arithmetic: 137 us -> 147 us
    ppermute x4 -> x11, waiting for transfers between devices: 8.89 us -> 62.8 us  [advance(): current['inward'] = lax.ppermute(sent, 'dp', ENDS)]
    ppermute x13 -> x5, starting transfers between devices: 80.7 us -> 32.1 us  [advance(): current['inward'] = lax.ppermute(array, 'dp', [(0, 1), (3, 2)])]
    ppermute x74, waiting for transfers between devices: 78.2 us -> 120 us  [hop(): lax.ppermute(array, 'row', [(a, a ^ row_xor) for a in range(self.rows)])]
    ppermute x13 -> x5, waiting for transfers between devices: 75.2 us -> 37.8 us  [advance(): current['back'] = lax.ppermute(back, 'dp', [(1, 0), (2, 3)])]
    ppermute x13 -> x5, waiting for transfers between devices: 48.2 us -> 15 us  [advance(): current['inward'] = lax.ppermute(array, 'dp', [(0, 1), (3, 2)])]
    ppermute x4 -> x11, starting transfers between devices: 8.4 us -> 40.7 us  [advance(): current['inward'] = lax.ppermute(sent, 'dp', ENDS)]
    ppermute x3 -> x0, waiting for transfers between devices: 18 us -> none  [the longest x1 15.6 us: group_total(): vector = vector + lax.ppermute(vector, 'dp', [(0, 1), (3, 2)])]
    ppermute x20, waiting for transfers between devices: 100 us -> 83 us  [hop(): lax.ppermute(array, 'col', [(a, a ^ col_xor) for a in range(self.cols)])]
  transfers between devices with their start and end apart: 147 -> 133, of which waited for: 60 -> 53; matrix products, arithmetic and copies ran while one was open for 30% -> 33% of each run, Pallas kernels for 0% -> 0%
where the time goes in v3:
time: 933 us; the launch traced here: 927 us
  waiting for transfers between devices  344 us (37%)
  starting transfers between devices  170 us (18%)
  other arithmetic  147 us (16%)
  local copies, waits for them, and re-layouts  132 us (14%)
  matrix products  116 us (12%)
  between operations  18.4 us (2%)
    ppermute x74, waiting for transfers between devices, hop(): lax.ppermute(array, 'row', [(a, a ^ row_xor) for a in range(self.rows)])  120 us
    ppermute x20, waiting for transfers between devices, hop(): lax.ppermute(array, 'col', [(a, a ^ col_xor) for a in range(self.cols)])  83 us
    ppermute x11, waiting for transfers between devices, advance(): current['inward'] = lax.ppermute(sent, 'dp', ENDS)  62.8 us
    unnamed x416, local copies, waits for them, and re-layouts  59.7 us
    ppermute x74, starting transfers between devices, hop(): lax.ppermute(array, 'row', [(a, a ^ row_xor) for a in range(self.rows)])  49 us
    ppermute x11, starting transfers between devices, advance(): current['inward'] = lax.ppermute(sent, 'dp', ENDS)  40.7 us
    dot_general x7, matrix products, through(): lax.dot_general(left_side, weight, (((1,), (1,)), ((), ())), preferred_el...  40.1 us
    dot_general x20, matrix products, against(): lax.dot_general(left_side, right_side, (((0,), (0,)), ((), ())), preferre...  38.7 us
  transfers between devices with their start and end apart: 133, of which 53 were waited for; matrix products, arithmetic and copies ran while one was open for 33% of the time, Pallas kernels for 0%

profile of v3, /device:TPU:0, one launch (start us, length us, event | category | flops | bytes accessed | tf_op | source)
XLA Modules:
  0.0 926.6 jit_solution(6092882698760356672)
XLA Ops:
  11.6 2.9 collective-permute-start.13
  28.2 5.0 collective-permute-done.7
  33.2 4.1 collective-permute-done.8
  52.2 5.9 collective-permute-done.16
  68.1 10.9 %collective-permute-done.11 = bf16[3,512,256]{2,1,0:T(8,128)(2,1)} collective-permute-done((bf16[3,512,256]{2,1,0:T(8,128)(2,1)}, bf16[3,512,256]{2,1,0:T(8,128)(2,1)}, u32[]{:S(2)}, u32[]{:S(2)}) %collective-permute-start.11) | collective-permute-done | bytes 786464 | tf_op jit(solution)/shard_map/ppermute | solution.py:72
  79.0 8.0 all-gather.3.cloned.1.call-done
  106.5 4.8 collective-permute-done.1
  129.2 2.9 subtract_convert_fusion
  140.8 4.9 convolution_convert_fusion.17
  146.9 3.9 fusion.231
  150.8 2.7 fusion.48
  154.1 6.4 collective-permute-done.21
  160.5 17.3 %all-gather.5.cloned.1.call-done = bf16[512,2048]{1,0:T(8,128)(2,1)} async-done(((bf16[128,2048]{1,0:T(8,128)(2,1)}), bf16[512,2048]{1,0:T(8,128)(2,1)}) %all-gather.5.cloned.1.call-update) | async-done | bytes 2097168 | tf_op jit(solution)/shard_map/all_gather | solution.py:334
  188.6 11.4 %collective-permute-done.25 = bf16[2,64,2048]{2,1,0:T(8,128)(2,1)S(1)} collective-permute-done((bf16[2,64,2048]{2,1,0:T(8,128)(2,1)S(1)}, bf16[2,64,2048]{2,1,0:T(8,128)(2,1)S(1)}, u32[]{:S(2)}, u32[]{:S(2)}) %collective-permute-start.25) | collective-permute-done | bytes 524320 | tf_op jit(solution)/shard_map/ppermute | solution.py:74
  204.9 2.8 collective-permute-done.26
  213.3 9.1 collective-permute-done.33
  228.0 7.5 collective-permute-done.35
  239.1 4.5 fusion.96
  243.7 6.6 multiply_convert_fusion.3
  250.3 4.8 convolution_convert_fusion.1
  263.2 5.1 fusion.176
  273.1 11.7 %collective-permute-done.43 = bf16[2,64,2048]{2,1,0:T(8,128)(2,1)} collective-permute-done((bf16[2,64,2048]{2,1,0:T(8,128)(2,1)}, bf16[2,64,2048]{2,1,0:T(8,128)(2,1)}, u32[]{:S(2)}, u32[]{:S(2)}) %collective-permute-start.43) | collective-permute-done | bytes 524320 | tf_op jit(solution)/shard_map/ppermute | solution.py:74
  291.5 3.1 collective-permute-done.44
  302.7 10.6 %collective-permute-done.48 = bf16[128,2048]{1,0:T(8,128)(2,1)S(1)} collective-permute-done((bf16[128,2048]{1,0:T(8,128)(2,1)S(1)}, bf16[128,2048]{1,0:T(8,128)(2,1)S(1)}, u32[]{:S(2)}, u32[]{:S(2)}) %collective-permute-start.48) | collective-permute-done | bytes 524320 | tf_op jit(solution)/shard_map/ppermute | solution.py:74
  317.8 6.2 collective-permute-done.50
  332.6 4.0 fusion.43
  341.1 10.2 %multiply_convert_fusion.1 = (bf16[1024,1024]{1,0:T(8,128)(2,1)S(1)}, bf16[1024,1024]{1,0:T(8,128)(2,1)S(1)}) fusion(f32[1024,1024]{1,0:T(8,128)} %copy-done.183, f32[1024,1024]{1,0:T(8,128)} %get-tuple-element.612, bf16[1024,2048]{1,0:T(8,128)(2,1)} %constant_dynamic-update-slice_fusion.29, bf16[1024,2048]{1,0:T(8,128)(2,1)S(1)} %copy-done.135), kind=kOutput, calls=%fused_computation.18 | convolution fusion | flops 4308598784 | bytes 20971520 | tf_op jit(solution)/shard_map/dot_general | solution.py:42
  356.2 3.1 collective-permute-start.54
  361.7 9.6 %fusion.94 = f32[1024,2048]{1,0:T(8,128)} fusion(bf16[1024,1024]{1,0:T(8,128)(2,1)S(1)} %get-tuple-element.180, bf16[512,1024]{1,0:T(8,128)(2,1)S(1)} %copy-done.124, bf16[512,1024]{1,0:T(8,128)(2,1)S(1)} %copy-done.122, bf16[512,1024]{1,0:T(8,128)(2,1)S(1)} %copy-done.174, bf16[512,1024]{1,0:T(8,128)(2,1)S(1)} %copy-done.85), kind=kOutput, calls=%fused_computation.289 | convolution fusion | flops 4311744512 | bytes 14680064 | tf_op jit(solution)/shard_map/dot_general | solution.py:42
  371.2 10.9 %add_convert_fusion.1 = bf16[1024,2048]{1,0:T(8,128)(2,1)} fusion(f32[1024,2048]{1,0:T(8,128)} %fusion.94, bf16[1024,1024]{1,0:T(8,128)(2,1)S(1)} %get-tuple-element.179, bf16[512,1024]{1,0:T(8,128)(2,1)} %copy-done.120, bf16[512,1024]{1,0:T(8,128)(2,1)} %copy-done.119, bf16[512,1024]{1,0:T(8,128)(2,1)} %copy-done.172, bf16[512,1024]{1,0:T(8,128)(2,1)S(1)} %copy-done.83), kind=kOutput, calls=%fused_computation.3 | convolution fusion | flops 4315938816 | bytes 18874368 | tf_op jit(solution)/shard_map/dot_general | solution.py:42
  398.0 7.3 collective-permute-start.59
  414.1 15.5 %collective-permute-start.57 = (bf16[512,1024]{1,0:T(8,128)(2,1)S(1)}, bf16[512,1024]{1,0:T(8,128)(2,1)S(1)}, u32[]{:S(2)}, u32[]{:S(2)}) collective-permute-start(bf16[512,1024]{1,0:T(8,128)(2,1)S(1)} %fusion.34), channel_id=1, source_target_pairs={{0,8},{24,16},{1,9},{25,17},{2,10},{26,18},{3,11},{27,19},{4,12},{... | collective-permute-start | bytes 3145736 | tf_op jit(solution)/shard_map/ppermute | solution.py:244
  439.0 14.1 %collective-permute-done.57 = bf16[512,1024]{1,0:T(8,128)(2,1)S(1)} collective-permute-done((bf16[512,1024]{1,0:T(8,128)(2,1)S(1)}, bf16[512,1024]{1,0:T(8,128)(2,1)S(1)}, u32[]{:S(2)}, u32[]{:S(2)}) %collective-permute-start.57) | collective-permute-done | bytes 1048608 | tf_op jit(solution)/shard_map/ppermute | solution.py:244
  470.5 5.1 collective-permute-done.67
  480.8 3.1 fusion.53
  483.9 2.7 add_convert_fusion.25
  491.5 4.2 collective-permute-done.73
  510.8 3.3 fusion.49
  542.0 6.4 collective-permute-start.77
  562.1 3.2 fusion.54
  565.5 3.8 collective-permute-start.83
  592.4 6.3 collective-permute-start.90
  617.0 4.8 add_convert_fusion
  627.2 2.9 collective-permute-done.111
  630.6 3.8 collective-permute-done.112
  642.4 2.9 collective-permute-start.96
  649.6 11.1 %collective-permute-done.93 = bf16[512,1024]{1,0:T(8,128)(2,1)S(1)} collective-permute-done((bf16[512,1024]{1,0:T(8,128)(2,1)S(1)}, bf16[512,1024]{1,0:T(8,128)(2,1)S(1)}, u32[]{:S(2)}, u32[]{:S(2)}) %collective-permute-start.93) | collective-permute-done | bytes 1048608 | tf_op jit(solution)/shard_map/ppermute | solution.py:240
  663.0 2.8 collective-permute-start.99
  665.9 17.2 %collective-permute-done.96 = bf16[512,1024]{1,0:T(8,128)(2,1)S(1)} collective-permute-done((bf16[512,1024]{1,0:T(8,128)(2,1)S(1)}, bf16[512,1024]{1,0:T(8,128)(2,1)S(1)}, u32[]{:S(2)}, u32[]{:S(2)}) %collective-permute-start.96) | collective-permute-done | bytes 1048608 | tf_op jit(solution)/shard_map/ppermute | solution.py:240
  686.1 3.9 collective-permute-start.109
  690.1 15.5 %collective-permute-done.99 = bf16[512,1024]{1,0:T(8,128)(2,1)S(1)} collective-permute-done((bf16[512,1024]{1,0:T(8,128)(2,1)S(1)}, bf16[512,1024]{1,0:T(8,128)(2,1)S(1)}, u32[]{:S(2)}, u32[]{:S(2)}) %collective-permute-start.99) | collective-permute-done | bytes 1048608 | tf_op jit(solution)/shard_map/ppermute | solution.py:240
  709.2 6.5 collective-permute-start.123
  716.8 11.2 %collective-permute-done.109 = bf16[512,1024]{1,0:T(8,128)(2,1)S(1)} collective-permute-done((bf16[512,1024]{1,0:T(8,128)(2,1)S(1)}, bf16[512,1024]{1,0:T(8,128)(2,1)S(1)}, u32[]{:S(2)}, u32[]{:S(2)}) %collective-permute-start.109) | collective-permute-done | bytes 1048608 | tf_op jit(solution)/shard_map/ppermute | solution.py:240
  730.5 8.0 collective-permute-done.104
  739.3 22.5 %collective-permute-done.102 = bf16[2,64,2048]{2,1,0:T(8,128)(2,1)S(1)} collective-permute-done((bf16[2,64,2048]{2,1,0:T(8,128)(2,1)S(1)}, bf16[2,64,2048]{2,1,0:T(8,128)(2,1)S(1)}, u32[]{:S(2)}, u32[]{:S(2)}) %collective-permute-start.102) | collective-permute-done | bytes 524320 | tf_op jit(solution)/shard_map/ppermute | solution.py:72
  763.9 4.3 collective-permute-done.105
  788.6 3.9 collective-permute-start.119
  792.6 13.8 %collective-permute-done.127 = bf16[512,1024]{1,0:T(8,128)(2,1)S(1)} collective-permute-done((bf16[512,1024]{1,0:T(8,128)(2,1)S(1)}, bf16[512,1024]{1,0:T(8,128)(2,1)S(1)}, u32[]{:S(2)}, u32[]{:S(2)}) %collective-permute-start.127) | collective-permute-done | bytes 1048608 | tf_op jit(solution)/shard_map/ppermute | solution.py:72
  809.3 4.8 collective-permute-done.117
  816.7 18.7 %collective-permute-done.114 = bf16[512,1024]{1,0:T(8,128)(2,1)S(1)} collective-permute-done((bf16[512,1024]{1,0:T(8,128)(2,1)S(1)}, bf16[512,1024]{1,0:T(8,128)(2,1)S(1)}, u32[]{:S(2)}, u32[]{:S(2)}) %collective-permute-start.114) | collective-permute-done | bytes 1048608 | tf_op jit(solution)/shard_map/ppermute | solution.py:247
  842.2 3.4 copy-done.24
  847.3 14.2 %collective-permute-done.118 = bf16[512,1024]{1,0:T(8,128)(2,1)S(1)} collective-permute-done((bf16[512,1024]{1,0:T(8,128)(2,1)S(1)}, bf16[512,1024]{1,0:T(8,128)(2,1)S(1)}, u32[]{:S(2)}, u32[]{:S(2)}) %collective-permute-start.118) | collective-permute-done | bytes 1048608 | tf_op jit(solution)/shard_map/ppermute | solution.py:72
  866.5 14.0 %collective-permute-done.115 = bf16[512,1024]{1,0:T(8,128)(2,1)} collective-permute-done((bf16[512,1024]{1,0:T(8,128)(2,1)}, bf16[512,1024]{1,0:T(8,128)(2,1)}, u32[]{:S(2)}, u32[]{:S(2)}) %collective-permute-start.115) | collective-permute-done | bytes 1048608 | tf_op jit(solution)/shard_map/ppermute | solution.py:72
  900.9 12.0 %collective-permute-done.125 = bf16[512,1024]{1,0:T(8,128)(2,1)S(1)} collective-permute-done((bf16[512,1024]{1,0:T(8,128)(2,1)S(1)}, bf16[512,1024]{1,0:T(8,128)(2,1)S(1)}, u32[]{:S(2)}, u32[]{:S(2)}) %collective-permute-start.125) | collective-permute-done | bytes 1048608 | tf_op jit(solution)/shard_map/ppermute | solution.py:247
  (1018 shorter events, 430.2 us)
Async XLA Ops:
  7.2 79.8 %all-gather.3.cloned.1.call-start = ((), (), s32[]{:S(2)}) async-start(), calls=%async_computation | async-start | bytes 2621440 | tf_op jit(solution)/shard_map/all_gather | solution.py:334
  11.6 27.9 %collective-permute-start.13 = (bf16[128,2048]{1,0:T(8,128)(2,1)}, bf16[128,2048]{1,0:T(8,128)(2,1)S(1)}, u32[]{:S(2)}, u32[]{:S(2)}) collective-permute-start(bf16[128,2048]{1,0:T(8,128)(2,1)} %pad_maximum_fusion.26), channel_id=1, source_target_pairs={{0,4},{2,6},{4,0},{6,2},{1,5},{3,7},{5,1},{7,3},{8,12},{10,14},{12... | collective-permute-start | bytes 1572872 | tf_op jit(solution)/shard_map/ppermute | solution.py:72
  15.4 28.5 %collective-permute-start.12 = (bf16[128,2048]{1,0:T(8,128)(2,1)}, bf16[128,2048]{1,0:T(8,128)(2,1)}, u32[]{:S(2)}, u32[]{:S(2)}) collective-permute-start(bf16[128,2048]{1,0:T(8,128)(2,1)} %pad_maximum_fusion.25), channel_id=1, source_target_pairs={{0,2},{2,0},{4,6},{6,4},{1,3},{3,1},{5,7},{7,5},{8,10},{10,8},{12,... | collective-permute-start | bytes 1572872 | tf_op jit(solution)/shard_map/ppermute | solution.py:72
  23.1 43.7 %collective-permute-start.9 = (bf16[3,512,256]{2,1,0:T(8,128)(2,1)}, bf16[3,512,256]{2,1,0:T(8,128)(2,1)}, u32[]{:S(2)}, u32[]{:S(2)}) collective-permute-start(bf16[3,512,256]{2,1,0:T(8,128)(2,1)} %pad_maximum_fusion.18), channel_id=1, source_target_pairs={{0,2},{2,0},{4,6},{6,4},{1,3},{3,1},{5,7},{7,5},{8,10},{10,8},{12,... | collective-permute-start | bytes 2359304 | tf_op jit(solution)/shard_map/ppermute | solution.py:72
  39.2 138.7 %all-gather.5.cloned.1.call-start = ((), (), s32[]{:S(2)}) async-start(), calls=%async_computation.1 | async-start | bytes 2621440 | tf_op jit(solution)/shard_map/all_gather | solution.py:334
  42.1 24.7 %collective-permute-start.10 = (bf16[3,512,256]{2,1,0:T(8,128)(2,1)}, bf16[3,512,256]{2,1,0:T(8,128)(2,1)}, u32[]{:S(2)}, u32[]{:S(2)}) collective-permute-start(bf16[3,512,256]{2,1,0:T(8,128)(2,1)} %pad_maximum_fusion.15), channel_id=1, source_target_pairs={{0,4},{2,6},{4,0},{6,2},{1,5},{3,7},{5,1},{7,3},{8,12},{10,14},{12... | collective-permute-start | bytes 2359304 | tf_op jit(solution)/shard_map/ppermute | solution.py:72
  43.9 35.1 %collective-permute-start.11 = (bf16[3,512,256]{2,1,0:T(8,128)(2,1)}, bf16[3,512,256]{2,1,0:T(8,128)(2,1)}, u32[]{:S(2)}, u32[]{:S(2)}) collective-permute-start(bf16[3,512,256]{2,1,0:T(8,128)(2,1)} %pad_maximum_fusion.16), channel_id=1, source_target_pairs={{0,6},{2,4},{4,2},{6,0},{1,7},{3,5},{5,3},{7,1},{8,14},{10,12},{12... | collective-permute-start | bytes 2359304 | tf_op jit(solution)/shard_map/ppermute | solution.py:72
  62.0 40.6 %collective-permute-start.2 = (bf16[256,512]{1,0:T(8,128)(2,1)}, bf16[256,512]{1,0:T(8,128)(2,1)}, u32[]{:S(2)}, u32[]{:S(2)}) collective-permute-start(bf16[256,512]{1,0:T(8,128)(2,1)} %get-tuple-element.431), channel_id=1, source_target_pairs={{0,2},{2,0},{4,6},{6,4},{1,3},{3,1},{5,7},{7,5},{8,10},{10,8},{12,... | collective-permute-start | bytes 786440 | tf_op jit(solution)/shard_map/ppermute | solution.py:72
  64.2 38.6 %collective-permute-start.3 = (bf16[256,512]{1,0:T(8,128)(2,1)}, bf16[256,512]{1,0:T(8,128)(2,1)}, u32[]{:S(2)}, u32[]{:S(2)}) collective-permute-start(bf16[256,512]{1,0:T(8,128)(2,1)} %get-tuple-element.433), channel_id=1, source_target_pairs={{0,4},{2,6},{4,0},{6,2},{1,5},{3,7},{5,1},{7,3},{8,12},{10,14},{12... | collective-permute-start | bytes 786440 | tf_op jit(solution)/shard_map/ppermute | solution.py:72
  66.8 36.0 %collective-permute-start.4 = (bf16[256,512]{1,0:T(8,128)(2,1)}, bf16[256,512]{1,0:T(8,128)(2,1)S(1)}, u32[]{:S(2)}, u32[]{:S(2)}) collective-permute-start(bf16[256,512]{1,0:T(8,128)(2,1)} %get-tuple-element.430), channel_id=1, source_target_pairs={{0,6},{2,4},{4,2},{6,0},{1,7},{3,5},{5,3},{7,1},{8,14},{10,12},{12... | collective-permute-start | bytes 786440 | tf_op jit(solution)/shard_map/ppermute | solution.py:72
  66.8 39.7 %collective-permute-start = (bf16[128,1024]{1,0:T(8,128)(2,1)}, bf16[128,1024]{1,0:T(8,128)(2,1)S(1)}, u32[]{:S(2)}, u32[]{:S(2)}) collective-permute-start(bf16[128,1024]{1,0:T(8,128)(2,1)} %get-tuple-element.346), channel_id=1, source_target_pairs={{0,4},{2,6},{4,0},{6,2},{1,5},{3,7},{5,1},{7,3},{8,12},{10,14},{12... | collective-permute-start | bytes 786440 | tf_op jit(solution)/shard_map/ppermute | solution.py:72
  102.8 29.7 %collective-permute-start.5 = (bf16[1024,512]{1,0:T(8,128)(2,1)}, bf16[1024,512]{1,0:T(8,128)(2,1)}, u32[]{:S(2)}, u32[]{:S(2)}) collective-permute-start(bf16[1024,512]{1,0:T(8,128)(2,1)} %get-tuple-element.149), channel_id=1, source_target_pairs={{0,2},{2,0},{4,6},{6,4},{1,3},{3,1},{5,7},{7,5},{8,10},{10,8},{12,... | collective-permute-start | bytes 3145736 | tf_op jit(solution)/shard_map/ppermute | solution.py:72
  103.5 29.9 %collective-permute-start.6 = (bf16[1024,512]{1,0:T(8,128)(2,1)}, bf16[1024,512]{1,0:T(8,128)(2,1)}, u32[]{:S(2)}, u32[]{:S(2)}) collective-permute-start(bf16[1024,512]{1,0:T(8,128)(2,1)} %get-tuple-element.150), channel_id=1, source_target_pairs={{0,4},{2,6},{4,0},{6,2},{1,5},{3,7},{5,1},{7,3},{8,12},{10,14},{12... | collective-permute-start | bytes 3145736 | tf_op jit(solution)/shard_map/ppermute | solution.py:72
  135.0 25.5 %collective-permute-start.21 = (bf16[1024,512]{1,0:T(8,128)(2,1)}, bf16[1024,512]{1,0:T(8,128)(2,1)}, u32[]{:S(2)}, u32[]{:S(2)}) collective-permute-start(bf16[1024,512]{1,0:T(8,128)(2,1)} %get-tuple-element.163), channel_id=1, source_target_pairs={{0,6},{2,4},{4,2},{6,0},{1,7},{3,5},{5,3},{7,1},{8,14},{10,12},{12... | collective-permute-start | bytes 3145736 | tf_op jit(solution)/shard_map/ppermute | solution.py:72
  182.3 56.7 %collective-permute-start.38 = (bf16[512,1024]{1,0:T(8,128)(2,1)S(1)}, bf16[512,1024]{1,0:T(8,128)(2,1)S(1)}, u32[]{:S(2)}, u32[]{:S(2)}) collective-permute-start(bf16[512,1024]{1,0:T(8,128)(2,1)S(1)} %get-tuple-element.335), channel_id=1, source_target_pairs={{0,2},{2,0},{4,6},{6,4},{1,3},{3,1},{5,7},{7,5},{8,10},{10,8},{12,... | collective-permute-start | bytes 3145736 | tf_op jit(solution)/shard_map/ppermute | solution.py:72
  184.0 59.7 %collective-permute-start.39 = (bf16[512,1024]{1,0:T(8,128)(2,1)S(1)}, bf16[512,1024]{1,0:T(8,128)(2,1)S(1)}, u32[]{:S(2)}, u32[]{:S(2)}) collective-permute-start(bf16[512,1024]{1,0:T(8,128)(2,1)S(1)} %get-tuple-element.337), channel_id=1, source_target_pairs={{0,2},{2,0},{4,6},{6,4},{1,3},{3,1},{5,7},{7,5},{8,10},{10,8},{12,... | collective-permute-start | bytes 3145736 | tf_op jit(solution)/shard_map/ppermute | solution.py:72
  356.2 26.1 %collective-permute-start.54 = (bf16[512,1024]{1,0:T(8,128)(2,1)}, bf16[512,1024]{1,0:T(8,128)(2,1)}, u32[]{:S(2)}, u32[]{:S(2)}) collective-permute-start(bf16[512,1024]{1,0:T(8,128)(2,1)} %fusion.43), channel_id=1, source_target_pairs={{0,8},{24,16},{1,9},{25,17},{2,10},{26,18},{3,11},{27,19},{4,12},{... | collective-permute-start | bytes 3145736 | tf_op jit(solution)/shard_map/ppermute | solution.py:244
  359.3 46.0 %collective-permute-start.53 = (bf16[512,1024]{1,0:T(8,128)(2,1)}, bf16[512,1024]{1,0:T(8,128)(2,1)}, u32[]{:S(2)}, u32[]{:S(2)}) collective-permute-start(bf16[512,1024]{1,0:T(8,128)(2,1)} %fusion.40), channel_id=1, source_target_pairs={{0,8},{24,16},{1,9},{25,17},{2,10},{26,18},{3,11},{27,19},{4,12},{... | collective-permute-start | bytes 3145736 | tf_op jit(solution)/shard_map/ppermute | solution.py:244
  398.0 31.6 %collective-permute-start.59 = (bf16[512,1024]{1,0:T(8,128)(2,1)S(1)}, bf16[512,1024]{1,0:T(8,128)(2,1)S(1)}, u32[]{:S(2)}, u32[]{:S(2)}) collective-permute-start(bf16[512,1024]{1,0:T(8,128)(2,1)S(1)} %copy-done.89), channel_id=1, source_target_pairs={{0,8},{24,16},{1,9},{25,17},{2,10},{26,18},{3,11},{27,19},{4,12},{... | collective-permute-start | bytes 3145736 | tf_op jit(solution)/shard_map/ppermute | solution.py:244
  413.3 25.7 %collective-permute-start.56 = (bf16[512,1024]{1,0:T(8,128)(2,1)S(1)}, bf16[512,1024]{1,0:T(8,128)(2,1)S(1)}, u32[]{:S(2)}, u32[]{:S(2)}) collective-permute-start(bf16[512,1024]{1,0:T(8,128)(2,1)S(1)} %add_convert_fusion.33), channel_id=1, source_target_pairs={{8,16},{16,8},{9,17},{17,9},{10,18},{18,10},{11,19},{19,11},{12,20... | collective-permute-start | bytes 3145736 | tf_op jit(solution)/shard_map/ppermute | solution.py:230
  414.1 39.0 %collective-permute-start.57 = (bf16[512,1024]{1,0:T(8,128)(2,1)S(1)}, bf16[512,1024]{1,0:T(8,128)(2,1)S(1)}, u32[]{:S(2)}, u32[]{:S(2)}) collective-permute-start(bf16[512,1024]{1,0:T(8,128)(2,1)S(1)} %fusion.34), channel_id=1, source_target_pairs={{0,8},{24,16},{1,9},{25,17},{2,10},{26,18},{3,11},{27,19},{4,12},{... | collective-permute-start | bytes 3145736 | tf_op jit(solution)/shard_map/ppermute | solution.py:244
  434.0 41.6 %collective-permute-start.67 = (bf16[512,1024]{1,0:T(8,128)(2,1)}, bf16[512,1024]{1,0:T(8,128)(2,1)}, u32[]{:S(2)}, u32[]{:S(2)}) collective-permute-start(bf16[512,1024]{1,0:T(8,128)(2,1)} %fusion.51), channel_id=1, source_target_pairs={{0,8},{8,0},{16,24},{24,16},{1,9},{9,1},{17,25},{25,17},{2,10},{10... | collective-permute-start | bytes 3145736 | tf_op jit(solution)/shard_map/ppermute | solution.py:240
  437.0 38.6 %collective-permute-start.66 = (bf16[512,1024]{1,0:T(8,128)(2,1)}, bf16[512,1024]{1,0:T(8,128)(2,1)}, u32[]{:S(2)}, u32[]{:S(2)}) collective-permute-start(bf16[512,1024]{1,0:T(8,128)(2,1)} %add_convert_fusion.29), channel_id=1, source_target_pairs={{8,16},{16,8},{9,17},{17,9},{10,18},{18,10},{11,19},{19,11},{12,20... | collective-permute-start | bytes 3145736 | tf_op jit(solution)/shard_map/ppermute | solution.py:230
  461.7 40.0 %collective-permute-start.65 = (bf16[512,1024]{1,0:T(8,128)(2,1)}, bf16[512,1024]{1,0:T(8,128)(2,1)}, u32[]{:S(2)}, u32[]{:S(2)}) collective-permute-start(bf16[512,1024]{1,0:T(8,128)(2,1)} %fusion.50), channel_id=1, source_target_pairs={{0,8},{8,0},{16,24},{24,16},{1,9},{9,1},{17,25},{25,17},{2,10},{10... | collective-permute-start | bytes 3145736 | tf_op jit(solution)/shard_map/ppermute | solution.py:240
  469.8 32.6 %collective-permute-start.64 = (bf16[512,1024]{1,0:T(8,128)(2,1)S(1)}, bf16[512,1024]{1,0:T(8,128)(2,1)S(1)}, u32[]{:S(2)}, u32[]{:S(2)}) collective-permute-start(bf16[512,1024]{1,0:T(8,128)(2,1)S(1)} %add_convert_fusion.31), channel_id=1, source_target_pairs={{8,16},{16,8},{9,17},{17,9},{10,18},{18,10},{11,19},{19,11},{12,20... | collective-permute-start | bytes 3145736 | tf_op jit(solution)/shard_map/ppermute | solution.py:230
  488.9 30.0 %collective-permute-start.81 = (bf16[512,1024]{1,0:T(8,128)(2,1)}, bf16[512,1024]{1,0:T(8,128)(2,1)}, u32[]{:S(2)}, u32[]{:S(2)}) collective-permute-start(bf16[512,1024]{1,0:T(8,128)(2,1)} %fusion.53), channel_id=1, source_target_pairs={{0,8},{8,0},{16,24},{24,16},{1,9},{9,1},{17,25},{25,17},{2,10},{10... | collective-permute-start | bytes 3145736 | tf_op jit(solution)/shard_map/ppermute | solution.py:240
  500.4 64.9 %collective-permute-start.78 = (bf16[512,512]{1,0:T(8,128)(2,1)}, bf16[512,512]{1,0:T(8,128)(2,1)}, u32[]{:S(2)}, u32[]{:S(2)}) collective-permute-start(bf16[512,512]{1,0:T(8,128)(2,1)} %get-tuple-element.403), channel_id=1, source_target_pairs={{0,4},{2,6},{4,0},{6,2},{1,5},{3,7},{5,1},{7,3},{8,12},{10,14},{12... | collective-permute-start | bytes 1572872 | tf_op jit(solution)/shard_map/ppermute | solution.py:72
  501.7 63.7 %collective-permute-start.79 = (bf16[512,512]{1,0:T(8,128)(2,1)}, bf16[512,512]{1,0:T(8,128)(2,1)}, u32[]{:S(2)}, u32[]{:S(2)}) collective-permute-start(bf16[512,512]{1,0:T(8,128)(2,1)} %get-tuple-element.402), channel_id=1, source_target_pairs={{0,6},{2,4},{4,2},{6,0},{1,7},{3,5},{5,3},{7,1},{8,14},{10,12},{12... | collective-permute-start | bytes 1572872 | tf_op jit(solution)/shard_map/ppermute | solution.py:72
  542.0 28.6 %collective-permute-start.77 = (bf16[512,1024]{1,0:T(8,128)(2,1)S(1)}, bf16[512,1024]{1,0:T(8,128)(2,1)S(1)}, u32[]{:S(2)}, u32[]{:S(2)}) collective-permute-start(bf16[512,1024]{1,0:T(8,128)(2,1)S(1)} %fusion.52), channel_id=1, source_target_pairs={{0,8},{8,0},{16,24},{24,16},{1,9},{9,1},{17,25},{25,17},{2,10},{10... | collective-permute-start | bytes 3145736 | tf_op jit(solution)/shard_map/ppermute | solution.py:240
  553.4 39.0 %collective-permute-start.84 = (bf16[512,512]{1,0:T(8,128)(2,1)}, bf16[512,512]{1,0:T(8,128)(2,1)}, u32[]{:S(2)}, u32[]{:S(2)}) collective-permute-start(bf16[512,512]{1,0:T(8,128)(2,1)} %get-tuple-element.401), channel_id=1, source_target_pairs={{0,4},{2,6},{4,0},{6,2},{1,5},{3,7},{5,1},{7,3},{8,12},{10,14},{12... | collective-permute-start | bytes 1572872 | tf_op jit(solution)/shard_map/ppermute | solution.py:72
  565.4 33.3 %collective-permute-start.85 = (bf16[512,512]{1,0:T(8,128)(2,1)}, bf16[512,512]{1,0:T(8,128)(2,1)}, u32[]{:S(2)}, u32[]{:S(2)}) collective-permute-start(bf16[512,512]{1,0:T(8,128)(2,1)} %get-tuple-element.400), channel_id=1, source_target_pairs={{0,6},{2,4},{4,2},{6,0},{1,7},{3,5},{5,3},{7,1},{8,14},{10,12},{12... | collective-permute-start | bytes 1572872 | tf_op jit(solution)/shard_map/ppermute | solution.py:72
  565.5 34.8 %collective-permute-start.83 = (bf16[512,1024]{1,0:T(8,128)(2,1)}, bf16[512,1024]{1,0:T(8,128)(2,1)}, u32[]{:S(2)}, u32[]{:S(2)}) collective-permute-start(bf16[512,1024]{1,0:T(8,128)(2,1)} %fusion.54), channel_id=1, source_target_pairs={{0,8},{8,0},{16,24},{24,16},{1,9},{9,1},{17,25},{25,17},{2,10},{10... | collective-permute-start | bytes 3145736 | tf_op jit(solution)/shard_map/ppermute | solution.py:240
  570.6 29.9 %collective-permute-start.82 = (bf16[512,1024]{1,0:T(8,128)(2,1)}, bf16[512,1024]{1,0:T(8,128)(2,1)}, u32[]{:S(2)}, u32[]{:S(2)}) collective-permute-start(bf16[512,1024]{1,0:T(8,128)(2,1)} %add_convert_fusion.23), channel_id=1, source_target_pairs={{8,16},{16,8},{9,17},{17,9},{10,18},{18,10},{11,19},{19,11},{12,20... | collective-permute-start | bytes 3145736 | tf_op jit(solution)/shard_map/ppermute | solution.py:230
  588.9 47.8 %collective-permute-start.91 = (bf16[512,512]{1,0:T(8,128)(2,1)}, bf16[512,512]{1,0:T(8,128)(2,1)}, u32[]{:S(2)}, u32[]{:S(2)}) collective-permute-start(bf16[512,512]{1,0:T(8,128)(2,1)} %get-tuple-element.398), channel_id=1, source_target_pairs={{0,2},{2,0},{4,6},{6,4},{1,3},{3,1},{5,7},{7,5},{8,10},{10,8},{12,... | collective-permute-start | bytes 1572872 | tf_op jit(solution)/shard_map/ppermute | solution.py:72
  592.4 45.3 %collective-permute-start.90 = (bf16[512,1024]{1,0:T(8,128)(2,1)}, bf16[512,1024]{1,0:T(8,128)(2,1)}, u32[]{:S(2)}, u32[]{:S(2)}) collective-permute-start(bf16[512,1024]{1,0:T(8,128)(2,1)} %fusion.55), channel_id=1, source_target_pairs={{0,8},{8,0},{16,24},{24,16},{1,9},{9,1},{17,25},{25,17},{2,10},{10... | collective-permute-start | bytes 3145736 | tf_op jit(solution)/shard_map/ppermute | solution.py:240
  598.7 40.3 %collective-permute-start.89 = (bf16[512,1024]{1,0:T(8,128)(2,1)}, bf16[512,1024]{1,0:T(8,128)(2,1)}, u32[]{:S(2)}, u32[]{:S(2)}) collective-permute-start(bf16[512,1024]{1,0:T(8,128)(2,1)} %add_convert_fusion.21), channel_id=1, source_target_pairs={{8,16},{16,8},{9,17},{17,9},{10,18},{18,10},{11,19},{19,11},{12,20... | collective-permute-start | bytes 3145736 | tf_op jit(solution)/shard_map/ppermute | solution.py:230
  600.3 47.2 %collective-permute-start.94 = (bf16[512,512]{1,0:T(8,128)(2,1)}, bf16[512,512]{1,0:T(8,128)(2,1)}, u32[]{:S(2)}, u32[]{:S(2)}) collective-permute-start(bf16[512,512]{1,0:T(8,128)(2,1)} %get-tuple-element.396), channel_id=1, source_target_pairs={{0,2},{2,0},{4,6},{6,4},{1,3},{3,1},{5,7},{7,5},{8,10},{10,8},{12,... | collective-permute-start | bytes 1572872 | tf_op jit(solution)/shard_map/ppermute | solution.py:72
  600.5 25.2 %collective-permute-start.110 = (f32[16,1024]{1,0:T(8,128)}, f32[16,1024]{1,0:T(8,128)S(1)}, u32[]{:S(2)}, u32[]{:S(2)}) collective-permute-start(f32[16,1024]{1,0:T(8,128)} %reshape.728), channel_id=1, source_target_pairs={{0,2},{2,0},{4,6},{6,4},{1,3},{3,1},{5,7},{7,5},{8,10},{10,8},{12,... | collective-permute-start | bytes 196616 | tf_op jit(solution)/shard_map/ppermute | solution.py:72
  634.4 26.2 %collective-permute-start.93 = (bf16[512,1024]{1,0:T(8,128)(2,1)S(1)}, bf16[512,1024]{1,0:T(8,128)(2,1)S(1)}, u32[]{:S(2)}, u32[]{:S(2)}) collective-permute-start(bf16[512,1024]{1,0:T(8,128)(2,1)S(1)} %fusion.56), channel_id=1, source_target_pairs={{0,8},{8,0},{16,24},{24,16},{1,9},{9,1},{17,25},{25,17},{2,10},{10... | collective-permute-start | bytes 3145736 | tf_op jit(solution)/shard_map/ppermute | solution.py:240
  636.7 23.9 %collective-permute-start.92 = (bf16[512,1024]{1,0:T(8,128)(2,1)S(1)}, bf16[512,1024]{1,0:T(8,128)(2,1)S(1)}, u32[]{:S(2)}, u32[]{:S(2)}) collective-permute-start(bf16[512,1024]{1,0:T(8,128)(2,1)S(1)} %add_convert_fusion.19), channel_id=1, source_target_pairs={{8,16},{16,8},{9,17},{17,9},{10,18},{18,10},{11,19},{19,11},{12,20... | collective-permute-start | bytes 3145736 | tf_op jit(solution)/shard_map/ppermute | solution.py:230
  637.7 25.3 %collective-permute-start.97 = (bf16[512,1024]{1,0:T(8,128)(2,1)S(1)}, bf16[512,1024]{1,0:T(8,128)(2,1)S(1)}, u32[]{:S(2)}, u32[]{:S(2)}) collective-permute-start(bf16[512,1024]{1,0:T(8,128)(2,1)S(1)} %broadcast_select_fusion.10), channel_id=1, source_target_pairs={{0,4},{2,6},{4,0},{6,2},{1,5},{3,7},{5,1},{7,3},{8,12},{10,14},{12... | collective-permute-start | bytes 3145736 | tf_op jit(solution)/shard_map/ppermute | solution.py:72
  642.4 40.7 %collective-permute-start.96 = (bf16[512,1024]{1,0:T(8,128)(2,1)S(1)}, bf16[512,1024]{1,0:T(8,128)(2,1)S(1)}, u32[]{:S(2)}, u32[]{:S(2)}) collective-permute-start(bf16[512,1024]{1,0:T(8,128)(2,1)S(1)} %fusion.57), channel_id=1, source_target_pairs={{0,8},{8,0},{16,24},{24,16},{1,9},{9,1},{17,25},{25,17},{2,10},{10... | collective-permute-start | bytes 3145736 | tf_op jit(solution)/shard_map/ppermute | solution.py:240
  647.4 36.5 %collective-permute-start.95 = (bf16[512,1024]{1,0:T(8,128)(2,1)S(1)}, bf16[512,1024]{1,0:T(8,128)(2,1)S(1)}, u32[]{:S(2)}, u32[]{:S(2)}) collective-permute-start(bf16[512,1024]{1,0:T(8,128)(2,1)S(1)} %add_convert_fusion.17), channel_id=1, source_target_pairs={{8,16},{16,8},{9,17},{17,9},{10,18},{18,10},{11,19},{19,11},{12,20... | collective-permute-start | bytes 3145736 | tf_op jit(solution)/shard_map/ppermute | solution.py:230
  660.6 48.6 %collective-permute-start.101 = (bf16[2,2,128,2048]{3,2,1,0:T(8,128)(2,1)S(1)}, bf16[2,2,128,2048]{3,2,1,0:T(8,128)(2,1)S(1)}, u32[]{:S(2)}, u32[]{:S(2)}) collective-permute-start(bf16[2,2,128,2048]{3,2,1,0:T(8,128)(2,1)S(1)} %fusion.22), channel_id=1, source_target_pairs={{0,2},{2,0},{4,6},{6,4},{1,3},{3,1},{5,7},{7,5},{8,10},{10,8},{12,... | collective-permute-start | bytes 6291464 | tf_op jit(solution)/shard_map/ppermute | solution.py:72
  660.6 25.5 %collective-permute-start.100 = (bf16[512,1024]{1,0:T(8,128)(2,1)S(1)}, bf16[512,1024]{1,0:T(8,128)(2,1)}, u32[]{:S(2)}, u32[]{:S(2)}) collective-permute-start(bf16[512,1024]{1,0:T(8,128)(2,1)S(1)} %broadcast_select_fusion.9), channel_id=1, source_target_pairs={{0,6},{2,4},{4,2},{6,0},{1,7},{3,5},{5,3},{7,1},{8,14},{10,12},{12... | collective-permute-start | bytes 3145736 | tf_op jit(solution)/shard_map/ppermute | solution.py:72
  663.0 42.5 %collective-permute-start.99 = (bf16[512,1024]{1,0:T(8,128)(2,1)S(1)}, bf16[512,1024]{1,0:T(8,128)(2,1)S(1)}, u32[]{:S(2)}, u32[]{:S(2)}) collective-permute-start(bf16[512,1024]{1,0:T(8,128)(2,1)S(1)} %fusion.58), channel_id=1, source_target_pairs={{0,8},{8,0},{16,24},{24,16},{1,9},{9,1},{17,25},{25,17},{2,10},{10... | collective-permute-start | bytes 3145736 | tf_op jit(solution)/shard_map/ppermute | solution.py:240
  685.1 96.5 %collective-permute-start.126 = (bf16[512,1024]{1,0:T(8,128)(2,1)}, bf16[512,1024]{1,0:T(8,128)(2,1)}, u32[]{:S(2)}, u32[]{:S(2)}) collective-permute-start(bf16[512,1024]{1,0:T(8,128)(2,1)} %broadcast_select_fusion.4), channel_id=1, source_target_pairs={{0,2},{2,0},{4,6},{6,4},{1,3},{3,1},{5,7},{7,5},{8,10},{10,8},{12,... | collective-permute-start | bytes 3145736 | tf_op jit(solution)/shard_map/ppermute | solution.py:72
  686.1 41.9 %collective-permute-start.109 = (bf16[512,1024]{1,0:T(8,128)(2,1)S(1)}, bf16[512,1024]{1,0:T(8,128)(2,1)S(1)}, u32[]{:S(2)}, u32[]{:S(2)}) collective-permute-start(bf16[512,1024]{1,0:T(8,128)(2,1)S(1)} %fusion.59), channel_id=1, source_target_pairs={{0,8},{8,0},{16,24},{24,16},{1,9},{9,1},{17,25},{25,17},{2,10},{10... | collective-permute-start | bytes 3145736 | tf_op jit(solution)/shard_map/ppermute | solution.py:240
  706.7 56.4 %collective-permute-start.116 = (bf16[512,1024]{1,0:T(8,128)(2,1)S(1)}, bf16[512,1024]{1,0:T(8,128)(2,1)S(1)}, u32[]{:S(2)}, u32[]{:S(2)}) collective-permute-start(bf16[512,1024]{1,0:T(8,128)(2,1)S(1)} %add_convert_fusion.9), channel_id=1, source_target_pairs={{8,16},{16,8},{9,17},{17,9},{10,18},{18,10},{11,19},{19,11},{12,20... | collective-permute-start | bytes 3145736 | tf_op jit(solution)/shard_map/ppermute | solution.py:230
  709.2 130.3 %collective-permute-start.123 = (bf16[512,1024]{1,0:T(8,128)(2,1)S(1)}, bf16[512,1024]{1,0:T(8,128)(2,1)}, u32[]{:S(2)}, u32[]{:S(2)}) collective-permute-start(bf16[512,1024]{1,0:T(8,128)(2,1)S(1)} %fusion.60), channel_id=1, source_target_pairs={{0,8},{8,0},{16,24},{24,16},{1,9},{9,1},{17,25},{25,17},{2,10},{10... | collective-permute-start | bytes 3145736 | tf_op jit(solution)/shard_map/ppermute | solution.py:240
  728.0 80.9 %collective-permute-start.128 = (bf16[512,1024]{1,0:T(8,128)(2,1)}, bf16[512,1024]{1,0:T(8,128)(2,1)S(1)}, u32[]{:S(2)}, u32[]{:S(2)}) collective-permute-start(bf16[512,1024]{1,0:T(8,128)(2,1)} %broadcast_select_fusion.2), channel_id=1, source_target_pairs={{0,4},{2,6},{4,0},{6,2},{1,5},{3,7},{5,1},{7,3},{8,12},{10,14},{12... | collective-permute-start | bytes 3145736 | tf_op jit(solution)/shard_map/ppermute | solution.py:72
  781.5 24.9 %collective-permute-start.127 = (bf16[512,1024]{1,0:T(8,128)(2,1)S(1)}, bf16[512,1024]{1,0:T(8,128)(2,1)S(1)}, u32[]{:S(2)}, u32[]{:S(2)}) collective-permute-start(bf16[512,1024]{1,0:T(8,128)(2,1)S(1)} %broadcast_select_fusion.3), channel_id=1, source_target_pairs={{0,6},{2,4},{4,2},{6,0},{1,7},{3,5},{5,3},{7,1},{8,14},{10,12},{12... | collective-permute-start | bytes 3145736 | tf_op jit(solution)/shard_map/ppermute | solution.py:72
  784.6 29.5 %collective-permute-start.117 = (bf16[512,1024]{1,0:T(8,128)(2,1)S(1)}, bf16[512,1024]{1,0:T(8,128)(2,1)S(1)}, u32[]{:S(2)}, u32[]{:S(2)}) collective-permute-start(bf16[512,1024]{1,0:T(8,128)(2,1)S(1)} %add_convert_fusion.8), channel_id=1, source_target_pairs={{8,0},{16,24},{9,1},{17,25},{10,2},{18,26},{11,3},{19,27},{12,4},{... | collective-permute-start | bytes 3145736 | tf_op jit(solution)/shard_map/ppermute | solution.py:247
  788.6 26.7 %collective-permute-start.119 = (bf16[528,1024]{1,0:T(8,128)(2,1)S(1)}, bf16[528,1024]{1,0:T(8,128)(2,1)S(1)}, u32[]{:S(2)}, u32[]{:S(2)}) collective-permute-start(bf16[528,1024]{1,0:T(8,128)(2,1)S(1)} %pad_maximum_fusion.3), channel_id=1, source_target_pairs={{0,8},{24,16},{1,9},{25,17},{2,10},{26,18},{3,11},{27,19},{4,12},{... | collective-permute-start | bytes 3244040 | tf_op jit(solution)/shard_map/ppermute | solution.py:244
  806.4 29.0 %collective-permute-start.114 = (bf16[512,1024]{1,0:T(8,128)(2,1)S(1)}, bf16[512,1024]{1,0:T(8,128)(2,1)S(1)}, u32[]{:S(2)}, u32[]{:S(2)}) collective-permute-start(bf16[512,1024]{1,0:T(8,128)(2,1)S(1)} %add_convert_fusion.10), channel_id=1, source_target_pairs={{8,0},{16,24},{9,1},{17,25},{10,2},{18,26},{11,3},{19,27},{12,4},{... | collective-permute-start | bytes 3145736 | tf_op jit(solution)/shard_map/ppermute | solution.py:247
  809.0 28.6 %collective-permute-start.130 = (bf16[512,1024]{1,0:T(8,128)(2,1)S(1)}, bf16[512,1024]{1,0:T(8,128)(2,1)S(1)}, u32[]{:S(2)}, u32[]{:S(2)}) collective-permute-start(bf16[512,1024]{1,0:T(8,128)(2,1)S(1)} %broadcast_select_fusion.1), channel_id=1, source_target_pairs={{0,2},{2,0},{4,6},{6,4},{1,3},{3,1},{5,7},{7,5},{8,10},{10,8},{12,... | collective-permute-start | bytes 3145736 | tf_op jit(solution)/shard_map/ppermute | solution.py:72
  814.1 31.5 %collective-permute-start.107 = (bf16[1,128,2048]{2,1,0:T(8,128)(2,1)S(1)}, bf16[1,128,2048]{2,1,0:T(8,128)(2,1)S(1)}, u32[]{:S(2)}, u32[]{:S(2)}) collective-permute-start(bf16[1,128,2048]{2,1,0:T(8,128)(2,1)S(1)} %maximum_bitcast_fusion.1), channel_id=1, source_target_pairs={{0,1},{1,0},{2,3},{3,2},{4,5},{5,4},{6,7},{7,6},{8,9},{9,8},{10,11... | collective-permute-start | bytes 1572872 | tf_op jit(solution)/shard_map/ppermute | solution.py:74
  815.3 32.0 %collective-permute-start.106 = (bf16[1,128,2048]{2,1,0:T(8,128)(2,1)S(1)}, bf16[1,128,2048]{2,1,0:T(8,128)(2,1)S(1)}, u32[]{:S(2)}, u32[]{:S(2)}) collective-permute-start(bf16[1,128,2048]{2,1,0:T(8,128)(2,1)S(1)} %maximum_bitcast_fusion), channel_id=1, source_target_pairs={{0,1},{1,0},{2,3},{3,2},{4,5},{5,4},{6,7},{7,6},{8,9},{9,8},{10,11... | collective-permute-start | bytes 1572872 | tf_op jit(solution)/shard_map/ppermute | solution.py:74
  835.4 26.1 %collective-permute-start.118 = (bf16[512,1024]{1,0:T(8,128)(2,1)S(1)}, bf16[512,1024]{1,0:T(8,128)(2,1)S(1)}, u32[]{:S(2)}, u32[]{:S(2)}) collective-permute-start(bf16[512,1024]{1,0:T(8,128)(2,1)S(1)} %broadcast_select_fusion.6), channel_id=1, source_target_pairs={{0,4},{2,6},{4,0},{6,2},{1,5},{3,7},{5,1},{7,3},{8,12},{10,14},{12... | collective-permute-start | bytes 3145736 | tf_op jit(solution)/shard_map/ppermute | solution.py:72
  837.6 25.9 %collective-permute-start.120 = (bf16[528,1024]{1,0:T(8,128)(2,1)S(1)}, bf16[528,1024]{1,0:T(8,128)(2,1)}, u32[]{:S(2)}, u32[]{:S(2)}) collective-permute-start(bf16[528,1024]{1,0:T(8,128)(2,1)S(1)} %add_convert_fusion.3), channel_id=1, source_target_pairs={{8,16},{16,8},{9,17},{17,9},{10,18},{18,10},{11,19},{19,11},{12,20... | collective-permute-start | bytes 3244040 | tf_op jit(solution)/shard_map/ppermute | solution.py:230
  839.5 40.9 %collective-permute-start.115 = (bf16[512,1024]{1,0:T(8,128)(2,1)}, bf16[512,1024]{1,0:T(8,128)(2,1)}, u32[]{:S(2)}, u32[]{:S(2)}) collective-permute-start(bf16[512,1024]{1,0:T(8,128)(2,1)} %broadcast_select_fusion.7), channel_id=1, source_target_pairs={{0,6},{2,4},{4,2},{6,0},{1,7},{3,5},{5,3},{7,1},{8,14},{10,12},{12... | collective-permute-start | bytes 3145736 | tf_op jit(solution)/shard_map/ppermute | solution.py:72
  845.5 36.9 %collective-permute-start.124 = (bf16[512,1024]{1,0:T(8,128)(2,1)S(1)}, bf16[512,1024]{1,0:T(8,128)(2,1)}, u32[]{:S(2)}, u32[]{:S(2)}) collective-permute-start(bf16[512,1024]{1,0:T(8,128)(2,1)S(1)} %get-tuple-element.384), channel_id=1, source_target_pairs={{8,16},{16,8},{9,17},{17,9},{10,18},{18,10},{11,19},{19,11},{12,20... | collective-permute-start | bytes 3145736 | tf_op jit(solution)/shard_map/ppermute | solution.py:230
  865.2 29.3 %collective-permute-start.121 = (bf16[528,1024]{1,0:T(8,128)(2,1)S(1)}, bf16[528,1024]{1,0:T(8,128)(2,1)}, u32[]{:S(2)}, u32[]{:S(2)}) collective-permute-start(bf16[528,1024]{1,0:T(8,128)(2,1)S(1)} %add_convert_fusion.2), channel_id=1, source_target_pairs={{8,0},{16,24},{9,1},{17,25},{10,2},{18,26},{11,3},{19,27},{12,4},{... | collective-permute-start | bytes 3244040 | tf_op jit(solution)/shard_map/ppermute | solution.py:247
  884.1 28.7 %collective-permute-start.125 = (bf16[512,1024]{1,0:T(8,128)(2,1)S(1)}, bf16[512,1024]{1,0:T(8,128)(2,1)S(1)}, u32[]{:S(2)}, u32[]{:S(2)}) collective-permute-start(bf16[512,1024]{1,0:T(8,128)(2,1)S(1)} %add_convert_fusion.5), channel_id=1, source_target_pairs={{8,0},{16,24},{9,1},{17,25},{10,2},{18,26},{11,3},{19,27},{12,4},{... | collective-permute-start | bytes 3145736 | tf_op jit(solution)/shard_map/ppermute | solution.py:247
  (255 other events, 2369.4 us)
Sparse Core Ops, SparseCore 0:
  39.3 47.6 all-gather.2
  133.5 44.2 all-gather.4

commit v4 on v3

--- a/solution.py
+++ b/solution.py
@@ -1,6 +1,8 @@
 import jax
 import jax.numpy as jnp
 from jax import lax
+from jax.experimental import pallas as pl
+from jax.experimental.pallas import tpu as pltpu
 from jax.sharding import PartitionSpec as P
 
 HD = 128
@@ -15,17 +17,69 @@
     return lax.rsqrt(jnp.mean(matrix * matrix, axis=-1, keepdims=True) + EPSILON)
 
 
-def rotate_pairs(matrix, cos_table, sin_table):
-    half_size = matrix.shape[-1] // 2
-    first_half = matrix[..., :half_size]
-    second_half = matrix[..., half_size:]
-    return jnp.concatenate(
-        [
-            first_half * cos_table - second_half * sin_table,
-            second_half * cos_table + first_half * sin_table,
-        ],
-        axis=-1,
-    )
+def masked_prob(length, q_rot, k_rot, place_col, place_row):
+    scores = through(q_rot, k_rot) * HD ** (-0.5)
+    allowed = (place_row <= place_col) & (place_row < length)
+    scores = jnp.where(allowed, scores, -MASK_VALUE)
+    exponent = jnp.exp(scores - jnp.max(scores, axis=-1, keepdims=True))
+    return exponent / jnp.sum(exponent, axis=-1, keepdims=True)
+
+
+def attend_kernel(
+    length, query, key, value, cos, sin, place_col, place_row, mix, q_out, k_out
+):
+    def turned(normed):
+        normed = normed[...]
+        return (normed * cos[...] + pltpu.roll(normed, HD // 2, 1) * sin[...]).astype(BF)
+
+    q_rot, k_rot = turned(query), turned(key)
+    q_out[...], k_out[...] = q_rot, k_rot
+    prob = masked_prob(length[pl.program_id(0)], q_rot, k_rot, place_col[...], place_row[...])
+    mix[...] = dot(prob.astype(BF), value[...]).astype(BF)
+
+
+def attend_back_kernel(
+    length, q_rot, k_rot, value, d_mix, cos, sin, place_col, place_row, d_query, d_key, d_value
+):
+    q_rot, k_rot, d_mix = q_rot[...], k_rot[...], d_mix[...]
+    prob = masked_prob(length[pl.program_id(0)], q_rot, k_rot, place_col[...], place_row[...])
+    d_value[...] = against(prob.astype(BF), d_mix).astype(BF)
+    d_prob = through(d_mix, value[...])
+    row_delta = jnp.sum(prob * d_prob, axis=-1, keepdims=True)
+    d_scores = (prob * (d_prob - row_delta)).astype(BF)
+
+    def turned_back(grad):
+        grad = grad * HD ** (-0.5)
+        return grad * cos[...] - pltpu.roll(grad, HD // 2, 1) * sin[...]
+
+    d_query[...] = turned_back(dot(d_scores, k_rot))
+    d_key[...] = turned_back(against(d_scores, q_rot))
+
+
+def over_heads(kernel, lengths, seq_len, outs, *arrays):
+    tokens, features = arrays[0].shape
+
+    def spec(shape):
+        if shape == (tokens, features):
+            return pl.BlockSpec((seq_len, HD), lambda s, h, *_: (s, h))
+        return pl.BlockSpec(shape, lambda s, h, *_: (0, 0))
+
+    count = tokens * features // HD
+    return pl.pallas_call(
+        kernel,
+        out_shape=tuple(jax.ShapeDtypeStruct((tokens, features), dtype) for dtype in outs),
+        grid_spec=pltpu.PrefetchScalarGridSpec(
+            num_scalar_prefetch=1,
+            grid=(tokens // seq_len, features // HD),
+            in_specs=[spec(array.shape) for array in arrays],
+            out_specs=tuple(spec((tokens, features)) for _ in outs),
+        ),
+        cost_estimate=pl.CostEstimate(
+            flops=4 * len(outs) * count * seq_len * HD,
+            bytes_accessed=4 * (len(arrays) + len(outs)) * tokens * features,
+            transcendentals=count * seq_len,
+        ),
+    )(lengths, *arrays)
 
 
 def dot(left_side, right_side):
@@ -209,6 +263,9 @@
             if array is not None:
                 self.arrays.append(array)
             return values
+        if 0 < len(self.arrays) <= self.depth + 2:
+            last = self.pending[-1]
+            last["inward"], array = together(last["inward"], array)
         pending, moving, array, values = together(
             self.pending.pop(0), self.moving.pop(0), array, values
         )
@@ -285,7 +342,6 @@
     tok_all = seq_grp * seq_len
     heads_cols = query_weight.shape[1]
     head_part = heads_cols // rows
-    heads_here = head_part // HD
     ff_part = gate_weight.shape[1] // rows
 
     first_own = col * seq_own
@@ -378,8 +434,6 @@
     scales = lax.rsqrt(plane.total(squares) / width + EPSILON)
     q_scale = scales[0][:, None]
     k_scale = scales[1][:, None]
-    q_unit = query_raw * q_scale
-    k_unit = key_raw * k_scale
     block_rows = row ^ jnp.arange(rows, dtype=jnp.int32)
     places = (
         block_rows[:, None] * tok_seq + jnp.arange(tok_seq, dtype=jnp.int32)[None, :]
@@ -398,41 +452,34 @@
     )
     frequency = ROPE_THETA ** (-(jnp.arange(HD // 2).astype(F32) * 2.0 / HD))
     angles = places.astype(F32)[:, None] * frequency[None, :]
-    cos_table = jnp.cos(angles)[None, :, None, :]
-    sin_table = jnp.sin(angles)[None, :, None, :]
-    head_shape = (seq_grp, seq_len, heads_here, HD)
-
-    def heads_of(array):
-        return by_sequence(array).reshape(head_shape)
+    cos_table = jnp.cos(angles)
+    sin_table = jnp.sin(angles)
+    cos_table = jnp.concatenate([cos_table, cos_table], axis=1)
+    sin_table = jnp.concatenate([-sin_table, sin_table], axis=1)
+    place_tables = places[:, None], places[None, :]
+
+    def in_rows(array):
+        return by_sequence(array).reshape(array.shape)
 
     def joined(array):
         return by_block(array.reshape(seq_grp, seq_len, head_part))
 
-    q_rot = rotate_pairs(heads_of(q_unit * q_gain_f), cos_table, sin_table).astype(BF)
-    k_rot = rotate_pairs(heads_of(k_unit * k_gain_f), cos_table, sin_table).astype(BF)
-    values = heads_of(value_low)
+    values = in_rows(value_low)
+    q_unit = query_raw * q_scale
+    k_unit = key_raw * k_scale
+    q_normed, k_normed = in_rows(q_unit * q_gain_f), in_rows(k_unit * k_gain_f)
     down_half = rows // 2
     out_pieces, down_pieces = together(out_pieces, down_pieces)
     down_pieces = [plane.hop(piece, k) for k, piece in enumerate(down_pieces)]
-    up_far, down_pieces[: down_half + 1], q_rot = together(
-        up_far, down_pieces[: down_half + 1], q_rot
-    )
+    up_far, q_normed = together(up_far, q_normed)
+    down_pieces[: down_half + 1], values = together(down_pieces[: down_half + 1], values)
     w_out = jnp.concatenate(out_pieces, axis=1)
     up_far = over_groups(up_far)
-    allowed = (places[None, None, :] <= places[None, :, None]) & (
-        places[None, None, :] < live_len[:, None, None]
-    )
-    score_scale = HD ** (-0.5)
-    scores = (
-        jnp.einsum("sqhd,skhd->shqk", q_rot, k_rot, preferred_element_type=F32) * score_scale
-    )
-    scores = jnp.where(allowed[:, None], scores, -MASK_VALUE)
-    exponent = jnp.exp(scores - jnp.max(scores, axis=-1, keepdims=True))
-    prob = exponent / jnp.sum(exponent, axis=-1, keepdims=True)
-    prob_low = prob.astype(BF)
-    attn_mix = joined(
-        jnp.einsum("shqk,skhd->sqhd", prob_low, values, preferred_element_type=F32).astype(BF)
-    )
+    attn_mix, q_rot, k_rot = over_heads(
+        attend_kernel, live_len, seq_len, (BF, BF, BF),
+        q_normed, k_normed, values, cos_table, sin_table, *place_tables,
+    )
+    attn_mix = joined(attn_mix)
     up_far, down_pieces, attn_mix = together(up_far, down_pieces, attn_mix)
     attn_raw = plane.scatter(dot(attn_mix, w_out).astype(BF))
     w_gate = whole(gate_pieces, gate_far, 0)
@@ -467,9 +514,9 @@
             first = rows // 2 if index < 2 else 0
             blocks = jnp.split(total, rows // 2, axis=1)
             return [plane.hop(block, first + k) for k, block in enumerate(blocks)]
-        if index == 3 + 3 * rows:
-            return plane.hop(total[:part], order[-1]), total[part:]
-        return plane.hop(total, order[index % rows])
+        if index == 4 + 2 * rows:
+            return plane.hop(total[:part], order[0]), total[part:]
+        return plane.hop(total, order[(index - 4) % rows])
 
     line = Line(move)
 
@@ -494,20 +541,12 @@
     d_a_unit = d_hidden * attn_gain_f
     d_attn = a_scale * (d_a_unit - a_unit * jnp.mean(d_a_unit * a_unit, axis=-1, keepdims=True))
     d_attn_all = plane.gather(d_attn.astype(BF), step)
-    d_mix = heads_of(through(d_attn_all, w_out).astype(BF))
-    d_prob = jnp.einsum("sqhd,skhd->shqk", d_mix, values, preferred_element_type=F32)
-    row_delta = jnp.sum(prob * d_prob, axis=-1, keepdims=True)
-    d_scores = step((prob * (d_prob - row_delta)).astype(BF))
-    d_qrot = (
-        jnp.einsum("shqk,skhd->sqhd", d_scores, k_rot, preferred_element_type=F32) * score_scale
-    )
-    d_krot = (
-        jnp.einsum("shqk,sqhd->skhd", d_scores, q_rot, preferred_element_type=F32) * score_scale
-    )
-    d_value = jnp.einsum("shqk,sqhd->skhd", prob_low, d_mix, preferred_element_type=F32)
-    d_qn = joined(rotate_pairs(d_qrot, cos_table, -sin_table))
-    d_kn = joined(rotate_pairs(d_krot, cos_table, -sin_table))
-    d_value = joined(d_value.astype(BF))
+    d_mix = step(in_rows(through(d_attn_all, w_out).astype(BF)))
+    d_qn, d_kn, d_value = over_heads(
+        attend_back_kernel, live_len, seq_len, (F32, F32, BF),
+        q_rot, k_rot, values, d_mix, cos_table, sin_table, *place_tables,
+    )
+    d_qn, d_kn, d_value = joined(d_qn), joined(d_kn), joined(d_value)
     d_q_hat = d_qn * q_gain_f
     d_k_hat = d_kn * k_gain_f
     d_q_hat, d_k_hat, d_value = step((d_q_hat, d_k_hat, d_value))
@@ -534,21 +573,6 @@
         (through(d_query, w_query) + through(d_key, w_key) + through(d_value, w_value)).astype(BF)
     )
     d_inputs = d_hidden + plane.scatter(partial)
-    while len(waiting) > 1:
-        step(())
-    line.placed, d_inputs, result_late = together(line.placed, d_inputs, result)
-
-    def home(array):
-        own = plane.relative((array).astype(BF)).reshape(seq_own, tok_seq, width)
-        pieces = [own] + [plane.hop(own, 0, k) for k in range(1, cols)]
-        out = jnp.zeros((seq_grp, tok_seq, width), BF)
-        for k in range(cols):
-            out = lax.dynamic_update_slice_in_dim(out, pieces[k], (col ^ k) * seq_own, axis=0)
-        return out
-
-    output = home(result_late)
-    grad_input = home(d_inputs * valid_rows)
-
     def sums_of(array):
         return jnp.sum(array.reshape(seq_own, tok_seq * width), axis=1)
 
@@ -587,6 +611,21 @@
     while col_xor < cols:
         vector = vector + plane.hop(vector, 0, col_xor)
         col_xor *= 2
+    waiting[-rows] = jnp.concatenate([waiting[-rows], vector.astype(BF)], axis=0)
+    while waiting:
+        step(())
+    line.placed, d_inputs, result_late = together(line.placed, d_inputs, result)
+
+    def home(array):
+        own = plane.relative((array).astype(BF)).reshape(seq_own, tok_seq, width)
+        pieces = [own] + [plane.hop(own, 0, k) for k in range(1, cols)]
+        out = jnp.zeros((seq_grp, tok_seq, width), BF)
+        for k in range(cols):
+            out = lax.dynamic_update_slice_in_dim(out, pieces[k], (col ^ k) * seq_own, axis=0)
+        return out
+
+    output = home(result_late)
+    grad_input = home(d_inputs * valid_rows)
 
     def finish(blocks, axis):
         size = blocks[0].shape[axis]
@@ -602,9 +641,8 @@
     def arrived_at(placed):
         return [placed[order.index(k)] for k in range(rows)]
 
-    line.step((), jnp.concatenate([waiting.pop(0), vector.astype(BF)], axis=0))
     placed = line.finish()
-    placed[-1], vector = placed[-1]
+    placed[4 + 2 * rows], vector = placed[4 + 2 * rows]
     vector = vector.astype(F32).reshape(-1)
     grad_down = [placed[2] + placed[0], placed[3] + placed[1]]
     grad_down = finish([jnp.concatenate(both, axis=0) for both in zip(*grad_down, strict=True)], 0)

time: 933 us -> 924 us (level)
  local copies, waits for them, and re-layouts: 132 us -> 113 us
  Pallas kernels: 0 us -> 16.9 us
  matrix products: 116 us -> 102 us
    ppermute x20, waiting for transfers between devices: 83 us -> 24.3 us  [hop(): lax.ppermute(array, 'col', [(a, a ^ col_xor) for a in range(self.cols)])]
    ppermute x74, waiting for transfers between devices: 120 us -> 164 us  [hop(): lax.ppermute(array, 'row', [(a, a ^ row_xor) for a in range(self.rows)])]
    ppermute x5, waiting for transfers between devices: 15 us -> 46.1 us  [advance(): current['inward'] = lax.ppermute(array, 'dp', [(0, 1), (3, 2)])]
    all_gather x2, waiting for transfers between devices: 25.3 us -> 0.01 us  [over_groups(): return lax.all_gather(part, 'dp', axis=0, tiled=True)]
    unnamed x416 -> x390, local copies, waits for them, and re-layouts: 59.7 us -> 37.5 us
    pallas_call x0 -> x2, Pallas kernels: none -> 16.9 us  [over_heads(): pl.pallas_call(kernel, out_shape=tuple((jax.ShapeDtypeStruct((tokens, fea...]
  transfers between devices with their start and end apart: 133 -> 133, of which waited for: 53 -> 52; matrix products, arithmetic and copies ran while one was open for 33% -> 31% of each run, Pallas kernels for 0% -> 2%
where the time goes in v4:
time: 924 us; the launch traced here: 912 us
  waiting for transfers between devices  344 us (37%)
  starting transfers between devices  172 us (19%)
  other arithmetic  146 us (16%)
  local copies, waits for them, and re-layouts  113 us (12%)
  matrix products  102 us (11%)
  between operations  18 us (2%)
  Pallas kernels  16.9 us (2%)
    ppermute x74, waiting for transfers between devices, hop(): lax.ppermute(array, 'row', [(a, a ^ row_xor) for a in range(self.rows)])  164 us
    ppermute x11, waiting for transfers between devices, advance(): current['inward'] = lax.ppermute(sent, 'dp', ENDS)  64.9 us
    ppermute x74, starting transfers between devices, hop(): lax.ppermute(array, 'row', [(a, a ^ row_xor) for a in range(self.rows)])  51 us
    ppermute x11, starting transfers between devices, advance(): current['inward'] = lax.ppermute(sent, 'dp', ENDS)  48.4 us
    ppermute x5, waiting for transfers between devices, advance(): current['inward'] = lax.ppermute(array, 'dp', [(0, 1), (3, 2)])  46.1 us
    ppermute x5, waiting for transfers between devices, advance(): current['back'] = lax.ppermute(back, 'dp', [(1, 0), (2, 3)])  44.3 us
    dot_general x7, matrix products, through(): lax.dot_general(left_side, weight, (((1,), (1,)), ((), ())), preferred_el...  39.4 us
    unnamed x390, local copies, waits for them, and re-layouts  37.5 us
  transfers between devices with their start and end apart: 133, of which 52 were waited for; matrix products, arithmetic and copies ran while one was open for 31% of the time, Pallas kernels for 2%

profile of v4, /device:TPU:0, one launch (start us, length us, event | category | flops | bytes accessed | tf_op | source)
XLA Modules:
  0.0 912.3 jit_solution(200554578717267227)
XLA Ops:
  27.3 8.4 collective-permute-done.8
  48.0 6.7 collective-permute-done.11
  59.0 15.8 %collective-permute-done.6 = bf16[3,512,256]{2,1,0:T(8,128)(2,1)} collective-permute-done((bf16[3,512,256]{2,1,0:T(8,128)(2,1)}, bf16[3,512,256]{2,1,0:T(8,128)(2,1)}, u32[]{:S(2)}, u32[]{:S(2)}) %collective-permute-start.6) | collective-permute-done | bytes 786464 | tf_op jit(solution)/shard_map/ppermute | solution.py:126
  90.1 10.1 %collective-permute-done.14 = f32[2,2,4,128]{3,2,1,0:T(4,128)S(1)} collective-permute-done((f32[2,2,4,128]{3,2,1,0:T(4,128)S(1)}, f32[2,2,4,128]{3,2,1,0:T(4,128)S(1)}, u32[]{:S(2)}, u32[]{:S(2)}) %collective-permute-start.14) | collective-permute-done | bytes 8224 | tf_op jit(solution)/shard_map/ppermute | solution.py:126
  113.2 3.9 constant_dynamic-slice_fusion.23
  117.1 4.6 collective-permute-done.18
  129.7 18.7 %collective-permute-done.20 = bf16[1024,512]{1,0:T(8,128)(2,1)S(1)} collective-permute-done((bf16[1024,512]{1,0:T(8,128)(2,1)S(1)}, bf16[1024,512]{1,0:T(8,128)(2,1)S(1)}, u32[]{:S(2)}, u32[]{:S(2)}) %collective-permute-start.20) | collective-permute-done | bytes 1048608 | tf_op jit(solution)/shard_map/ppermute | solution.py:126
  152.2 7.9 shard_map.254
  160.2 8.9 collective-permute-done.21
  169.1 2.6 convolution_convert_fusion
  181.0 11.3 %collective-permute-done.23 = bf16[2,64,2048]{2,1,0:T(8,128)(2,1)S(1)} collective-permute-done((bf16[2,64,2048]{2,1,0:T(8,128)(2,1)S(1)}, bf16[2,64,2048]{2,1,0:T(8,128)(2,1)S(1)}, u32[]{:S(2)}, u32[]{:S(2)}) %collective-permute-start.23) | collective-permute-done | bytes 524320 | tf_op jit(solution)/shard_map/ppermute | solution.py:126
  195.5 3.9 collective-permute-done.24
  204.8 8.8 collective-permute-done.31
  220.8 6.6 collective-permute-done.36
  229.8 4.5 fusion.81
  234.4 6.6 multiply_convert_fusion.2
  241.0 4.7 convolution_convert_fusion.1
  247.4 3.2 collective-permute-done.40
  250.5 2.9 fusion.153
  260.2 8.5 collective-permute-done.41
  272.9 2.8 collective-permute-start.44
  277.6 2.6 collective-permute-done.44
  290.0 7.7 collective-permute-done.46
  307.0 3.3 collective-permute-done.51
  317.7 3.0 fusion.34
  326.5 3.6 collective-permute-start.53
  330.2 10.2 %multiply_convert_fusion = (bf16[1024,1024]{1,0:T(8,128)(2,1)S(1)}, bf16[1024,1024]{1,0:T(8,128)(2,1)S(1)}) fusion(f32[1024,1024]{1,0:T(8,128)} %copy-done.176, f32[1024,1024]{1,0:T(8,128)} %get-tuple-element.626, bf16[1024,2048]{1,0:T(8,128)(2,1)} %constant_dynamic-update-slice_fusion.29, bf16[1024,2048]{1,0:T(8,128)(2,1)S(1)} %copy-done.133), kind=kOutput, calls=%fused_computation.13 | convolution fusion | flops 4308598784 | bytes 20971520 | tf_op jit(solution)/shard_map/dot_general | solution.py:96
  340.4 12.7 %collective-permute-done.53 = bf16[512,1024]{1,0:T(8,128)(2,1)S(1)} collective-permute-done((bf16[512,1024]{1,0:T(8,128)(2,1)S(1)}, bf16[512,1024]{1,0:T(8,128)(2,1)S(1)}, u32[]{:S(2)}, u32[]{:S(2)}) %collective-permute-start.53) | collective-permute-done | bytes 1048608 | tf_op jit(solution)/shard_map/ppermute | solution.py:301
  357.7 5.6 collective-permute-start.54
  363.3 9.6 %fusion.79 = f32[1024,2048]{1,0:T(8,128)} fusion(bf16[1024,1024]{1,0:T(8,128)(2,1)S(1)} %get-tuple-element.202, bf16[512,1024]{1,0:T(8,128)(2,1)S(1)} %copy-done.118, bf16[512,1024]{1,0:T(8,128)(2,1)S(1)} %copy-done.116, bf16[512,1024]{1,0:T(8,128)(2,1)S(1)} %copy-done.169, bf16[512,1024]{1,0:T(8,128)(2,1)S(1)} %copy-done.71), kind=kOutput, calls=%fused_computation.256 | convolution fusion | flops 4311744512 | bytes 14680064 | tf_op jit(solution)/shard_map/dot_general | solution.py:96
  372.8 10.9 %add_convert_fusion.1 = bf16[1024,2048]{1,0:T(8,128)(2,1)} fusion(f32[1024,2048]{1,0:T(8,128)} %fusion.79, bf16[1024,1024]{1,0:T(8,128)(2,1)S(1)} %get-tuple-element.201, bf16[512,1024]{1,0:T(8,128)(2,1)} %copy-done.114, bf16[512,1024]{1,0:T(8,128)(2,1)} %copy-done.113, bf16[512,1024]{1,0:T(8,128)(2,1)} %copy-done.167, bf16[512,1024]{1,0:T(8,128)(2,1)S(1)} %copy-done.69), kind=kOutput, calls=%fused_computation.1 | convolution fusion | flops 4315938816 | bytes 18874368 | tf_op jit(solution)/shard_map/dot_general | solution.py:96
  390.2 4.7 collective-permute-start.55
  403.0 15.1 %collective-permute-done.55 = bf16[512,1024]{1,0:T(8,128)(2,1)S(1)} collective-permute-done((bf16[512,1024]{1,0:T(8,128)(2,1)}, bf16[512,1024]{1,0:T(8,128)(2,1)S(1)}, u32[]{:S(2)}, u32[]{:S(2)}) %collective-permute-start.55) | collective-permute-done | bytes 1048608 | tf_op jit(solution)/shard_map/ppermute | solution.py:301
  419.0 4.3 collective-permute-start.58
  429.9 15.7 %collective-permute-done.58 = bf16[512,1024]{1,0:T(8,128)(2,1)S(1)} collective-permute-done((bf16[512,1024]{1,0:T(8,128)(2,1)S(1)}, bf16[512,1024]{1,0:T(8,128)(2,1)S(1)}, u32[]{:S(2)}, u32[]{:S(2)}) %collective-permute-start.58) | collective-permute-done | bytes 1048608 | tf_op jit(solution)/shard_map/ppermute | solution.py:301
  447.5 2.6 add_convert_fusion.29
  453.3 4.1 collective-permute-start.67
  497.0 4.9 collective-permute-done.74
  507.2 3.3 collective-permute-start.81
  518.4 3.1 fusion.39
  521.5 3.3 convolution_convert_fusion.14.d_mix
  524.8 11.5 %collective-permute-start.77 = (bf16[512,1024]{1,0:T(8,128)(2,1)}, bf16[512,1024]{1,0:T(8,128)(2,1)}, u32[]{:S(2)}, u32[]{:S(2)}) collective-permute-start(bf16[512,1024]{1,0:T(8,128)(2,1)} %fusion.39), channel_id=1, source_target_pairs={{0,8},{8,0},{16,24},{24,16},{1,9},{9,1},{17,25},{25,17},{2,10},{10... | collective-permute-start | bytes 3145736 | tf_op jit(solution)/shard_map/ppermute | solution.py:297
  537.3 8.9 shard_map.255
  566.6 3.2 fusion.42
  571.9 10.5 %collective-permute-done.87 = f32[2,2,4,128]{3,2,1,0:T(4,128)S(1)} collective-permute-done((f32[2,2,4,128]{3,2,1,0:T(4,128)S(1)}, f32[2,2,4,128]{3,2,1,0:T(4,128)S(1)}, u32[]{:S(2)}, u32[]{:S(2)}) %collective-permute-start.87) | collective-permute-done | bytes 8224 | tf_op jit(solution)/shard_map/ppermute | solution.py:126
  611.0 2.6 add_convert_fusion.19
  613.6 2.8 add_convert_fusion
  626.7 3.6 collective-permute-done.97
  643.4 14.2 %collective-permute-done.93 = bf16[512,1024]{1,0:T(8,128)(2,1)S(1)} collective-permute-done((bf16[512,1024]{1,0:T(8,128)(2,1)S(1)}, bf16[512,1024]{1,0:T(8,128)(2,1)S(1)}, u32[]{:S(2)}, u32[]{:S(2)}) %collective-permute-start.93) | collective-permute-done | bytes 1048608 | tf_op jit(solution)/shard_map/ppermute | solution.py:297
  661.7 15.3 %collective-permute-done.99 = bf16[512,1024]{1,0:T(8,128)(2,1)S(1)} collective-permute-done((bf16[512,1024]{1,0:T(8,128)(2,1)S(1)}, bf16[512,1024]{1,0:T(8,128)(2,1)S(1)}, u32[]{:S(2)}, u32[]{:S(2)}) %collective-permute-start.99) | collective-permute-done | bytes 1048608 | tf_op jit(solution)/shard_map/ppermute | solution.py:297
  677.0 7.5 collective-permute-start.103
  686.6 17.1 %collective-permute-start.106 = (bf16[512,1024]{1,0:T(8,128)(2,1)S(1)}, bf16[512,1024]{1,0:T(8,128)(2,1)S(1)}, u32[]{:S(2)}, u32[]{:S(2)}) collective-permute-start(bf16[512,1024]{1,0:T(8,128)(2,1)S(1)} %fusion.45), channel_id=1, source_target_pairs={{0,8},{8,0},{16,24},{24,16},{1,9},{9,1},{17,25},{25,17},{2,10},{10... | collective-permute-start | bytes 3145736 | tf_op jit(solution)/shard_map/ppermute | solution.py:297
  711.1 12.9 %collective-permute-done.106 = bf16[512,1024]{1,0:T(8,128)(2,1)S(1)} collective-permute-done((bf16[512,1024]{1,0:T(8,128)(2,1)S(1)}, bf16[512,1024]{1,0:T(8,128)(2,1)S(1)}, u32[]{:S(2)}, u32[]{:S(2)}) %collective-permute-start.106) | collective-permute-done | bytes 1048608 | tf_op jit(solution)/shard_map/ppermute | solution.py:297
  727.5 15.9 %collective-permute-done.108 = bf16[2,64,2048]{2,1,0:T(8,128)(2,1)S(1)} collective-permute-done((bf16[2,64,2048]{2,1,0:T(8,128)(2,1)S(1)}, bf16[2,64,2048]{2,1,0:T(8,128)(2,1)S(1)}, u32[]{:S(2)}, u32[]{:S(2)}) %collective-permute-start.108) | collective-permute-done | bytes 524320 | tf_op jit(solution)/shard_map/ppermute | solution.py:126
  747.8 3.7 collective-permute-done.109
  752.5 2.6 collective-permute-start.120
  768.4 20.6 %collective-permute-done.120 = bf16[512,1024]{1,0:T(8,128)(2,1)S(1)} collective-permute-done((bf16[512,1024]{1,0:T(8,128)(2,1)S(1)}, bf16[512,1024]{1,0:T(8,128)(2,1)S(1)}, u32[]{:S(2)}, u32[]{:S(2)}) %collective-permute-start.120) | collective-permute-done | bytes 1048608 | tf_op jit(solution)/shard_map/ppermute | solution.py:297
  794.2 4.4 broadcast.334.clone
  802.5 10.9 %collective-permute-done.118 = bf16[528,1024]{1,0:T(8,128)(2,1)S(1)} collective-permute-done((bf16[528,1024]{1,0:T(8,128)(2,1)S(1)}, bf16[528,1024]{1,0:T(8,128)(2,1)S(1)}, u32[]{:S(2)}, u32[]{:S(2)}) %collective-permute-start.118) | collective-permute-done | bytes 1081376 | tf_op jit(solution)/shard_map/ppermute | solution.py:304
  825.9 2.8 convert_dynamic-update-slice_fusion.5
  828.7 3.9 convert_dynamic-update-slice_fusion.4
  834.3 10.4 %collective-permute-done.115 = bf16[512,1024]{1,0:T(8,128)(2,1)S(1)} collective-permute-done((bf16[512,1024]{1,0:T(8,128)(2,1)S(1)}, bf16[512,1024]{1,0:T(8,128)(2,1)S(1)}, u32[]{:S(2)}, u32[]{:S(2)}) %collective-permute-start.115) | collective-permute-done | bytes 1048608 | tf_op jit(solution)/shard_map/ppermute | solution.py:304
  852.6 14.4 %collective-permute-done.122 = bf16[512,1024]{1,0:T(8,128)(2,1)} collective-permute-done((bf16[512,1024]{1,0:T(8,128)(2,1)S(1)}, bf16[512,1024]{1,0:T(8,128)(2,1)}, u32[]{:S(2)}, u32[]{:S(2)}) %collective-permute-start.122) | collective-permute-done | bytes 1048608 | tf_op jit(solution)/shard_map/ppermute | solution.py:304
  889.8 8.7 collective-permute-done.126
  (973 shorter events, 403.9 us)
Async XLA Ops:
  7.2 67.7 %all-gather.3.cloned.1.call-start = ((), (), s32[]{:S(2)}) async-start(), calls=%async_computation | async-start | bytes 2621440 | tf_op jit(solution)/shard_map/all_gather | solution.py:390
  16.7 23.7 %collective-permute-start.7 = (bf16[128,2048]{1,0:T(8,128)(2,1)}, bf16[128,2048]{1,0:T(8,128)(2,1)}, u32[]{:S(2)}, u32[]{:S(2)}) collective-permute-start(bf16[128,2048]{1,0:T(8,128)(2,1)} %pad_maximum_fusion.23), channel_id=1, source_target_pairs={{0,2},{2,0},{4,6},{6,4},{1,3},{3,1},{5,7},{7,5},{8,10},{10,8},{12,... | collective-permute-start | bytes 1572872 | tf_op jit(solution)/shard_map/ppermute | solution.py:126
  27.3 141.8 %all-gather.5.cloned.1.call-start = ((), (), s32[]{:S(2)}) async-start(), calls=%async_computation.1 | async-start | bytes 2621440 | tf_op jit(solution)/shard_map/all_gather | solution.py:390
  37.6 20.0 %collective-permute-start.4 = (bf16[3,512,256]{2,1,0:T(8,128)(2,1)}, bf16[3,512,256]{2,1,0:T(8,128)(2,1)S(1)}, u32[]{:S(2)}, u32[]{:S(2)}) collective-permute-start(bf16[3,512,256]{2,1,0:T(8,128)(2,1)} %pad_maximum_fusion.16), channel_id=1, source_target_pairs={{0,2},{2,0},{4,6},{6,4},{1,3},{3,1},{5,7},{7,5},{8,10},{10,8},{12,... | collective-permute-start | bytes 2359304 | tf_op jit(solution)/shard_map/ppermute | solution.py:126
  38.1 20.9 %collective-permute-start.5 = (bf16[3,512,256]{2,1,0:T(8,128)(2,1)}, bf16[3,512,256]{2,1,0:T(8,128)(2,1)}, u32[]{:S(2)}, u32[]{:S(2)}) collective-permute-start(bf16[3,512,256]{2,1,0:T(8,128)(2,1)} %pad_maximum_fusion.13), channel_id=1, source_target_pairs={{0,4},{2,6},{4,0},{6,2},{1,5},{3,7},{5,1},{7,3},{8,12},{10,14},{12... | collective-permute-start | bytes 2359304 | tf_op jit(solution)/shard_map/ppermute | solution.py:126
  40.4 34.4 %collective-permute-start.6 = (bf16[3,512,256]{2,1,0:T(8,128)(2,1)}, bf16[3,512,256]{2,1,0:T(8,128)(2,1)}, u32[]{:S(2)}, u32[]{:S(2)}) collective-permute-start(bf16[3,512,256]{2,1,0:T(8,128)(2,1)} %pad_maximum_fusion.14), channel_id=1, source_target_pairs={{0,6},{2,4},{4,2},{6,0},{1,7},{3,5},{5,3},{7,1},{8,14},{10,12},{12... | collective-permute-start | bytes 2359304 | tf_op jit(solution)/shard_map/ppermute | solution.py:126
  122.4 26.0 %collective-permute-start.20 = (bf16[1024,512]{1,0:T(8,128)(2,1)S(1)}, bf16[1024,512]{1,0:T(8,128)(2,1)S(1)}, u32[]{:S(2)}, u32[]{:S(2)}) collective-permute-start(bf16[1024,512]{1,0:T(8,128)(2,1)S(1)} %get-tuple-element.175), channel_id=1, source_target_pairs={{0,4},{2,6},{4,0},{6,2},{1,5},{3,7},{5,1},{7,3},{8,12},{10,14},{12... | collective-permute-start | bytes 3145736 | tf_op jit(solution)/shard_map/ppermute | solution.py:126
  124.7 44.4 %collective-permute-start.21 = (bf16[1024,512]{1,0:T(8,128)(2,1)}, bf16[1024,512]{1,0:T(8,128)(2,1)}, u32[]{:S(2)}, u32[]{:S(2)}) collective-permute-start(bf16[1024,512]{1,0:T(8,128)(2,1)} %get-tuple-element.179), channel_id=1, source_target_pairs={{0,6},{2,4},{4,2},{6,0},{1,7},{3,5},{5,3},{7,1},{8,14},{10,12},{12... | collective-permute-start | bytes 3145736 | tf_op jit(solution)/shard_map/ppermute | solution.py:126
  175.4 54.3 %collective-permute-start.38 = (bf16[512,1024]{1,0:T(8,128)(2,1)S(1)}, bf16[512,1024]{1,0:T(8,128)(2,1)S(1)}, u32[]{:S(2)}, u32[]{:S(2)}) collective-permute-start(bf16[512,1024]{1,0:T(8,128)(2,1)S(1)} %get-tuple-element.367), channel_id=1, source_target_pairs={{0,2},{2,0},{4,6},{6,4},{1,3},{3,1},{5,7},{7,5},{8,10},{10,8},{12,... | collective-permute-start | bytes 3145736 | tf_op jit(solution)/shard_map/ppermute | solution.py:126
  176.3 58.0 %collective-permute-start.39 = (bf16[512,1024]{1,0:T(8,128)(2,1)S(1)}, bf16[512,1024]{1,0:T(8,128)(2,1)S(1)}, u32[]{:S(2)}, u32[]{:S(2)}) collective-permute-start(bf16[512,1024]{1,0:T(8,128)(2,1)S(1)} %get-tuple-element.369), channel_id=1, source_target_pairs={{0,2},{2,0},{4,6},{6,4},{1,3},{3,1},{5,7},{7,5},{8,10},{10,8},{12,... | collective-permute-start | bytes 3145736 | tf_op jit(solution)/shard_map/ppermute | solution.py:126
  326.5 26.6 %collective-permute-start.53 = (bf16[512,1024]{1,0:T(8,128)(2,1)S(1)}, bf16[512,1024]{1,0:T(8,128)(2,1)S(1)}, u32[]{:S(2)}, u32[]{:S(2)}) collective-permute-start(bf16[512,1024]{1,0:T(8,128)(2,1)S(1)} %fusion.34), channel_id=1, source_target_pairs={{0,8},{24,16},{1,9},{25,17},{2,10},{26,18},{3,11},{27,19},{4,12},{... | collective-permute-start | bytes 3145736 | tf_op jit(solution)/shard_map/ppermute | solution.py:301
  357.7 26.8 %collective-permute-start.54 = (bf16[512,1024]{1,0:T(8,128)(2,1)S(1)}, bf16[512,1024]{1,0:T(8,128)(2,1)}, u32[]{:S(2)}, u32[]{:S(2)}) collective-permute-start(bf16[512,1024]{1,0:T(8,128)(2,1)S(1)} %fusion.31), channel_id=1, source_target_pairs={{0,8},{24,16},{1,9},{25,17},{2,10},{26,18},{3,11},{27,19},{4,12},{... | collective-permute-start | bytes 3145736 | tf_op jit(solution)/shard_map/ppermute | solution.py:301
  386.6 31.5 %collective-permute-start.56 = (bf16[2,2,128,2048]{3,2,1,0:T(8,128)(2,1)S(1)}, bf16[2,2,128,2048]{3,2,1,0:T(8,128)(2,1)S(1)}, u32[]{:S(2)}, u32[]{:S(2)}) collective-permute-start(bf16[2,2,128,2048]{3,2,1,0:T(8,128)(2,1)S(1)} %fusion.14), channel_id=1, source_target_pairs={{0,2},{2,0},{4,6},{6,4},{1,3},{3,1},{5,7},{7,5},{8,10},{10,8},{12,... | collective-permute-start | bytes 6291464 | tf_op jit(solution)/shard_map/ppermute | solution.py:126
  390.2 27.9 %collective-permute-start.55 = (bf16[512,1024]{1,0:T(8,128)(2,1)}, bf16[512,1024]{1,0:T(8,128)(2,1)S(1)}, u32[]{:S(2)}, u32[]{:S(2)}) collective-permute-start(bf16[512,1024]{1,0:T(8,128)(2,1)} %fusion.25), channel_id=1, source_target_pairs={{0,8},{24,16},{1,9},{25,17},{2,10},{26,18},{3,11},{27,19},{4,12},{... | collective-permute-start | bytes 3145736 | tf_op jit(solution)/shard_map/ppermute | solution.py:301
  402.1 43.5 %collective-permute-start.59 = (bf16[512,1024]{1,0:T(8,128)(2,1)S(1)}, bf16[512,1024]{1,0:T(8,128)(2,1)S(1)}, u32[]{:S(2)}, u32[]{:S(2)}) collective-permute-start(bf16[512,1024]{1,0:T(8,128)(2,1)S(1)} %add_convert_fusion.32), channel_id=1, source_target_pairs={{8,16},{16,8},{9,17},{17,9},{10,18},{18,10},{11,19},{19,11},{12,20... | collective-permute-start | bytes 3145736 | tf_op jit(solution)/shard_map/ppermute | solution.py:287
  419.0 26.6 %collective-permute-start.58 = (bf16[512,1024]{1,0:T(8,128)(2,1)S(1)}, bf16[512,1024]{1,0:T(8,128)(2,1)S(1)}, u32[]{:S(2)}, u32[]{:S(2)}) collective-permute-start(bf16[512,1024]{1,0:T(8,128)(2,1)S(1)} %copy-done.72), channel_id=1, source_target_pairs={{0,8},{24,16},{1,9},{25,17},{2,10},{26,18},{3,11},{27,19},{4,12},{... | collective-permute-start | bytes 3145736 | tf_op jit(solution)/shard_map/ppermute | solution.py:301
  423.4 22.2 %collective-permute-start.60 = (bf16[2,64,2048]{2,1,0:T(8,128)(2,1)S(1)}, bf16[2,64,2048]{2,1,0:T(8,128)(2,1)S(1)}, u32[]{:S(2)}, u32[]{:S(2)}) collective-permute-start(bf16[2,64,2048]{2,1,0:T(8,128)(2,1)S(1)} %pad_maximum_fusion.43), channel_id=1, source_target_pairs={{0,4},{2,6},{4,0},{6,2},{1,5},{3,7},{5,1},{7,3},{8,12},{10,14},{12... | collective-permute-start | bytes 1572872 | tf_op jit(solution)/shard_map/ppermute | solution.py:126
  423.9 21.7 %collective-permute-start.61 = (bf16[2,64,2048]{2,1,0:T(8,128)(2,1)S(1)}, bf16[2,64,2048]{2,1,0:T(8,128)(2,1)S(1)}, u32[]{:S(2)}, u32[]{:S(2)}) collective-permute-start(bf16[2,64,2048]{2,1,0:T(8,128)(2,1)S(1)} %pad_maximum_fusion.44), channel_id=1, source_target_pairs={{0,1},{1,0},{2,3},{3,2},{4,5},{5,4},{6,7},{7,6},{8,9},{9,8},{10,11... | collective-permute-start | bytes 1572872 | tf_op jit(solution)/shard_map/ppermute | solution.py:128
  429.1 28.6 %collective-permute-start.57 = (bf16[512,1024]{1,0:T(8,128)(2,1)S(1)}, bf16[512,1024]{1,0:T(8,128)(2,1)S(1)}, u32[]{:S(2)}, u32[]{:S(2)}) collective-permute-start(bf16[512,1024]{1,0:T(8,128)(2,1)S(1)} %add_convert_fusion.33), channel_id=1, source_target_pairs={{8,16},{16,8},{9,17},{17,9},{10,18},{18,10},{11,19},{19,11},{12,20... | collective-permute-start | bytes 3145736 | tf_op jit(solution)/shard_map/ppermute | solution.py:287
  450.1 29.1 %collective-permute-start.66 = (bf16[512,1024]{1,0:T(8,128)(2,1)}, bf16[512,1024]{1,0:T(8,128)(2,1)}, u32[]{:S(2)}, u32[]{:S(2)}) collective-permute-start(bf16[512,1024]{1,0:T(8,128)(2,1)} %add_convert_fusion.29), channel_id=1, source_target_pairs={{8,16},{16,8},{9,17},{17,9},{10,18},{18,10},{11,19},{19,11},{12,20... | collective-permute-start | bytes 3145736 | tf_op jit(solution)/shard_map/ppermute | solution.py:287
  453.3 27.6 %collective-permute-start.67 = (bf16[512,1024]{1,0:T(8,128)(2,1)}, bf16[512,1024]{1,0:T(8,128)(2,1)}, u32[]{:S(2)}, u32[]{:S(2)}) collective-permute-start(bf16[512,1024]{1,0:T(8,128)(2,1)} %fusion.38), channel_id=1, source_target_pairs={{0,8},{8,0},{16,24},{24,16},{1,9},{9,1},{17,25},{25,17},{2,10},{10... | collective-permute-start | bytes 3145736 | tf_op jit(solution)/shard_map/ppermute | solution.py:297
  463.7 43.5 %collective-permute-start.64 = (bf16[512,1024]{1,0:T(8,128)(2,1)}, bf16[512,1024]{1,0:T(8,128)(2,1)}, u32[]{:S(2)}, u32[]{:S(2)}) collective-permute-start(bf16[512,1024]{1,0:T(8,128)(2,1)} %add_convert_fusion.31), channel_id=1, source_target_pairs={{8,16},{16,8},{9,17},{17,9},{10,18},{18,10},{11,19},{19,11},{12,20... | collective-permute-start | bytes 3145736 | tf_op jit(solution)/shard_map/ppermute | solution.py:287
  478.0 32.6 %collective-permute-start.65 = (bf16[512,1024]{1,0:T(8,128)(2,1)S(1)}, bf16[512,1024]{1,0:T(8,128)(2,1)S(1)}, u32[]{:S(2)}, u32[]{:S(2)}) collective-permute-start(bf16[512,1024]{1,0:T(8,128)(2,1)S(1)} %fusion.37), channel_id=1, source_target_pairs={{0,8},{8,0},{16,24},{24,16},{1,9},{9,1},{17,25},{25,17},{2,10},{10... | collective-permute-start | bytes 3145736 | tf_op jit(solution)/shard_map/ppermute | solution.py:297
  495.2 61.2 %collective-permute-start.78 = (bf16[512,512]{1,0:T(8,128)(2,1)}, bf16[512,512]{1,0:T(8,128)(2,1)}, u32[]{:S(2)}, u32[]{:S(2)}) collective-permute-start(bf16[512,512]{1,0:T(8,128)(2,1)} %get-tuple-element.427), channel_id=1, source_target_pairs={{0,4},{2,6},{4,0},{6,2},{1,5},{3,7},{5,1},{7,3},{8,12},{10,14},{12... | collective-permute-start | bytes 1572872 | tf_op jit(solution)/shard_map/ppermute | solution.py:126
  496.0 62.1 %collective-permute-start.79 = (bf16[512,512]{1,0:T(8,128)(2,1)}, bf16[512,512]{1,0:T(8,128)(2,1)}, u32[]{:S(2)}, u32[]{:S(2)}) collective-permute-start(bf16[512,512]{1,0:T(8,128)(2,1)} %get-tuple-element.426), channel_id=1, source_target_pairs={{0,6},{2,4},{4,2},{6,0},{1,7},{3,5},{5,3},{7,1},{8,14},{10,12},{12... | collective-permute-start | bytes 1572872 | tf_op jit(solution)/shard_map/ppermute | solution.py:126
  507.2 29.1 %collective-permute-start.81 = (bf16[512,1024]{1,0:T(8,128)(2,1)S(1)}, bf16[512,1024]{1,0:T(8,128)(2,1)S(1)}, u32[]{:S(2)}, u32[]{:S(2)}) collective-permute-start(bf16[512,1024]{1,0:T(8,128)(2,1)S(1)} %fusion.40), channel_id=1, source_target_pairs={{0,8},{8,0},{16,24},{24,16},{1,9},{9,1},{17,25},{25,17},{2,10},{10... | collective-permute-start | bytes 3145736 | tf_op jit(solution)/shard_map/ppermute | solution.py:297
  515.5 44.1 %collective-permute-start.76 = (bf16[512,1024]{1,0:T(8,128)(2,1)}, bf16[512,1024]{1,0:T(8,128)(2,1)}, u32[]{:S(2)}, u32[]{:S(2)}) collective-permute-start(bf16[512,1024]{1,0:T(8,128)(2,1)} %add_convert_fusion.27), channel_id=1, source_target_pairs={{8,16},{16,8},{9,17},{17,9},{10,18},{18,10},{11,19},{19,11},{12,20... | collective-permute-start | bytes 3145736 | tf_op jit(solution)/shard_map/ppermute | solution.py:287
  524.8 34.9 %collective-permute-start.77 = (bf16[512,1024]{1,0:T(8,128)(2,1)}, bf16[512,1024]{1,0:T(8,128)(2,1)}, u32[]{:S(2)}, u32[]{:S(2)}) collective-permute-start(bf16[512,1024]{1,0:T(8,128)(2,1)} %fusion.39), channel_id=1, source_target_pairs={{0,8},{8,0},{16,24},{24,16},{1,9},{9,1},{17,25},{25,17},{2,10},{10... | collective-permute-start | bytes 3145736 | tf_op jit(solution)/shard_map/ppermute | solution.py:297
  549.5 46.7 %collective-permute-start.82 = (bf16[512,1024]{1,0:T(8,128)(2,1)}, bf16[512,1024]{1,0:T(8,128)(2,1)}, u32[]{:S(2)}, u32[]{:S(2)}) collective-permute-start(bf16[512,1024]{1,0:T(8,128)(2,1)} %add_convert_fusion.23), channel_id=1, source_target_pairs={{8,16},{16,8},{9,17},{17,9},{10,18},{18,10},{11,19},{19,11},{12,20... | collective-permute-start | bytes 3145736 | tf_op jit(solution)/shard_map/ppermute | solution.py:287
  556.4 39.8 %collective-permute-start.83 = (bf16[512,1024]{1,0:T(8,128)(2,1)}, bf16[512,1024]{1,0:T(8,128)(2,1)}, u32[]{:S(2)}, u32[]{:S(2)}) collective-permute-start(bf16[512,1024]{1,0:T(8,128)(2,1)} %fusion.41), channel_id=1, source_target_pairs={{0,8},{8,0},{16,24},{24,16},{1,9},{9,1},{17,25},{25,17},{2,10},{10... | collective-permute-start | bytes 3145736 | tf_op jit(solution)/shard_map/ppermute | solution.py:297
  558.1 34.6 %collective-permute-start.84 = (bf16[512,512]{1,0:T(8,128)(2,1)}, bf16[512,512]{1,0:T(8,128)(2,1)}, u32[]{:S(2)}, u32[]{:S(2)}) collective-permute-start(bf16[512,512]{1,0:T(8,128)(2,1)} %get-tuple-element.425), channel_id=1, source_target_pairs={{0,4},{2,6},{4,0},{6,2},{1,5},{3,7},{5,1},{7,3},{8,12},{10,14},{12... | collective-permute-start | bytes 1572872 | tf_op jit(solution)/shard_map/ppermute | solution.py:126
  559.6 35.2 %collective-permute-start.85 = (bf16[512,512]{1,0:T(8,128)(2,1)}, bf16[512,512]{1,0:T(8,128)(2,1)}, u32[]{:S(2)}, u32[]{:S(2)}) collective-permute-start(bf16[512,512]{1,0:T(8,128)(2,1)} %get-tuple-element.424), channel_id=1, source_target_pairs={{0,6},{2,4},{4,2},{6,0},{1,7},{3,5},{5,3},{7,1},{8,14},{10,12},{12... | collective-permute-start | bytes 1572872 | tf_op jit(solution)/shard_map/ppermute | solution.py:126
  589.3 41.9 %collective-permute-start.91 = (bf16[512,512]{1,0:T(8,128)(2,1)}, bf16[512,512]{1,0:T(8,128)(2,1)}, u32[]{:S(2)}, u32[]{:S(2)}) collective-permute-start(bf16[512,512]{1,0:T(8,128)(2,1)} %get-tuple-element.422), channel_id=1, source_target_pairs={{0,2},{2,0},{4,6},{6,4},{1,3},{3,1},{5,7},{7,5},{8,10},{10,8},{12,... | collective-permute-start | bytes 1572872 | tf_op jit(solution)/shard_map/ppermute | solution.py:126
  592.7 40.8 %collective-permute-start.89 = (bf16[512,1024]{1,0:T(8,128)(2,1)}, bf16[512,1024]{1,0:T(8,128)(2,1)}, u32[]{:S(2)}, u32[]{:S(2)}) collective-permute-start(bf16[512,1024]{1,0:T(8,128)(2,1)} %add_convert_fusion.21), channel_id=1, source_target_pairs={{8,16},{16,8},{9,17},{17,9},{10,18},{18,10},{11,19},{19,11},{12,20... | collective-permute-start | bytes 3145736 | tf_op jit(solution)/shard_map/ppermute | solution.py:287
  594.8 40.5 %collective-permute-start.90 = (bf16[512,1024]{1,0:T(8,128)(2,1)}, bf16[512,1024]{1,0:T(8,128)(2,1)}, u32[]{:S(2)}, u32[]{:S(2)}) collective-permute-start(bf16[512,1024]{1,0:T(8,128)(2,1)} %fusion.42), channel_id=1, source_target_pairs={{0,8},{8,0},{16,24},{24,16},{1,9},{9,1},{17,25},{25,17},{2,10},{10... | collective-permute-start | bytes 3145736 | tf_op jit(solution)/shard_map/ppermute | solution.py:297
  596.2 45.3 %collective-permute-start.94 = (bf16[512,512]{1,0:T(8,128)(2,1)}, bf16[512,512]{1,0:T(8,128)(2,1)}, u32[]{:S(2)}, u32[]{:S(2)}) collective-permute-start(bf16[512,512]{1,0:T(8,128)(2,1)} %get-tuple-element.420), channel_id=1, source_target_pairs={{0,2},{2,0},{4,6},{6,4},{1,3},{3,1},{5,7},{7,5},{8,10},{10,8},{12,... | collective-permute-start | bytes 1572872 | tf_op jit(solution)/shard_map/ppermute | solution.py:126
  596.2 24.4 %collective-permute-start.95 = (f32[16,1024]{1,0:T(8,128)}, f32[16,1024]{1,0:T(8,128)}, u32[]{:S(2)}, u32[]{:S(2)}) collective-permute-start(f32[16,1024]{1,0:T(8,128)} %reshape.596), channel_id=1, source_target_pairs={{0,2},{2,0},{4,6},{6,4},{1,3},{3,1},{5,7},{7,5},{8,10},{10,8},{12,... | collective-permute-start | bytes 196616 | tf_op jit(solution)/shard_map/ppermute | solution.py:126
  631.2 26.5 %collective-permute-start.93 = (bf16[512,1024]{1,0:T(8,128)(2,1)S(1)}, bf16[512,1024]{1,0:T(8,128)(2,1)S(1)}, u32[]{:S(2)}, u32[]{:S(2)}) collective-permute-start(bf16[512,1024]{1,0:T(8,128)(2,1)S(1)} %fusion.43), channel_id=1, source_target_pairs={{0,8},{8,0},{16,24},{24,16},{1,9},{9,1},{17,25},{25,17},{2,10},{10... | collective-permute-start | bytes 3145736 | tf_op jit(solution)/shard_map/ppermute | solution.py:297
  633.6 26.1 %collective-permute-start.100 = (bf16[512,1024]{1,0:T(8,128)(2,1)S(1)}, bf16[512,1024]{1,0:T(8,128)(2,1)S(1)}, u32[]{:S(2)}, u32[]{:S(2)}) collective-permute-start(bf16[512,1024]{1,0:T(8,128)(2,1)S(1)} %broadcast_select_fusion.10), channel_id=1, source_target_pairs={{0,4},{2,6},{4,0},{6,2},{1,5},{3,7},{5,1},{7,3},{8,12},{10,14},{12... | collective-permute-start | bytes 3145736 | tf_op jit(solution)/shard_map/ppermute | solution.py:126
  637.0 23.4 %collective-permute-start.98 = (bf16[512,1024]{1,0:T(8,128)(2,1)S(1)}, bf16[512,1024]{1,0:T(8,128)(2,1)S(1)}, u32[]{:S(2)}, u32[]{:S(2)}) collective-permute-start(bf16[512,1024]{1,0:T(8,128)(2,1)S(1)} %add_convert_fusion.17), channel_id=1, source_target_pairs={{8,16},{16,8},{9,17},{17,9},{10,18},{18,10},{11,19},{19,11},{12,20... | collective-permute-start | bytes 3145736 | tf_op jit(solution)/shard_map/ppermute | solution.py:287
  641.4 35.6 %collective-permute-start.99 = (bf16[512,1024]{1,0:T(8,128)(2,1)S(1)}, bf16[512,1024]{1,0:T(8,128)(2,1)S(1)}, u32[]{:S(2)}, u32[]{:S(2)}) collective-permute-start(bf16[512,1024]{1,0:T(8,128)(2,1)S(1)} %fusion.44), channel_id=1, source_target_pairs={{0,8},{8,0},{16,24},{24,16},{1,9},{9,1},{17,25},{25,17},{2,10},{10... | collective-permute-start | bytes 3145736 | tf_op jit(solution)/shard_map/ppermute | solution.py:297
  643.4 42.5 %collective-permute-start.104 = (bf16[512,1024]{1,0:T(8,128)(2,1)S(1)}, bf16[512,1024]{1,0:T(8,128)(2,1)S(1)}, u32[]{:S(2)}, u32[]{:S(2)}) collective-permute-start(bf16[512,1024]{1,0:T(8,128)(2,1)S(1)} %broadcast_select_fusion.9), channel_id=1, source_target_pairs={{0,6},{2,4},{4,2},{6,0},{1,7},{3,5},{5,3},{7,1},{8,14},{10,12},{12... | collective-permute-start | bytes 3145736 | tf_op jit(solution)/shard_map/ppermute | solution.py:126
  657.6 50.8 %collective-permute-start.107 = (bf16[2,2,128,2048]{3,2,1,0:T(8,128)(2,1)S(1)}, bf16[2,2,128,2048]{3,2,1,0:T(8,128)(2,1)S(1)}, u32[]{:S(2)}, u32[]{:S(2)}) collective-permute-start(bf16[2,2,128,2048]{3,2,1,0:T(8,128)(2,1)S(1)} %fusion.16), channel_id=1, source_target_pairs={{0,2},{2,0},{4,6},{6,4},{1,3},{3,1},{5,7},{7,5},{8,10},{10,8},{12,... | collective-permute-start | bytes 6291464 | tf_op jit(solution)/shard_map/ppermute | solution.py:126
  659.7 26.9 %collective-permute-start.101 = (bf16[512,1024]{1,0:T(8,128)(2,1)S(1)}, bf16[512,1024]{1,0:T(8,128)(2,1)S(1)}, u32[]{:S(2)}, u32[]{:S(2)}) collective-permute-start(bf16[512,1024]{1,0:T(8,128)(2,1)S(1)} %add_convert_fusion.15), channel_id=1, source_target_pairs={{8,16},{16,8},{9,17},{17,9},{10,18},{18,10},{11,19},{19,11},{12,20... | collective-permute-start | bytes 3145736 | tf_op jit(solution)/shard_map/ppermute | solution.py:287
  660.4 43.2 %collective-permute-start.102 = (bf16[512,1024]{1,0:T(8,128)(2,1)S(1)}, bf16[512,1024]{1,0:T(8,128)(2,1)S(1)}, u32[]{:S(2)}, u32[]{:S(2)}) collective-permute-start(bf16[512,1024]{1,0:T(8,128)(2,1)S(1)} %add_convert_fusion.14), channel_id=1, source_target_pairs={{8,0},{16,24},{9,1},{17,25},{10,2},{18,26},{11,3},{19,27},{12,4},{... | collective-permute-start | bytes 3145736 | tf_op jit(solution)/shard_map/ppermute | solution.py:304
  677.0 28.5 %collective-permute-start.103 = (bf16[528,1024]{1,0:T(8,128)(2,1)S(1)}, bf16[528,1024]{1,0:T(8,128)(2,1)S(1)}, u32[]{:S(2)}, u32[]{:S(2)}) collective-permute-start(bf16[528,1024]{1,0:T(8,128)(2,1)S(1)} %pad_maximum_fusion.3), channel_id=1, source_target_pairs={{0,8},{24,16},{1,9},{25,17},{2,10},{26,18},{3,11},{27,19},{4,12},{... | collective-permute-start | bytes 3244040 | tf_op jit(solution)/shard_map/ppermute | solution.py:301
  685.8 25.3 %collective-permute-start.105 = (bf16[512,1024]{1,0:T(8,128)(2,1)S(1)}, bf16[512,1024]{1,0:T(8,128)(2,1)S(1)}, u32[]{:S(2)}, u32[]{:S(2)}) collective-permute-start(bf16[512,1024]{1,0:T(8,128)(2,1)S(1)} %add_convert_fusion.13), channel_id=1, source_target_pairs={{8,16},{16,8},{9,17},{17,9},{10,18},{18,10},{11,19},{19,11},{12,20... | collective-permute-start | bytes 3145736 | tf_op jit(solution)/shard_map/ppermute | solution.py:287
  686.6 37.5 %collective-permute-start.106 = (bf16[512,1024]{1,0:T(8,128)(2,1)S(1)}, bf16[512,1024]{1,0:T(8,128)(2,1)S(1)}, u32[]{:S(2)}, u32[]{:S(2)}) collective-permute-start(bf16[512,1024]{1,0:T(8,128)(2,1)S(1)} %fusion.45), channel_id=1, source_target_pairs={{0,8},{8,0},{16,24},{24,16},{1,9},{9,1},{17,25},{25,17},{2,10},{10... | collective-permute-start | bytes 3145736 | tf_op jit(solution)/shard_map/ppermute | solution.py:297
  703.6 62.9 %collective-permute-start.127 = (bf16[512,1024]{1,0:T(8,128)(2,1)S(1)}, bf16[512,1024]{1,0:T(8,128)(2,1)S(1)}, u32[]{:S(2)}, u32[]{:S(2)}) collective-permute-start(bf16[512,1024]{1,0:T(8,128)(2,1)S(1)} %broadcast_select_fusion.4), channel_id=1, source_target_pairs={{0,2},{2,0},{4,6},{6,4},{1,3},{3,1},{5,7},{7,5},{8,10},{10,8},{12,... | collective-permute-start | bytes 3145736 | tf_op jit(solution)/shard_map/ppermute | solution.py:126
  705.9 40.0 %collective-permute-start.117 = (bf16[528,1024]{1,0:T(8,128)(2,1)S(1)}, bf16[528,1024]{1,0:T(8,128)(2,1)S(1)}, u32[]{:S(2)}, u32[]{:S(2)}) collective-permute-start(bf16[528,1024]{1,0:T(8,128)(2,1)S(1)} %add_convert_fusion.3), channel_id=1, source_target_pairs={{8,16},{16,8},{9,17},{17,9},{10,18},{18,10},{11,19},{19,11},{12,20... | collective-permute-start | bytes 3244040 | tf_op jit(solution)/shard_map/ppermute | solution.py:287
  708.4 91.8 %collective-permute-start.129 = (bf16[512,1024]{1,0:T(8,128)(2,1)S(1)}, bf16[512,1024]{1,0:T(8,128)(2,1)S(1)}, u32[]{:S(2)}, u32[]{:S(2)}) collective-permute-start(bf16[512,1024]{1,0:T(8,128)(2,1)S(1)} %broadcast_select_fusion.2), channel_id=1, source_target_pairs={{0,4},{2,6},{4,0},{6,2},{1,5},{3,7},{5,1},{7,3},{8,12},{10,14},{12... | collective-permute-start | bytes 3145736 | tf_op jit(solution)/shard_map/ppermute | solution.py:126
  743.5 85.2 %collective-permute-start.124 = (bf16[512,1024]{1,0:T(8,128)(2,1)}, bf16[512,1024]{1,0:T(8,128)(2,1)}, u32[]{:S(2)}, u32[]{:S(2)}) collective-permute-start(bf16[512,1024]{1,0:T(8,128)(2,1)} %fusion.47), channel_id=1, source_target_pairs={{0,8},{8,0},{16,24},{24,16},{1,9},{9,1},{17,25},{25,17},{2,10},{10... | collective-permute-start | bytes 3145736 | tf_op jit(solution)/shard_map/ppermute | solution.py:297
  751.5 40.2 %collective-permute-start.114 = (bf16[512,1024]{1,0:T(8,128)(2,1)S(1)}, bf16[512,1024]{1,0:T(8,128)(2,1)S(1)}, u32[]{:S(2)}, u32[]{:S(2)}) collective-permute-start(bf16[512,1024]{1,0:T(8,128)(2,1)S(1)} %add_convert_fusion.11), channel_id=1, source_target_pairs={{8,16},{16,8},{9,17},{17,9},{10,18},{18,10},{11,19},{19,11},{12,20... | collective-permute-start | bytes 3145736 | tf_op jit(solution)/shard_map/ppermute | solution.py:287
  752.5 36.5 %collective-permute-start.120 = (bf16[512,1024]{1,0:T(8,128)(2,1)S(1)}, bf16[512,1024]{1,0:T(8,128)(2,1)S(1)}, u32[]{:S(2)}, u32[]{:S(2)}) collective-permute-start(bf16[512,1024]{1,0:T(8,128)(2,1)S(1)} %fusion.46), channel_id=1, source_target_pairs={{0,8},{8,0},{16,24},{24,16},{1,9},{9,1},{17,25},{25,17},{2,10},{10... | collective-permute-start | bytes 3145736 | tf_op jit(solution)/shard_map/ppermute | solution.py:297
  766.5 26.2 %collective-permute-start.128 = (bf16[512,1024]{1,0:T(8,128)(2,1)S(1)}, bf16[512,1024]{1,0:T(8,128)(2,1)S(1)}, u32[]{:S(2)}, u32[]{:S(2)}) collective-permute-start(bf16[512,1024]{1,0:T(8,128)(2,1)S(1)} %broadcast_select_fusion.3), channel_id=1, source_target_pairs={{0,6},{2,4},{4,2},{6,0},{1,7},{3,5},{5,3},{7,1},{8,14},{10,12},{12... | collective-permute-start | bytes 3145736 | tf_op jit(solution)/shard_map/ppermute | solution.py:126
  788.9 24.5 %collective-permute-start.118 = (bf16[528,1024]{1,0:T(8,128)(2,1)S(1)}, bf16[528,1024]{1,0:T(8,128)(2,1)S(1)}, u32[]{:S(2)}, u32[]{:S(2)}) collective-permute-start(bf16[528,1024]{1,0:T(8,128)(2,1)S(1)} %add_convert_fusion.2), channel_id=1, source_target_pairs={{8,0},{16,24},{9,1},{17,25},{10,2},{18,26},{11,3},{19,27},{12,4},{... | collective-permute-start | bytes 3244040 | tf_op jit(solution)/shard_map/ppermute | solution.py:304
  791.7 25.2 %collective-permute-start.112 = (bf16[1,128,2048]{2,1,0:T(8,128)(2,1)}, bf16[1,128,2048]{2,1,0:T(8,128)(2,1)}, u32[]{:S(2)}, u32[]{:S(2)}) collective-permute-start(bf16[1,128,2048]{2,1,0:T(8,128)(2,1)} %maximum_bitcast_fusion), channel_id=1, source_target_pairs={{0,1},{1,0},{2,3},{3,2},{4,5},{5,4},{6,7},{7,6},{8,9},{9,8},{10,11... | collective-permute-start | bytes 1572872 | tf_op jit(solution)/shard_map/ppermute | solution.py:128
  792.7 53.8 %collective-permute-start.113 = (bf16[1,128,2048]{2,1,0:T(8,128)(2,1)}, bf16[1,128,2048]{2,1,0:T(8,128)(2,1)}, u32[]{:S(2)}, u32[]{:S(2)}) collective-permute-start(bf16[1,128,2048]{2,1,0:T(8,128)(2,1)} %maximum_bitcast_fusion.1), channel_id=1, source_target_pairs={{0,1},{1,0},{2,3},{3,2},{4,5},{5,4},{6,7},{7,6},{8,9},{9,8},{10,11... | collective-permute-start | bytes 1572872 | tf_op jit(solution)/shard_map/ppermute | solution.py:128
  816.9 27.8 %collective-permute-start.115 = (bf16[512,1024]{1,0:T(8,128)(2,1)S(1)}, bf16[512,1024]{1,0:T(8,128)(2,1)S(1)}, u32[]{:S(2)}, u32[]{:S(2)}) collective-permute-start(bf16[512,1024]{1,0:T(8,128)(2,1)S(1)} %add_convert_fusion.10), channel_id=1, source_target_pairs={{8,0},{16,24},{9,1},{17,25},{10,2},{18,26},{11,3},{19,27},{12,4},{... | collective-permute-start | bytes 3145736 | tf_op jit(solution)/shard_map/ppermute | solution.py:304
  821.0 26.6 %collective-permute-start.119 = (bf16[512,1024]{1,0:T(8,128)(2,1)}, bf16[512,1024]{1,0:T(8,128)(2,1)S(1)}, u32[]{:S(2)}, u32[]{:S(2)}) collective-permute-start(bf16[512,1024]{1,0:T(8,128)(2,1)} %slice.1316), channel_id=1, source_target_pairs={{0,4},{2,6},{4,0},{6,2},{1,5},{3,7},{5,1},{7,3},{8,12},{10,14},{12... | collective-permute-start | bytes 3145736 | tf_op jit(solution)/shard_map/ppermute | solution.py:126
  824.5 42.5 %collective-permute-start.122 = (bf16[512,1024]{1,0:T(8,128)(2,1)S(1)}, bf16[512,1024]{1,0:T(8,128)(2,1)}, u32[]{:S(2)}, u32[]{:S(2)}) collective-permute-start(bf16[512,1024]{1,0:T(8,128)(2,1)S(1)} %add_convert_fusion.7), channel_id=1, source_target_pairs={{8,0},{16,24},{9,1},{17,25},{10,2},{18,26},{11,3},{19,27},{12,4},{... | collective-permute-start | bytes 3145736 | tf_op jit(solution)/shard_map/ppermute | solution.py:304
  832.6 36.7 %collective-permute-start.125 = (bf16[512,1024]{1,0:T(8,128)(2,1)S(1)}, bf16[512,1024]{1,0:T(8,128)(2,1)}, u32[]{:S(2)}, u32[]{:S(2)}) collective-permute-start(bf16[512,1024]{1,0:T(8,128)(2,1)S(1)} %get-tuple-element.408), channel_id=1, source_target_pairs={{8,16},{16,8},{9,17},{17,9},{10,18},{18,10},{11,19},{19,11},{12,20... | collective-permute-start | bytes 3145736 | tf_op jit(solution)/shard_map/ppermute | solution.py:287
  845.8 26.3 %collective-permute-start.116 = (bf16[512,1024]{1,0:T(8,128)(2,1)}, bf16[512,1024]{1,0:T(8,128)(2,1)}, u32[]{:S(2)}, u32[]{:S(2)}) collective-permute-start(bf16[512,1024]{1,0:T(8,128)(2,1)} %broadcast_select_fusion.7), channel_id=1, source_target_pairs={{0,6},{2,4},{4,2},{6,0},{1,7},{3,5},{5,3},{7,1},{8,14},{10,12},{12... | collective-permute-start | bytes 3145736 | tf_op jit(solution)/shard_map/ppermute | solution.py:126
  870.9 27.6 %collective-permute-start.126 = (bf16[512,1024]{1,0:T(8,128)(2,1)S(1)}, bf16[512,1024]{1,0:T(8,128)(2,1)}, u32[]{:S(2)}, u32[]{:S(2)}) collective-permute-start(bf16[512,1024]{1,0:T(8,128)(2,1)S(1)} %add_convert_fusion.4), channel_id=1, source_target_pairs={{8,0},{16,24},{9,1},{17,25},{10,2},{18,26},{11,3},{19,27},{12,4},{... | collective-permute-start | bytes 3145736 | tf_op jit(solution)/shard_map/ppermute | solution.py:304
  (246 other events, 2477.5 us)
Sparse Core Ops, SparseCore 0:
  27.4 47.1 all-gather.2
  106.7 46.6 all-gather.4

commit v5 on v4

--- a/solution.py
+++ b/solution.py
@@ -572,7 +572,6 @@
     partial = step(
         (through(d_query, w_query) + through(d_key, w_key) + through(d_value, w_value)).astype(BF)
     )
-    d_inputs = d_hidden + plane.scatter(partial)
     def sums_of(array):
         return jnp.sum(array.reshape(seq_own, tok_seq * width), axis=1)
 
@@ -612,9 +611,11 @@
         vector = vector + plane.hop(vector, 0, col_xor)
         col_xor *= 2
     waiting[-rows] = jnp.concatenate([waiting[-rows], vector.astype(BF)], axis=0)
-    while waiting:
+    while len(waiting) > 1:
         step(())
-    line.placed, d_inputs, result_late = together(line.placed, d_inputs, result)
+    partial = step(partial)
+    d_inputs = d_hidden + plane.scatter(partial)
+    d_inputs, result_late = together(d_inputs, result)
 
     def home(array):
         own = plane.relative((array).astype(BF)).reshape(seq_own, tok_seq, width)

time: 924 us -> 963 us (1.042)
  waiting for transfers between devices: 344 us -> 366 us
  starting transfers between devices: 172 us -> 159 us
  other arithmetic: 146 us -> 158 us
  matrix products: 102 us -> 113 us
    ppermute x74, waiting for transfers between devices: 164 us -> 183 us  [hop(): lax.ppermute(array, 'row', [(a, a ^ row_xor) for a in range(self.rows)])]
    dot_general x7, matrix products: 25.1 us -> 34.9 us  [dot(): return jnp.dot(left_side, right_side, preferred_element_type=F32)]
    unnamed x390 -> x412, local copies, waits for them, and re-layouts: 37.5 us -> 38.7 us
  transfers between devices with their start and end apart: 133 -> 133, of which waited for: 52 -> 51; matrix products, arithmetic and copies ran while one was open for 31% -> 32% of each run, Pallas kernels for 2% -> 2%
where the time goes in v5:
time: 963 us; the launch traced here: 950 us
  waiting for transfers between devices  366 us (38%)
  starting transfers between devices  159 us (17%)
  other arithmetic  158 us (16%)
  local copies, waits for them, and re-layouts  119 us (12%)
  matrix products  113 us (12%)
  between operations  18.4 us (2%)
  Pallas kernels  16.7 us (2%)
    ppermute x74, waiting for transfers between devices, hop(): lax.ppermute(array, 'row', [(a, a ^ row_xor) for a in range(self.rows)])  183 us
    ppermute x11, waiting for transfers between devices, advance(): current['inward'] = lax.ppermute(sent, 'dp', ENDS)  70.5 us
    ppermute x5, waiting for transfers between devices, advance(): current['inward'] = lax.ppermute(array, 'dp', [(0, 1), (3, 2)])  46.6 us
    ppermute x11, starting transfers between devices, advance(): current['inward'] = lax.ppermute(sent, 'dp', ENDS)  44 us
    ppermute x74, starting transfers between devices, hop(): lax.ppermute(array, 'row', [(a, a ^ row_xor) for a in range(self.rows)])  42.3 us
    ppermute x5, waiting for transfers between devices, advance(): current['back'] = lax.ppermute(back, 'dp', [(1, 0), (2, 3)])  41.5 us
    dot_general x7, matrix products, through(): lax.dot_general(left_side, weight, (((1,), (1,)), ((), ())), preferred_el...  39.7 us
    dot_general x20, matrix products, against(): lax.dot_general(left_side, right_side, (((0,), (0,)), ((), ())), preferre...  38.8 us
  transfers between devices with their start and end apart: 133, of which 51 were waited for; matrix products, arithmetic and copies ran while one was open for 32% of the time, Pallas kernels for 2%

profile of v5, /device:TPU:0, one launch (start us, length us, event | category | flops | bytes accessed | tf_op | source)
XLA Modules:
  0.0 950.3 jit_solution(14248601331741109366)
XLA Ops:
  27.3 8.4 collective-permute-done.8
  48.0 6.7 collective-permute-done.11
  59.0 15.8 %collective-permute-done.6 = bf16[3,512,256]{2,1,0:T(8,128)(2,1)} collective-permute-done((bf16[3,512,256]{2,1,0:T(8,128)(2,1)}, bf16[3,512,256]{2,1,0:T(8,128)(2,1)}, u32[]{:S(2)}, u32[]{:S(2)}) %collective-permute-start.6) | collective-permute-done | bytes 786464 | tf_op jit(solution)/shard_map/ppermute | solution.py:126
  90.1 10.1 %collective-permute-done.14 = f32[2,2,4,128]{3,2,1,0:T(4,128)S(1)} collective-permute-done((f32[2,2,4,128]{3,2,1,0:T(4,128)S(1)}, f32[2,2,4,128]{3,2,1,0:T(4,128)S(1)}, u32[]{:S(2)}, u32[]{:S(2)}) %collective-permute-start.14) | collective-permute-done | bytes 8224 | tf_op jit(solution)/shard_map/ppermute | solution.py:126
  113.2 3.9 constant_dynamic-slice_fusion.23
  117.1 4.7 collective-permute-done.18
  129.8 18.6 %collective-permute-done.20 = bf16[1024,512]{1,0:T(8,128)(2,1)S(1)} collective-permute-done((bf16[1024,512]{1,0:T(8,128)(2,1)S(1)}, bf16[1024,512]{1,0:T(8,128)(2,1)S(1)}, u32[]{:S(2)}, u32[]{:S(2)}) %collective-permute-start.20) | collective-permute-done | bytes 1048608 | tf_op jit(solution)/shard_map/ppermute | solution.py:126
  152.2 7.7 shard_map.254
  160.0 9.1 collective-permute-done.21
  181.0 11.3 %collective-permute-done.23 = bf16[2,64,2048]{2,1,0:T(8,128)(2,1)S(1)} collective-permute-done((bf16[2,64,2048]{2,1,0:T(8,128)(2,1)S(1)}, bf16[2,64,2048]{2,1,0:T(8,128)(2,1)S(1)}, u32[]{:S(2)}, u32[]{:S(2)}) %collective-permute-start.23) | collective-permute-done | bytes 524320 | tf_op jit(solution)/shard_map/ppermute | solution.py:126
  195.4 3.9 collective-permute-done.24
  204.8 8.8 collective-permute-done.31
  220.8 6.6 collective-permute-done.36
  229.8 4.5 fusion.81
  234.4 16.4 %multiply_convert_fusion.2 = (bf16[1024,1024]{1,0:T(8,128)(2,1)S(1)}, f32[1024,1024]{1,0:T(8,128)}) fusion(f32[1024,1024]{1,0:T(8,128)S(1)} %fusion.81, bf16[1024,2048]{1,0:T(8,128)(2,1)S(1)} %constant_dynamic-update-slice_fusion.14, bf16[512,1024]{1,0:T(8,128)(2,1)S(1)} %get-tuple-element.378, bf16[512,1024]{1,0:T(8,128)(2,1)S(1)} %get-tuple-element.377, ...), kind=kOutput, calls=%fused_computation.15 | convolution fusion | flops 4318035968 | bytes 18874368 | tf_op jit(solution)/shard_map/dot_general | solution.py:86
  250.9 4.7 convolution_convert_fusion.1
  257.2 3.2 collective-permute-done.40
  260.4 2.9 fusion.153
  272.6 6.8 collective-permute-done.41
  281.9 3.5 collective-permute-done.43
  302.6 7.4 collective-permute-done.46
  311.4 3.2 collective-permute-done.48
  319.9 3.7 collective-permute-done.51
  331.0 3.0 fusion.34
  339.9 3.5 collective-permute-start.53
  343.4 9.0 multiply_convert_fusion
  352.4 14.0 %collective-permute-done.53 = bf16[512,1024]{1,0:T(8,128)(2,1)S(1)} collective-permute-done((bf16[512,1024]{1,0:T(8,128)(2,1)S(1)}, bf16[512,1024]{1,0:T(8,128)(2,1)S(1)}, u32[]{:S(2)}, u32[]{:S(2)}) %collective-permute-start.53) | collective-permute-done | bytes 1048608 | tf_op jit(solution)/shard_map/ppermute | solution.py:301
  370.0 5.5 collective-permute-start.54
  375.6 9.6 %fusion.79 = f32[1024,2048]{1,0:T(8,128)} fusion(bf16[1024,1024]{1,0:T(8,128)(2,1)S(1)} %get-tuple-element.192, bf16[512,1024]{1,0:T(8,128)(2,1)S(1)} %copy-done.124, bf16[512,1024]{1,0:T(8,128)(2,1)S(1)} %copy-done.122, bf16[512,1024]{1,0:T(8,128)(2,1)S(1)} %copy-done.180, bf16[512,1024]{1,0:T(8,128)(2,1)S(1)} %copy-done.78), kind=kOutput, calls=%fused_computation.256 | convolution fusion | flops 4311744512 | bytes 14680064 | tf_op jit(solution)/shard_map/dot_general | solution.py:96
  385.1 10.9 %add_convert_fusion.1 = bf16[1024,2048]{1,0:T(8,128)(2,1)} fusion(f32[1024,2048]{1,0:T(8,128)} %fusion.79, bf16[1024,1024]{1,0:T(8,128)(2,1)S(1)} %get-tuple-element.191, bf16[512,1024]{1,0:T(8,128)(2,1)} %copy-done.120, bf16[512,1024]{1,0:T(8,128)(2,1)} %copy-done.119, bf16[512,1024]{1,0:T(8,128)(2,1)} %copy-done.178, bf16[512,1024]{1,0:T(8,128)(2,1)S(1)} %copy-done.76), kind=kOutput, calls=%fused_computation.1 | convolution fusion | flops 4315938816 | bytes 18874368 | tf_op jit(solution)/shard_map/dot_general | solution.py:96
  403.6 4.7 collective-permute-start.55
  415.4 15.7 %collective-permute-done.55 = bf16[512,1024]{1,0:T(8,128)(2,1)S(1)} collective-permute-done((bf16[512,1024]{1,0:T(8,128)(2,1)S(1)}, bf16[512,1024]{1,0:T(8,128)(2,1)S(1)}, u32[]{:S(2)}, u32[]{:S(2)}) %collective-permute-start.55) | collective-permute-done | bytes 1048608 | tf_op jit(solution)/shard_map/ppermute | solution.py:301
  432.1 4.5 collective-permute-start.58
  442.9 15.9 %collective-permute-done.58 = bf16[512,1024]{1,0:T(8,128)(2,1)S(1)} collective-permute-done((bf16[512,1024]{1,0:T(8,128)(2,1)S(1)}, bf16[512,1024]{1,0:T(8,128)(2,1)S(1)}, u32[]{:S(2)}, u32[]{:S(2)}) %collective-permute-start.58) | collective-permute-done | bytes 1048608 | tf_op jit(solution)/shard_map/ppermute | solution.py:301
  465.1 4.3 collective-permute-start.67
  509.3 4.4 collective-permute-done.74
  519.2 3.7 collective-permute-start.81
  529.6 3.2 fusion.39
  534.9 13.7 %collective-permute-start.77 = (bf16[512,1024]{1,0:T(8,128)(2,1)}, bf16[512,1024]{1,0:T(8,128)(2,1)}, u32[]{:S(2)}, u32[]{:S(2)}) collective-permute-start(bf16[512,1024]{1,0:T(8,128)(2,1)} %fusion.39), channel_id=1, source_target_pairs={{0,8},{8,0},{16,24},{24,16},{1,9},{9,1},{17,25},{25,17},{2,10},{10... | collective-permute-start | bytes 3145736 | tf_op jit(solution)/shard_map/ppermute | solution.py:297
  549.7 8.9 shard_map.255
  583.0 3.2 fusion.41
  587.4 3.1 collective-permute-done.90
  602.3 9.0 collective-permute-done.88
  629.7 5.6 add_convert_fusion
  645.2 3.5 collective-permute-done.101
  649.7 3.5 collective-permute-done.102
  653.1 3.5 collective-permute-start.98
  665.2 15.5 %collective-permute-done.98 = bf16[512,1024]{1,0:T(8,128)(2,1)S(1)} collective-permute-done((bf16[512,1024]{1,0:T(8,128)(2,1)S(1)}, bf16[512,1024]{1,0:T(8,128)(2,1)S(1)}, u32[]{:S(2)}, u32[]{:S(2)}) %collective-permute-start.98) | collective-permute-done | bytes 1048608 | tf_op jit(solution)/shard_map/ppermute | solution.py:297
  686.4 6.4 collective-permute-start.115
  693.2 10.0 %collective-permute-done.93 = bf16[512,1024]{1,0:T(8,128)(2,1)S(1)} collective-permute-done((bf16[512,1024]{1,0:T(8,128)(2,1)S(1)}, bf16[512,1024]{1,0:T(8,128)(2,1)S(1)}, u32[]{:S(2)}, u32[]{:S(2)}) %collective-permute-start.93) | collective-permute-done | bytes 1048608 | tf_op jit(solution)/shard_map/ppermute | solution.py:297
  705.1 4.4 collective-permute-start.96
  709.6 16.1 %collective-permute-done.114 = bf16[512,1024]{1,0:T(8,128)(2,1)S(1)} collective-permute-done((bf16[512,1024]{1,0:T(8,128)(2,1)S(1)}, bf16[512,1024]{1,0:T(8,128)(2,1)S(1)}, u32[]{:S(2)}, u32[]{:S(2)}) %collective-permute-start.114) | collective-permute-done | bytes 1048608 | tf_op jit(solution)/shard_map/ppermute | solution.py:304
  731.5 4.8 collective-permute-start.124
  736.3 12.1 %collective-permute-done.96 = bf16[512,1024]{1,0:T(8,128)(2,1)S(1)} collective-permute-done((bf16[512,1024]{1,0:T(8,128)(2,1)S(1)}, bf16[512,1024]{1,0:T(8,128)(2,1)S(1)}, u32[]{:S(2)}, u32[]{:S(2)}) %collective-permute-start.96) | collective-permute-done | bytes 1048608 | tf_op jit(solution)/shard_map/ppermute | solution.py:297
  752.0 4.9 collective-permute-start.120
  759.5 31.3 %collective-permute-done.120 = bf16[512,1024]{1,0:T(8,128)(2,1)S(1)} collective-permute-done((bf16[512,1024]{1,0:T(8,128)(2,1)S(1)}, bf16[512,1024]{1,0:T(8,128)(2,1)S(1)}, u32[]{:S(2)}, u32[]{:S(2)}) %collective-permute-start.120) | collective-permute-done | bytes 1048608 | tf_op jit(solution)/shard_map/ppermute | solution.py:297
  796.3 4.4 broadcast.334.clone
  805.5 14.0 %collective-permute-done.118 = bf16[528,1024]{1,0:T(8,128)(2,1)S(1)} collective-permute-done((bf16[528,1024]{1,0:T(8,128)(2,1)S(1)}, bf16[528,1024]{1,0:T(8,128)(2,1)S(1)}, u32[]{:S(2)}, u32[]{:S(2)}) %collective-permute-start.118) | collective-permute-done | bytes 1081376 | tf_op jit(solution)/shard_map/ppermute | solution.py:304
  830.6 3.1 fusion.155
  833.9 5.1 collective-permute-done.111
  848.1 19.0 %collective-permute-done.104 = bf16[2,64,2048]{2,1,0:T(8,128)(2,1)S(1)} collective-permute-done((bf16[2,64,2048]{2,1,0:T(8,128)(2,1)S(1)}, bf16[2,64,2048]{2,1,0:T(8,128)(2,1)S(1)}, u32[]{:S(2)}, u32[]{:S(2)}) %collective-permute-start.104) | collective-permute-done | bytes 524320 | tf_op jit(solution)/shard_map/ppermute | solution.py:126
  871.5 3.9 convert_dynamic-update-slice_fusion.4
  878.3 16.6 %collective-permute-done.107 = bf16[64,2048]{1,0:T(8,128)(2,1)} collective-permute-done((bf16[64,2048]{1,0:T(8,128)(2,1)}, bf16[64,2048]{1,0:T(8,128)(2,1)}, u32[]{:S(2)}, u32[]{:S(2)}) %collective-permute-start.107) | collective-permute-done | bytes 262176 | tf_op jit(solution)/shard_map/ppermute | solution.py:126
  929.9 6.4 collective-permute-done.126
  (995 shorter events, 416.2 us)
Async XLA Ops:
  7.2 67.7 %all-gather.3.cloned.1.call-start = ((), (), s32[]{:S(2)}) async-start(), calls=%async_computation | async-start | bytes 2621440 | tf_op jit(solution)/shard_map/all_gather | solution.py:390
  16.7 23.7 %collective-permute-start.7 = (bf16[128,2048]{1,0:T(8,128)(2,1)}, bf16[128,2048]{1,0:T(8,128)(2,1)}, u32[]{:S(2)}, u32[]{:S(2)}) collective-permute-start(bf16[128,2048]{1,0:T(8,128)(2,1)} %pad_maximum_fusion.24), channel_id=1, source_target_pairs={{0,2},{2,0},{4,6},{6,4},{1,3},{3,1},{5,7},{7,5},{8,10},{10,8},{12,... | collective-permute-start | bytes 1572872 | tf_op jit(solution)/shard_map/ppermute | solution.py:126
  27.3 141.8 %all-gather.5.cloned.1.call-start = ((), (), s32[]{:S(2)}) async-start(), calls=%async_computation.1 | async-start | bytes 2621440 | tf_op jit(solution)/shard_map/all_gather | solution.py:390
  40.4 34.4 %collective-permute-start.6 = (bf16[3,512,256]{2,1,0:T(8,128)(2,1)}, bf16[3,512,256]{2,1,0:T(8,128)(2,1)}, u32[]{:S(2)}, u32[]{:S(2)}) collective-permute-start(bf16[3,512,256]{2,1,0:T(8,128)(2,1)} %pad_maximum_fusion.14), channel_id=1, source_target_pairs={{0,6},{2,4},{4,2},{6,0},{1,7},{3,5},{5,3},{7,1},{8,14},{10,12},{12... | collective-permute-start | bytes 2359304 | tf_op jit(solution)/shard_map/ppermute | solution.py:126
  122.4 26.0 %collective-permute-start.20 = (bf16[1024,512]{1,0:T(8,128)(2,1)S(1)}, bf16[1024,512]{1,0:T(8,128)(2,1)S(1)}, u32[]{:S(2)}, u32[]{:S(2)}) collective-permute-start(bf16[1024,512]{1,0:T(8,128)(2,1)S(1)} %get-tuple-element.165), channel_id=1, source_target_pairs={{0,4},{2,6},{4,0},{6,2},{1,5},{3,7},{5,1},{7,3},{8,12},{10,14},{12... | collective-permute-start | bytes 3145736 | tf_op jit(solution)/shard_map/ppermute | solution.py:126
  124.7 44.4 %collective-permute-start.21 = (bf16[1024,512]{1,0:T(8,128)(2,1)}, bf16[1024,512]{1,0:T(8,128)(2,1)}, u32[]{:S(2)}, u32[]{:S(2)}) collective-permute-start(bf16[1024,512]{1,0:T(8,128)(2,1)} %get-tuple-element.169), channel_id=1, source_target_pairs={{0,6},{2,4},{4,2},{6,0},{1,7},{3,5},{5,3},{7,1},{8,14},{10,12},{12... | collective-permute-start | bytes 3145736 | tf_op jit(solution)/shard_map/ppermute | solution.py:126
  175.4 54.4 %collective-permute-start.38 = (bf16[512,1024]{1,0:T(8,128)(2,1)S(1)}, bf16[512,1024]{1,0:T(8,128)(2,1)S(1)}, u32[]{:S(2)}, u32[]{:S(2)}) collective-permute-start(bf16[512,1024]{1,0:T(8,128)(2,1)S(1)} %get-tuple-element.347), channel_id=1, source_target_pairs={{0,2},{2,0},{4,6},{6,4},{1,3},{3,1},{5,7},{7,5},{8,10},{10,8},{12,... | collective-permute-start | bytes 3145736 | tf_op jit(solution)/shard_map/ppermute | solution.py:126
  176.3 58.1 %collective-permute-start.39 = (bf16[512,1024]{1,0:T(8,128)(2,1)S(1)}, bf16[512,1024]{1,0:T(8,128)(2,1)S(1)}, u32[]{:S(2)}, u32[]{:S(2)}) collective-permute-start(bf16[512,1024]{1,0:T(8,128)(2,1)S(1)} %get-tuple-element.349), channel_id=1, source_target_pairs={{0,2},{2,0},{4,6},{6,4},{1,3},{3,1},{5,7},{7,5},{8,10},{10,8},{12,... | collective-permute-start | bytes 3145736 | tf_op jit(solution)/shard_map/ppermute | solution.py:126
  339.9 26.5 %collective-permute-start.53 = (bf16[512,1024]{1,0:T(8,128)(2,1)S(1)}, bf16[512,1024]{1,0:T(8,128)(2,1)S(1)}, u32[]{:S(2)}, u32[]{:S(2)}) collective-permute-start(bf16[512,1024]{1,0:T(8,128)(2,1)S(1)} %fusion.34), channel_id=1, source_target_pairs={{0,8},{24,16},{1,9},{25,17},{2,10},{26,18},{3,11},{27,19},{4,12},{... | collective-permute-start | bytes 3145736 | tf_op jit(solution)/shard_map/ppermute | solution.py:301
  370.0 26.8 %collective-permute-start.54 = (bf16[512,1024]{1,0:T(8,128)(2,1)S(1)}, bf16[512,1024]{1,0:T(8,128)(2,1)}, u32[]{:S(2)}, u32[]{:S(2)}) collective-permute-start(bf16[512,1024]{1,0:T(8,128)(2,1)S(1)} %fusion.31), channel_id=1, source_target_pairs={{0,8},{24,16},{1,9},{25,17},{2,10},{26,18},{3,11},{27,19},{4,12},{... | collective-permute-start | bytes 3145736 | tf_op jit(solution)/shard_map/ppermute | solution.py:301
  398.9 32.2 %collective-permute-start.56 = (bf16[2,2,128,2048]{3,2,1,0:T(8,128)(2,1)S(1)}, bf16[2,2,128,2048]{3,2,1,0:T(8,128)(2,1)S(1)}, u32[]{:S(2)}, u32[]{:S(2)}) collective-permute-start(bf16[2,2,128,2048]{3,2,1,0:T(8,128)(2,1)S(1)} %fusion.14), channel_id=1, source_target_pairs={{0,2},{2,0},{4,6},{6,4},{1,3},{3,1},{5,7},{7,5},{8,10},{10,8},{12,... | collective-permute-start | bytes 6291464 | tf_op jit(solution)/shard_map/ppermute | solution.py:126
  403.6 27.5 %collective-permute-start.55 = (bf16[512,1024]{1,0:T(8,128)(2,1)S(1)}, bf16[512,1024]{1,0:T(8,128)(2,1)S(1)}, u32[]{:S(2)}, u32[]{:S(2)}) collective-permute-start(bf16[512,1024]{1,0:T(8,128)(2,1)S(1)} %copy-done.82), channel_id=1, source_target_pairs={{0,8},{24,16},{1,9},{25,17},{2,10},{26,18},{3,11},{27,19},{4,12},{... | collective-permute-start | bytes 3145736 | tf_op jit(solution)/shard_map/ppermute | solution.py:301
  414.5 44.2 %collective-permute-start.59 = (bf16[512,1024]{1,0:T(8,128)(2,1)S(1)}, bf16[512,1024]{1,0:T(8,128)(2,1)S(1)}, u32[]{:S(2)}, u32[]{:S(2)}) collective-permute-start(bf16[512,1024]{1,0:T(8,128)(2,1)S(1)} %add_convert_fusion.32), channel_id=1, source_target_pairs={{8,16},{16,8},{9,17},{17,9},{10,18},{18,10},{11,19},{19,11},{12,20... | collective-permute-start | bytes 3145736 | tf_op jit(solution)/shard_map/ppermute | solution.py:287
  432.1 26.7 %collective-permute-start.58 = (bf16[512,1024]{1,0:T(8,128)(2,1)S(1)}, bf16[512,1024]{1,0:T(8,128)(2,1)S(1)}, u32[]{:S(2)}, u32[]{:S(2)}) collective-permute-start(bf16[512,1024]{1,0:T(8,128)(2,1)S(1)} %copy-done.81), channel_id=1, source_target_pairs={{0,8},{24,16},{1,9},{25,17},{2,10},{26,18},{3,11},{27,19},{4,12},{... | collective-permute-start | bytes 3145736 | tf_op jit(solution)/shard_map/ppermute | solution.py:301
  442.1 27.6 %collective-permute-start.57 = (bf16[512,1024]{1,0:T(8,128)(2,1)S(1)}, bf16[512,1024]{1,0:T(8,128)(2,1)S(1)}, u32[]{:S(2)}, u32[]{:S(2)}) collective-permute-start(bf16[512,1024]{1,0:T(8,128)(2,1)S(1)} %add_convert_fusion.33), channel_id=1, source_target_pairs={{8,16},{16,8},{9,17},{17,9},{10,18},{18,10},{11,19},{19,11},{12,20... | collective-permute-start | bytes 3145736 | tf_op jit(solution)/shard_map/ppermute | solution.py:287
  461.9 29.5 %collective-permute-start.66 = (bf16[512,1024]{1,0:T(8,128)(2,1)}, bf16[512,1024]{1,0:T(8,128)(2,1)}, u32[]{:S(2)}, u32[]{:S(2)}) collective-permute-start(bf16[512,1024]{1,0:T(8,128)(2,1)} %add_convert_fusion.29), channel_id=1, source_target_pairs={{8,16},{16,8},{9,17},{17,9},{10,18},{18,10},{11,19},{19,11},{12,20... | collective-permute-start | bytes 3145736 | tf_op jit(solution)/shard_map/ppermute | solution.py:287
  465.1 27.8 %collective-permute-start.67 = (bf16[512,1024]{1,0:T(8,128)(2,1)}, bf16[512,1024]{1,0:T(8,128)(2,1)}, u32[]{:S(2)}, u32[]{:S(2)}) collective-permute-start(bf16[512,1024]{1,0:T(8,128)(2,1)} %fusion.38), channel_id=1, source_target_pairs={{0,8},{8,0},{16,24},{24,16},{1,9},{9,1},{17,25},{25,17},{2,10},{10... | collective-permute-start | bytes 3145736 | tf_op jit(solution)/shard_map/ppermute | solution.py:297
  475.6 43.6 %collective-permute-start.64 = (bf16[512,1024]{1,0:T(8,128)(2,1)}, bf16[512,1024]{1,0:T(8,128)(2,1)}, u32[]{:S(2)}, u32[]{:S(2)}) collective-permute-start(bf16[512,1024]{1,0:T(8,128)(2,1)} %add_convert_fusion.31), channel_id=1, source_target_pairs={{8,16},{16,8},{9,17},{17,9},{10,18},{18,10},{11,19},{19,11},{12,20... | collective-permute-start | bytes 3145736 | tf_op jit(solution)/shard_map/ppermute | solution.py:287
  489.9 33.0 %collective-permute-start.65 = (bf16[512,1024]{1,0:T(8,128)(2,1)S(1)}, bf16[512,1024]{1,0:T(8,128)(2,1)S(1)}, u32[]{:S(2)}, u32[]{:S(2)}) collective-permute-start(bf16[512,1024]{1,0:T(8,128)(2,1)S(1)} %fusion.37), channel_id=1, source_target_pairs={{0,8},{8,0},{16,24},{24,16},{1,9},{9,1},{17,25},{25,17},{2,10},{10... | collective-permute-start | bytes 3145736 | tf_op jit(solution)/shard_map/ppermute | solution.py:297
  507.5 62.8 %collective-permute-start.78 = (bf16[512,512]{1,0:T(8,128)(2,1)}, bf16[512,512]{1,0:T(8,128)(2,1)}, u32[]{:S(2)}, u32[]{:S(2)}) collective-permute-start(bf16[512,512]{1,0:T(8,128)(2,1)} %get-tuple-element.407), channel_id=1, source_target_pairs={{0,4},{2,6},{4,0},{6,2},{1,5},{3,7},{5,1},{7,3},{8,12},{10,14},{12... | collective-permute-start | bytes 1572872 | tf_op jit(solution)/shard_map/ppermute | solution.py:126
  507.9 64.5 %collective-permute-start.79 = (bf16[512,512]{1,0:T(8,128)(2,1)}, bf16[512,512]{1,0:T(8,128)(2,1)}, u32[]{:S(2)}, u32[]{:S(2)}) collective-permute-start(bf16[512,512]{1,0:T(8,128)(2,1)} %get-tuple-element.406), channel_id=1, source_target_pairs={{0,6},{2,4},{4,2},{6,0},{1,7},{3,5},{5,3},{7,1},{8,14},{10,12},{12... | collective-permute-start | bytes 1572872 | tf_op jit(solution)/shard_map/ppermute | solution.py:126
  519.2 29.5 %collective-permute-start.81 = (bf16[512,1024]{1,0:T(8,128)(2,1)S(1)}, bf16[512,1024]{1,0:T(8,128)(2,1)S(1)}, u32[]{:S(2)}, u32[]{:S(2)}) collective-permute-start(bf16[512,1024]{1,0:T(8,128)(2,1)S(1)} %fusion.40), channel_id=1, source_target_pairs={{0,8},{8,0},{16,24},{24,16},{1,9},{9,1},{17,25},{25,17},{2,10},{10... | collective-permute-start | bytes 3145736 | tf_op jit(solution)/shard_map/ppermute | solution.py:297
  526.6 47.7 %collective-permute-start.76 = (bf16[512,1024]{1,0:T(8,128)(2,1)}, bf16[512,1024]{1,0:T(8,128)(2,1)}, u32[]{:S(2)}, u32[]{:S(2)}) collective-permute-start(bf16[512,1024]{1,0:T(8,128)(2,1)} %add_convert_fusion.27), channel_id=1, source_target_pairs={{8,16},{16,8},{9,17},{17,9},{10,18},{18,10},{11,19},{19,11},{12,20... | collective-permute-start | bytes 3145736 | tf_op jit(solution)/shard_map/ppermute | solution.py:287
  534.9 40.9 %collective-permute-start.77 = (bf16[512,1024]{1,0:T(8,128)(2,1)}, bf16[512,1024]{1,0:T(8,128)(2,1)}, u32[]{:S(2)}, u32[]{:S(2)}) collective-permute-start(bf16[512,1024]{1,0:T(8,128)(2,1)} %fusion.39), channel_id=1, source_target_pairs={{0,8},{8,0},{16,24},{24,16},{1,9},{9,1},{17,25},{25,17},{2,10},{10... | collective-permute-start | bytes 3145736 | tf_op jit(solution)/shard_map/ppermute | solution.py:297
  562.0 94.9 %collective-permute-start.84 = (bf16[512,512]{1,0:T(8,128)(2,1)}, bf16[512,512]{1,0:T(8,128)(2,1)}, u32[]{:S(2)}, u32[]{:S(2)}) collective-permute-start(bf16[512,512]{1,0:T(8,128)(2,1)} %get-tuple-element.404), channel_id=1, source_target_pairs={{0,2},{2,0},{4,6},{6,4},{1,3},{3,1},{5,7},{7,5},{8,10},{10,8},{12,... | collective-permute-start | bytes 1572872 | tf_op jit(solution)/shard_map/ppermute | solution.py:126
  570.3 41.3 %collective-permute-start.85 = (bf16[512,1024]{1,0:T(8,128)(2,1)}, bf16[512,1024]{1,0:T(8,128)(2,1)}, u32[]{:S(2)}, u32[]{:S(2)}) collective-permute-start(bf16[512,1024]{1,0:T(8,128)(2,1)} %add_convert_fusion.21), channel_id=1, source_target_pairs={{8,16},{16,8},{9,17},{17,9},{10,18},{18,10},{11,19},{19,11},{12,20... | collective-permute-start | bytes 3145736 | tf_op jit(solution)/shard_map/ppermute | solution.py:287
  572.5 39.2 %collective-permute-start.86 = (bf16[512,1024]{1,0:T(8,128)(2,1)}, bf16[512,1024]{1,0:T(8,128)(2,1)}, u32[]{:S(2)}, u32[]{:S(2)}) collective-permute-start(bf16[512,1024]{1,0:T(8,128)(2,1)} %fusion.42), channel_id=1, source_target_pairs={{0,8},{8,0},{16,24},{24,16},{1,9},{9,1},{17,25},{25,17},{2,10},{10... | collective-permute-start | bytes 3145736 | tf_op jit(solution)/shard_map/ppermute | solution.py:297
  574.3 26.4 %collective-permute-start.87 = (bf16[512,512]{1,0:T(8,128)(2,1)}, bf16[512,512]{1,0:T(8,128)(2,1)}, u32[]{:S(2)}, u32[]{:S(2)}) collective-permute-start(bf16[512,512]{1,0:T(8,128)(2,1)} %get-tuple-element.403), channel_id=1, source_target_pairs={{0,4},{2,6},{4,0},{6,2},{1,5},{3,7},{5,1},{7,3},{8,12},{10,14},{12... | collective-permute-start | bytes 1572872 | tf_op jit(solution)/shard_map/ppermute | solution.py:126
  600.7 56.2 %collective-permute-start.82 = (bf16[512,1024]{1,0:T(8,128)(2,1)}, bf16[512,1024]{1,0:T(8,128)(2,1)}, u32[]{:S(2)}, u32[]{:S(2)}) collective-permute-start(bf16[512,1024]{1,0:T(8,128)(2,1)} %add_convert_fusion.23), channel_id=1, source_target_pairs={{8,16},{16,8},{9,17},{17,9},{10,18},{18,10},{11,19},{19,11},{12,20... | collective-permute-start | bytes 3145736 | tf_op jit(solution)/shard_map/ppermute | solution.py:287
  611.3 46.5 %collective-permute-start.83 = (bf16[512,1024]{1,0:T(8,128)(2,1)}, bf16[512,1024]{1,0:T(8,128)(2,1)}, u32[]{:S(2)}, u32[]{:S(2)}) collective-permute-start(bf16[512,1024]{1,0:T(8,128)(2,1)} %fusion.41), channel_id=1, source_target_pairs={{0,8},{8,0},{16,24},{24,16},{1,9},{9,1},{17,25},{25,17},{2,10},{10... | collective-permute-start | bytes 3145736 | tf_op jit(solution)/shard_map/ppermute | solution.py:297
  611.7 31.6 %collective-permute-start.100 = (f32[16,1024]{1,0:T(8,128)}, f32[16,1024]{1,0:T(8,128)}, u32[]{:S(2)}, u32[]{:S(2)}) collective-permute-start(f32[16,1024]{1,0:T(8,128)} %reshape.596), channel_id=1, source_target_pairs={{0,2},{2,0},{4,6},{6,4},{1,3},{3,1},{5,7},{7,5},{8,10},{10,8},{12,... | collective-permute-start | bytes 196616 | tf_op jit(solution)/shard_map/ppermute | solution.py:126
  628.6 36.2 %collective-permute-start.97 = (bf16[512,1024]{1,0:T(8,128)(2,1)}, bf16[512,1024]{1,0:T(8,128)(2,1)S(1)}, u32[]{:S(2)}, u32[]{:S(2)}) collective-permute-start(bf16[512,1024]{1,0:T(8,128)(2,1)} %add_convert_fusion.15), channel_id=1, source_target_pairs={{8,16},{16,8},{9,17},{17,9},{10,18},{18,10},{11,19},{19,11},{12,20... | collective-permute-start | bytes 3145736 | tf_op jit(solution)/shard_map/ppermute | solution.py:287
  653.1 27.6 %collective-permute-start.98 = (bf16[512,1024]{1,0:T(8,128)(2,1)S(1)}, bf16[512,1024]{1,0:T(8,128)(2,1)S(1)}, u32[]{:S(2)}, u32[]{:S(2)}) collective-permute-start(bf16[512,1024]{1,0:T(8,128)(2,1)S(1)} %fusion.45), channel_id=1, source_target_pairs={{0,8},{8,0},{16,24},{24,16},{1,9},{9,1},{17,25},{25,17},{2,10},{10... | collective-permute-start | bytes 3145736 | tf_op jit(solution)/shard_map/ppermute | solution.py:297
  656.9 28.1 %collective-permute-start.94 = (bf16[512,1024]{1,0:T(8,128)(2,1)S(1)}, bf16[512,1024]{1,0:T(8,128)(2,1)S(1)}, u32[]{:S(2)}, u32[]{:S(2)}) collective-permute-start(bf16[512,1024]{1,0:T(8,128)(2,1)S(1)} %broadcast_select_fusion.11), channel_id=1, source_target_pairs={{0,4},{2,6},{4,0},{6,2},{1,5},{3,7},{5,1},{7,3},{8,12},{10,14},{12... | collective-permute-start | bytes 3145736 | tf_op jit(solution)/shard_map/ppermute | solution.py:126
  659.5 26.9 %collective-permute-start.92 = (bf16[512,1024]{1,0:T(8,128)(2,1)S(1)}, bf16[512,1024]{1,0:T(8,128)(2,1)S(1)}, u32[]{:S(2)}, u32[]{:S(2)}) collective-permute-start(bf16[512,1024]{1,0:T(8,128)(2,1)S(1)} %add_convert_fusion.19), channel_id=1, source_target_pairs={{8,16},{16,8},{9,17},{17,9},{10,18},{18,10},{11,19},{19,11},{12,20... | collective-permute-start | bytes 3145736 | tf_op jit(solution)/shard_map/ppermute | solution.py:287
  663.6 39.5 %collective-permute-start.93 = (bf16[512,1024]{1,0:T(8,128)(2,1)S(1)}, bf16[512,1024]{1,0:T(8,128)(2,1)S(1)}, u32[]{:S(2)}, u32[]{:S(2)}) collective-permute-start(bf16[512,1024]{1,0:T(8,128)(2,1)S(1)} %fusion.43), channel_id=1, source_target_pairs={{0,8},{8,0},{16,24},{24,16},{1,9},{9,1},{17,25},{25,17},{2,10},{10... | collective-permute-start | bytes 3145736 | tf_op jit(solution)/shard_map/ppermute | solution.py:297
  664.8 40.3 %collective-permute-start.116 = (bf16[512,1024]{1,0:T(8,128)(2,1)S(1)}, bf16[512,1024]{1,0:T(8,128)(2,1)S(1)}, u32[]{:S(2)}, u32[]{:S(2)}) collective-permute-start(bf16[512,1024]{1,0:T(8,128)(2,1)S(1)} %broadcast_select_fusion.7), channel_id=1, source_target_pairs={{0,6},{2,4},{4,2},{6,0},{1,7},{3,5},{5,3},{7,1},{8,14},{10,12},{12... | collective-permute-start | bytes 3145736 | tf_op jit(solution)/shard_map/ppermute | solution.py:126
  681.1 28.4 %collective-permute-start.113 = (bf16[512,1024]{1,0:T(8,128)(2,1)S(1)}, bf16[512,1024]{1,0:T(8,128)(2,1)S(1)}, u32[]{:S(2)}, u32[]{:S(2)}) collective-permute-start(bf16[512,1024]{1,0:T(8,128)(2,1)S(1)} %add_convert_fusion.11), channel_id=1, source_target_pairs={{8,16},{16,8},{9,17},{17,9},{10,18},{18,10},{11,19},{19,11},{12,20... | collective-permute-start | bytes 3145736 | tf_op jit(solution)/shard_map/ppermute | solution.py:287
  685.0 40.7 %collective-permute-start.114 = (bf16[512,1024]{1,0:T(8,128)(2,1)S(1)}, bf16[512,1024]{1,0:T(8,128)(2,1)S(1)}, u32[]{:S(2)}, u32[]{:S(2)}) collective-permute-start(bf16[512,1024]{1,0:T(8,128)(2,1)S(1)} %add_convert_fusion.10), channel_id=1, source_target_pairs={{8,0},{16,24},{9,1},{17,25},{10,2},{18,26},{11,3},{19,27},{12,4},{... | collective-permute-start | bytes 3145736 | tf_op jit(solution)/shard_map/ppermute | solution.py:304
  686.4 39.5 %collective-permute-start.115 = (bf16[528,1024]{1,0:T(8,128)(2,1)S(1)}, bf16[528,1024]{1,0:T(8,128)(2,1)S(1)}, u32[]{:S(2)}, u32[]{:S(2)}) collective-permute-start(bf16[528,1024]{1,0:T(8,128)(2,1)S(1)} %pad_maximum_fusion.3), channel_id=1, source_target_pairs={{0,8},{24,16},{1,9},{25,17},{2,10},{26,18},{3,11},{27,19},{4,12},{... | collective-permute-start | bytes 3244040 | tf_op jit(solution)/shard_map/ppermute | solution.py:301
  703.6 27.9 %collective-permute-start.95 = (bf16[512,1024]{1,0:T(8,128)(2,1)S(1)}, bf16[512,1024]{1,0:T(8,128)(2,1)S(1)}, u32[]{:S(2)}, u32[]{:S(2)}) collective-permute-start(bf16[512,1024]{1,0:T(8,128)(2,1)S(1)} %add_convert_fusion.17), channel_id=1, source_target_pairs={{8,16},{16,8},{9,17},{17,9},{10,18},{18,10},{11,19},{19,11},{12,20... | collective-permute-start | bytes 3145736 | tf_op jit(solution)/shard_map/ppermute | solution.py:287
  705.1 43.2 %collective-permute-start.96 = (bf16[512,1024]{1,0:T(8,128)(2,1)S(1)}, bf16[512,1024]{1,0:T(8,128)(2,1)S(1)}, u32[]{:S(2)}, u32[]{:S(2)}) collective-permute-start(bf16[512,1024]{1,0:T(8,128)(2,1)S(1)} %fusion.44), channel_id=1, source_target_pairs={{0,8},{8,0},{16,24},{24,16},{1,9},{9,1},{17,25},{25,17},{2,10},{10... | collective-permute-start | bytes 3145736 | tf_op jit(solution)/shard_map/ppermute | solution.py:297
  709.6 42.4 %collective-permute-start.127 = (bf16[512,1024]{1,0:T(8,128)(2,1)S(1)}, bf16[512,1024]{1,0:T(8,128)(2,1)S(1)}, u32[]{:S(2)}, u32[]{:S(2)}) collective-permute-start(bf16[512,1024]{1,0:T(8,128)(2,1)S(1)} %broadcast_select_fusion.4), channel_id=1, source_target_pairs={{0,2},{2,0},{4,6},{6,4},{1,3},{3,1},{5,7},{7,5},{8,10},{10,8},{12,... | collective-permute-start | bytes 3145736 | tf_op jit(solution)/shard_map/ppermute | solution.py:126
  726.3 32.7 %collective-permute-start.117 = (bf16[528,1024]{1,0:T(8,128)(2,1)S(1)}, bf16[528,1024]{1,0:T(8,128)(2,1)S(1)}, u32[]{:S(2)}, u32[]{:S(2)}) collective-permute-start(bf16[528,1024]{1,0:T(8,128)(2,1)S(1)} %add_convert_fusion.3), channel_id=1, source_target_pairs={{8,16},{16,8},{9,17},{17,9},{10,18},{18,10},{11,19},{19,11},{12,20... | collective-permute-start | bytes 3244040 | tf_op jit(solution)/shard_map/ppermute | solution.py:287
  727.4 74.9 %collective-permute-start.129 = (bf16[512,1024]{1,0:T(8,128)(2,1)S(1)}, bf16[512,1024]{1,0:T(8,128)(2,1)S(1)}, u32[]{:S(2)}, u32[]{:S(2)}) collective-permute-start(bf16[512,1024]{1,0:T(8,128)(2,1)S(1)} %broadcast_select_fusion.2), channel_id=1, source_target_pairs={{0,4},{2,6},{4,0},{6,2},{1,5},{3,7},{5,1},{7,3},{8,12},{10,14},{12... | collective-permute-start | bytes 3145736 | tf_op jit(solution)/shard_map/ppermute | solution.py:126
  731.5 139.2 %collective-permute-start.124 = (bf16[512,1024]{1,0:T(8,128)(2,1)}, bf16[512,1024]{1,0:T(8,128)(2,1)}, u32[]{:S(2)}, u32[]{:S(2)}) collective-permute-start(bf16[512,1024]{1,0:T(8,128)(2,1)} %fusion.47), channel_id=1, source_target_pairs={{0,8},{8,0},{16,24},{24,16},{1,9},{9,1},{17,25},{25,17},{2,10},{10... | collective-permute-start | bytes 3145736 | tf_op jit(solution)/shard_map/ppermute | solution.py:297
  748.8 44.8 %collective-permute-start.110 = (bf16[512,1024]{1,0:T(8,128)(2,1)S(1)}, bf16[512,1024]{1,0:T(8,128)(2,1)S(1)}, u32[]{:S(2)}, u32[]{:S(2)}) collective-permute-start(bf16[512,1024]{1,0:T(8,128)(2,1)S(1)} %add_convert_fusion.13), channel_id=1, source_target_pairs={{8,16},{16,8},{9,17},{17,9},{10,18},{18,10},{11,19},{19,11},{12,20... | collective-permute-start | bytes 3145736 | tf_op jit(solution)/shard_map/ppermute | solution.py:287
  752.0 38.8 %collective-permute-start.120 = (bf16[512,1024]{1,0:T(8,128)(2,1)S(1)}, bf16[512,1024]{1,0:T(8,128)(2,1)S(1)}, u32[]{:S(2)}, u32[]{:S(2)}) collective-permute-start(bf16[512,1024]{1,0:T(8,128)(2,1)S(1)} %fusion.46), channel_id=1, source_target_pairs={{0,8},{8,0},{16,24},{24,16},{1,9},{9,1},{17,25},{25,17},{2,10},{10... | collective-permute-start | bytes 3145736 | tf_op jit(solution)/shard_map/ppermute | solution.py:297
  759.0 36.0 %collective-permute-start.128 = (bf16[512,1024]{1,0:T(8,128)(2,1)S(1)}, bf16[512,1024]{1,0:T(8,128)(2,1)S(1)}, u32[]{:S(2)}, u32[]{:S(2)}) collective-permute-start(bf16[512,1024]{1,0:T(8,128)(2,1)S(1)} %broadcast_select_fusion.3), channel_id=1, source_target_pairs={{0,6},{2,4},{4,2},{6,0},{1,7},{3,5},{5,3},{7,1},{8,14},{10,12},{12... | collective-permute-start | bytes 3145736 | tf_op jit(solution)/shard_map/ppermute | solution.py:126
  790.8 28.7 %collective-permute-start.118 = (bf16[528,1024]{1,0:T(8,128)(2,1)S(1)}, bf16[528,1024]{1,0:T(8,128)(2,1)S(1)}, u32[]{:S(2)}, u32[]{:S(2)}) collective-permute-start(bf16[528,1024]{1,0:T(8,128)(2,1)S(1)} %add_convert_fusion.2), channel_id=1, source_target_pairs={{8,0},{16,24},{9,1},{17,25},{10,2},{18,26},{11,3},{19,27},{12,4},{... | collective-permute-start | bytes 3244040 | tf_op jit(solution)/shard_map/ppermute | solution.py:304
  793.6 36.1 %collective-permute-start.103 = (bf16[2,2,128,2048]{3,2,1,0:T(8,128)(2,1)}, bf16[2,2,128,2048]{3,2,1,0:T(8,128)(2,1)}, u32[]{:S(2)}, u32[]{:S(2)}) collective-permute-start(bf16[2,2,128,2048]{3,2,1,0:T(8,128)(2,1)} %fusion.16), channel_id=1, source_target_pairs={{0,2},{2,0},{4,6},{6,4},{1,3},{3,1},{5,7},{7,5},{8,10},{10,8},{12,... | collective-permute-start | bytes 6291464 | tf_op jit(solution)/shard_map/ppermute | solution.py:126
  795.0 43.9 %collective-permute-start.111 = (bf16[512,1024]{1,0:T(8,128)(2,1)}, bf16[512,1024]{1,0:T(8,128)(2,1)}, u32[]{:S(2)}, u32[]{:S(2)}) collective-permute-start(bf16[512,1024]{1,0:T(8,128)(2,1)} %add_convert_fusion.12), channel_id=1, source_target_pairs={{8,0},{16,24},{9,1},{17,25},{10,2},{18,26},{11,3},{19,27},{12,4},{... | collective-permute-start | bytes 3145736 | tf_op jit(solution)/shard_map/ppermute | solution.py:304
  802.3 39.8 %collective-permute-start.121 = (bf16[512,1024]{1,0:T(8,128)(2,1)S(1)}, bf16[512,1024]{1,0:T(8,128)(2,1)}, u32[]{:S(2)}, u32[]{:S(2)}) collective-permute-start(bf16[512,1024]{1,0:T(8,128)(2,1)S(1)} %add_convert_fusion.8), channel_id=1, source_target_pairs={{8,16},{16,8},{9,17},{17,9},{10,18},{18,10},{11,19},{19,11},{12,20... | collective-permute-start | bytes 3145736 | tf_op jit(solution)/shard_map/ppermute | solution.py:287
  819.5 25.8 %collective-permute-start.130 = (bf16[512,1024]{1,0:T(8,128)(2,1)}, bf16[512,1024]{1,0:T(8,128)(2,1)}, u32[]{:S(2)}, u32[]{:S(2)}) collective-permute-start(bf16[512,1024]{1,0:T(8,128)(2,1)} %broadcast_select_fusion.1), channel_id=1, source_target_pairs={{0,2},{2,0},{4,6},{6,4},{1,3},{3,1},{5,7},{7,5},{8,10},{10,8},{12,... | collective-permute-start | bytes 3145736 | tf_op jit(solution)/shard_map/ppermute | solution.py:126
  829.7 45.6 %collective-permute-start.119 = (bf16[512,1024]{1,0:T(8,128)(2,1)}, bf16[512,1024]{1,0:T(8,128)(2,1)S(1)}, u32[]{:S(2)}, u32[]{:S(2)}) collective-permute-start(bf16[512,1024]{1,0:T(8,128)(2,1)} %slice.1316), channel_id=1, source_target_pairs={{0,4},{2,6},{4,0},{6,2},{1,5},{3,7},{5,1},{7,3},{8,12},{10,14},{12... | collective-permute-start | bytes 3145736 | tf_op jit(solution)/shard_map/ppermute | solution.py:126
  838.9 28.2 %collective-permute-start.104 = (bf16[2,64,2048]{2,1,0:T(8,128)(2,1)S(1)}, bf16[2,64,2048]{2,1,0:T(8,128)(2,1)S(1)}, u32[]{:S(2)}, u32[]{:S(2)}) collective-permute-start(bf16[2,64,2048]{2,1,0:T(8,128)(2,1)S(1)} %pad_maximum_fusion.50), channel_id=1, source_target_pairs={{0,4},{2,6},{4,0},{6,2},{1,5},{3,7},{5,1},{7,3},{8,12},{10,14},{12... | collective-permute-start | bytes 1572872 | tf_op jit(solution)/shard_map/ppermute | solution.py:126
  842.1 27.1 %collective-permute-start.106 = (bf16[2,64,2048]{2,1,0:T(8,128)(2,1)S(1)}, bf16[2,64,2048]{2,1,0:T(8,128)(2,1)S(1)}, u32[]{:S(2)}, u32[]{:S(2)}) collective-permute-start(bf16[2,64,2048]{2,1,0:T(8,128)(2,1)S(1)} %pad_maximum_fusion.51), channel_id=1, source_target_pairs={{0,1},{1,0},{2,3},{3,2},{4,5},{5,4},{6,7},{7,6},{8,9},{9,8},{10,11... | collective-permute-start | bytes 1572872 | tf_op jit(solution)/shard_map/ppermute | solution.py:128
  845.3 64.7 %collective-permute-start.112 = (bf16[512,1024]{1,0:T(8,128)(2,1)}, bf16[512,1024]{1,0:T(8,128)(2,1)}, u32[]{:S(2)}, u32[]{:S(2)}) collective-permute-start(bf16[512,1024]{1,0:T(8,128)(2,1)} %broadcast_select_fusion.8), channel_id=1, source_target_pairs={{0,6},{2,4},{4,2},{6,0},{1,7},{3,5},{5,3},{7,1},{8,14},{10,12},{12... | collective-permute-start | bytes 3145736 | tf_op jit(solution)/shard_map/ppermute | solution.py:126
  867.1 37.6 %collective-permute-start.122 = (bf16[512,1024]{1,0:T(8,128)(2,1)}, bf16[512,1024]{1,0:T(8,128)(2,1)}, u32[]{:S(2)}, u32[]{:S(2)}) collective-permute-start(bf16[512,1024]{1,0:T(8,128)(2,1)} %add_convert_fusion.7), channel_id=1, source_target_pairs={{8,0},{16,24},{9,1},{17,25},{10,2},{18,26},{11,3},{19,27},{12,4},{... | collective-permute-start | bytes 3145736 | tf_op jit(solution)/shard_map/ppermute | solution.py:304
  870.7 24.3 %collective-permute-start.107 = (bf16[64,2048]{1,0:T(8,128)(2,1)}, bf16[64,2048]{1,0:T(8,128)(2,1)}, u32[]{:S(2)}, u32[]{:S(2)}) collective-permute-start(bf16[64,2048]{1,0:T(8,128)(2,1)} %pad_maximum_fusion.60), channel_id=1, source_target_pairs={{0,4},{2,6},{4,0},{6,2},{1,5},{3,7},{5,1},{7,3},{8,12},{10,14},{12... | collective-permute-start | bytes 786440 | tf_op jit(solution)/shard_map/ppermute | solution.py:126
  875.4 31.7 %collective-permute-start.125 = (bf16[512,1024]{1,0:T(8,128)(2,1)S(1)}, bf16[512,1024]{1,0:T(8,128)(2,1)}, u32[]{:S(2)}, u32[]{:S(2)}) collective-permute-start(bf16[512,1024]{1,0:T(8,128)(2,1)S(1)} %get-tuple-element.388), channel_id=1, source_target_pairs={{8,16},{16,8},{9,17},{17,9},{10,18},{18,10},{11,19},{19,11},{12,20... | collective-permute-start | bytes 3145736 | tf_op jit(solution)/shard_map/ppermute | solution.py:287
  898.6 23.2 %collective-permute-start.108 = (bf16[1,128,2048]{2,1,0:T(8,128)(2,1)}, bf16[1,128,2048]{2,1,0:T(8,128)(2,1)}, u32[]{:S(2)}, u32[]{:S(2)}) collective-permute-start(bf16[1,128,2048]{2,1,0:T(8,128)(2,1)} %maximum_bitcast_fusion), channel_id=1, source_target_pairs={{0,1},{1,0},{2,3},{3,2},{4,5},{5,4},{6,7},{7,6},{8,9},{9,8},{10,11... | collective-permute-start | bytes 1572872 | tf_op jit(solution)/shard_map/ppermute | solution.py:128
  900.3 23.7 %collective-permute-start.109 = (bf16[1,128,2048]{2,1,0:T(8,128)(2,1)}, bf16[1,128,2048]{2,1,0:T(8,128)(2,1)}, u32[]{:S(2)}, u32[]{:S(2)}) collective-permute-start(bf16[1,128,2048]{2,1,0:T(8,128)(2,1)} %maximum_bitcast_fusion.1), channel_id=1, source_target_pairs={{0,1},{1,0},{2,3},{3,2},{4,5},{5,4},{6,7},{7,6},{8,9},{9,8},{10,11... | collective-permute-start | bytes 1572872 | tf_op jit(solution)/shard_map/ppermute | solution.py:128
  908.7 27.6 %collective-permute-start.126 = (bf16[512,1024]{1,0:T(8,128)(2,1)S(1)}, bf16[512,1024]{1,0:T(8,128)(2,1)}, u32[]{:S(2)}, u32[]{:S(2)}) collective-permute-start(bf16[512,1024]{1,0:T(8,128)(2,1)S(1)} %add_convert_fusion.4), channel_id=1, source_target_pairs={{8,0},{16,24},{9,1},{17,25},{10,2},{18,26},{11,3},{19,27},{12,4},{... | collective-permute-start | bytes 3145736 | tf_op jit(solution)/shard_map/ppermute | solution.py:304
  (257 other events, 2575.8 us)
Sparse Core Ops, SparseCore 0:
  27.4 47.1 all-gather.2
  106.7 46.6 all-gather.4
